TPU v7x, 32 devices: a whole 2x2x4 slice. The times are simulated.
32 devices in a mesh: groups: 2 (over y), section: 4 (over z), mp: 4 (over x, core).
Axes of the slice: x: 2, y: 2, z: 4, core: 2. Of those that a mesh axis runs over, the one named last changes fastest.
Arguments:
- memory: bfloat16 [16, 8, 4096], P(('section', 'mp'), 'groups'), parts along dimension 1, may hold values from -6 to 6
- decoder_in: bfloat16 [8, 32, 4096], P('groups'), parts along dimension 0, may hold values from -6 to 6
- cotangent: bfloat16 [8, 32, 4096], P('groups'), parts along dimension 0, may hold values from -6 to 6
- src_lengths: int32 [8, 4], P('groups'), parts along dimension 0, may hold values from 1 to 8, 16 in all within a row
- tgt_segments: int32 [8, 32], P('groups'), parts along dimension 0, may hold values from 0 to 3, never falling along the last dimension, each value on 1 to 16 neighbouring positions
- seeds: int32 [8, 4], P('groups', 'section'), parts along dimension 0, may hold values from 0 to 1073741823
- w_query: bfloat16 [4, 4096, 2048], P('section', None, 'mp'), may hold values from -0.09375 to 0.09375
- w_key: bfloat16 [4, 4096, 2048], P('section', None, 'mp'), may hold values from -0.09375 to 0.09375
- w_value: bfloat16 [4, 4096, 2048], P('section', None, 'mp'), may hold values from -0.09375 to 0.09375
- w_out: bfloat16 [4, 2048, 4096], P('section', 'mp'), may hold values from -0.125 to 0.125
Outputs:
- section_out: bfloat16 [4, 8, 32, 4096], P('section', 'groups', None, 'mp'), parts along dimension 1
- mem_grad: float32 [16, 8, 4096], P(('section', 'mp'), 'groups'), parts along dimension 1
There are 2 independent parts, one for each index of `groups`. A program takes and returns all parts, laid end to end along the dimension named above; an argument that names none is the same for every part. Nothing has to cross between parts.
Inputs may be any that keep to these rules, and one draw needn't show every extreme that they name: `src_lengths`: in each micro-batch the 4 lengths sum to 16, and the longest is exactly 8. `tgt_segments`: ids never fall along a micro-batch's tokens.
All inputs are finite; a program needn't handle non-finite values.
Results may differ from a plain program's by a relative error of at most 0.02.
Values may be sent and summed in bfloat16 or wider, within the bound.
No kernel may reach another device: no remote copies, remote signals or barrier semaphores. Data moves between devices by JAX's collectives and lax.ppermute only.
A program may use at most 128 MiB of HBM per device.

v0:
```python
import math

import jax
import jax.numpy as jnp
from jax import lax
from jax.sharding import PartitionSpec as P

HD = 256


NEG_FILL = -1e30
KEEP_SCALE = 8.0 / 7.0


def from_behind(array, axis, by):
    size = lax.axis_size(axis)
    pairs = [(i, i + by) for i in range(size) if 0 <= i + by < size]
    return lax.ppermute(array, axis, pairs)


def shifted_right(source_bits, amount):
    return lax.shift_right_logical(source_bits, jnp.full(source_bits.shape, amount, jnp.int32))


def keep_factor(seed_value, row_count, col_count):
    position = (
        jnp.arange(row_count, dtype=jnp.int32)[:, None] * col_count
        + jnp.arange(col_count, dtype=jnp.int32)[None, :]
    )
    hashed = position ^ seed_value * 1640531527
    hashed = hashed ^ shifted_right(hashed, 16)
    hashed = hashed * 2146121005
    hashed = hashed ^ shifted_right(hashed, 15)
    hashed = hashed * 1911520717
    hashed = hashed ^ shifted_right(hashed, 16)
    is_kept = shifted_right(hashed, 8) & 7 != 0
    return jnp.where(is_kept, KEEP_SCALE, 0.0).astype(jnp.float32)


def document_rows(lengths_row, src_rows):
    doc_ends = jnp.cumsum(lengths_row)
    row_index = jnp.arange(src_rows, dtype=jnp.int32)
    return jnp.sum((doc_ends[None, :] <= row_index[:, None]).astype(jnp.int32), axis=1)


def keep_slot(stack_rows, item_rows, mb_slot, is_valid):
    return jnp.where(
        is_valid, lax.dynamic_update_index_in_dim(stack_rows, item_rows, mb_slot, 0), stack_rows
    )


def head_sum(head_terms):
    return lax.psum(head_terms.astype(jnp.bfloat16), "mp").astype(jnp.float32)


def per_device(
    memory, decoder_in, cotangent, src_lengths, tgt_segments, seeds, w_query, w_key, w_value, w_out
):
    micro_count, tgt_rows, model_dim = decoder_in.shape
    local_cols = w_query.shape[2]
    local_heads = local_cols // HD
    score_scale = 1.0 / math.sqrt(HD)
    sections = lax.axis_size("section")
    section_index = lax.axis_index("section")
    mp_index = lax.axis_index("mp")
    wq_local = w_query[0]
    wk_local = w_key[0]
    wv_local = w_value[0]
    wo_local = w_out[0]
    row_piece = lax.all_gather(memory, ("section", "mp"), axis=0, tiled=True)
    key_part = jnp.einsum(
        "rbd,dk->rbk", row_piece, wk_local, preferred_element_type=jnp.float32
    ).astype(jnp.bfloat16)
    value_part = jnp.einsum(
        "rbd,dk->rbk", row_piece, wv_local, preferred_element_type=jnp.float32
    ).astype(jnp.bfloat16)
    key_value = jnp.concatenate([key_part, value_part], axis=2)
    src_rows = key_value.shape[0]
    doc_ids = jax.vmap(lambda lengths_row: document_rows(lengths_row, src_rows))(src_lengths)
    allowed_all = tgt_segments[:, :, None] == doc_ids[:, None, :]
    seed_column = seeds[:, 0]

    def micro_inputs(mb_slot):
        kv_pair = lax.dynamic_index_in_dim(key_value, mb_slot, 1, keepdims=False)
        key_heads = kv_pair[:, :local_cols].reshape(src_rows, local_heads, HD)
        value_heads = kv_pair[:, local_cols:].reshape(src_rows, local_heads, HD)
        allowed = lax.dynamic_index_in_dim(allowed_all, mb_slot, 0, keepdims=False)
        seed_value = lax.dynamic_index_in_dim(seed_column, mb_slot, 0, keepdims=False)
        factor = keep_factor(seed_value, tgt_rows, model_dim)
        return (key_heads, value_heads, allowed, factor)

    def score_rows(query_rows, key_heads, allowed):
        query_heads = query_rows.reshape(tgt_rows, local_heads, HD)
        scores = (
            jnp.einsum("thd,shd->hts", query_heads, key_heads, preferred_element_type=jnp.float32)
            * score_scale
        )
        scores = jnp.where(allowed[None, :, :], scores, NEG_FILL)
        row_peak = jnp.max(scores, axis=2, keepdims=True)
        exp_terms = jnp.exp(scores - row_peak)
        return exp_terms / jnp.sum(exp_terms, axis=2, keepdims=True)

    def forward_step(step_index, carry):
        buffer, inputs_kept, outputs_kept, stash_kept = carry
        micro_index = step_index - section_index
        is_valid = (micro_index >= 0) & (micro_index < micro_count)
        mb_slot = jnp.clip(micro_index, 0, micro_count - 1)
        fresh_rows = lax.dynamic_index_in_dim(decoder_in, mb_slot, 0, keepdims=False)
        current = jnp.where(section_index == 0, fresh_rows, buffer)
        key_heads, value_heads, allowed, factor = micro_inputs(mb_slot)
        query_rows = jnp.dot(current, wq_local, preferred_element_type=jnp.float32).astype(
            jnp.bfloat16
        )
        prob_rows = score_rows(query_rows, key_heads, allowed)
        attended = jnp.einsum(
            "hts,shd->thd",
            prob_rows.astype(jnp.bfloat16),
            value_heads,
            preferred_element_type=jnp.float32,
        ).astype(jnp.bfloat16)
        head_terms = jnp.dot(
            attended.reshape(tgt_rows, local_cols), wo_local, preferred_element_type=jnp.float32
        )
        sum_heads = head_sum(head_terms)
        following = (current.astype(jnp.float32) + factor * sum_heads).astype(jnp.bfloat16)
        inputs_kept = keep_slot(inputs_kept, current, mb_slot, is_valid)
        outputs_kept = keep_slot(outputs_kept, following, mb_slot, is_valid)
        buffer = from_behind(following, "section", 1)
        return (buffer, inputs_kept, outputs_kept, stash_kept)

    stash_init = ()
    zero_rows = jnp.zeros((tgt_rows, model_dim), jnp.bfloat16)
    zero_stack = jnp.zeros((micro_count, tgt_rows, model_dim), jnp.bfloat16)
    step_count = sections + micro_count - 1
    buffer, inputs_kept, outputs_kept, stash_kept = lax.fori_loop(
        0, step_count, forward_step, (zero_rows, zero_stack, zero_stack, stash_init)
    )

    def backward_step(step_index, carry):
        buffer, grads_kv = carry
        micro_index = step_index - (sections - 1 - section_index)
        is_valid = (micro_index >= 0) & (micro_index < micro_count)
        mb_slot = jnp.clip(micro_index, 0, micro_count - 1)
        fresh_grad = lax.dynamic_index_in_dim(cotangent, mb_slot, 0, keepdims=False)
        grad_rows = jnp.where(section_index == sections - 1, fresh_grad, buffer)
        current = lax.dynamic_index_in_dim(inputs_kept, mb_slot, 0, keepdims=False)
        key_heads, value_heads, allowed, factor = micro_inputs(mb_slot)
        query_rows = jnp.dot(current, wq_local, preferred_element_type=jnp.float32).astype(
            jnp.bfloat16
        )
        prob_rows = score_rows(query_rows, key_heads, allowed)
        weights_b = prob_rows.astype(jnp.bfloat16)
        d_out = (grad_rows.astype(jnp.float32) * factor).astype(jnp.bfloat16)
        d_att = jnp.einsum("td,kd->tk", d_out, wo_local, preferred_element_type=jnp.float32).astype(
            jnp.bfloat16
        )
        d_heads = d_att.reshape(tgt_rows, local_heads, HD)
        d_probs = jnp.einsum(
            "thd,shd->hts", d_heads, value_heads, preferred_element_type=jnp.float32
        )
        inner_sum = jnp.sum(prob_rows * d_probs, axis=2, keepdims=True)
        d_scores = (prob_rows * (d_probs - inner_sum) * score_scale).astype(jnp.bfloat16)
        query_heads = query_rows.reshape(tgt_rows, local_heads, HD)
        d_query = (
            jnp.einsum("hts,shd->thd", d_scores, key_heads, preferred_element_type=jnp.float32)
            .astype(jnp.bfloat16)
            .reshape(tgt_rows, local_cols)
        )
        d_keys = (
            jnp.einsum("hts,thd->shd", d_scores, query_heads, preferred_element_type=jnp.float32)
            .astype(jnp.bfloat16)
            .reshape(src_rows, local_cols)
        )
        d_values = (
            jnp.einsum("hts,thd->shd", weights_b, d_heads, preferred_element_type=jnp.float32)
            .astype(jnp.bfloat16)
            .reshape(src_rows, local_cols)
        )
        back_terms = jnp.einsum("tk,dk->td", d_query, wq_local, preferred_element_type=jnp.float32)
        grad_prev = (grad_rows.astype(jnp.float32) + head_sum(back_terms)).astype(jnp.bfloat16)
        grad_pair = jnp.concatenate([d_keys, d_values], axis=1)
        grads_kv = jnp.where(
            is_valid, lax.dynamic_update_index_in_dim(grads_kv, grad_pair, mb_slot, 1), grads_kv
        )
        buffer = from_behind(grad_prev, "section", -1)
        return (buffer, grads_kv)

    grads_init = jnp.zeros((src_rows, micro_count, 2 * local_cols), jnp.bfloat16)
    buffer, grads_kv = lax.fori_loop(0, step_count, backward_step, (zero_rows, grads_init))
    key_terms = jnp.einsum(
        "rbk,dk->rbd", grads_kv[:, :, :local_cols], wk_local, preferred_element_type=jnp.float32
    )
    value_terms = jnp.einsum(
        "rbk,dk->rbd", grads_kv[:, :, local_cols:], wv_local, preferred_element_type=jnp.float32
    )
    mem_grad = lax.psum_scatter(
        key_terms + value_terms, ("section", "mp"), scatter_dimension=0, tiled=True
    )
    out_cols = model_dim // lax.axis_size("mp")
    section_out = lax.dynamic_slice_in_dim(outputs_kept, mp_index * out_cols, out_cols, 2)[None]
    return (section_out, mem_grad)


def solution(mesh):
    return jax.shard_map(
        per_device,
        mesh=mesh,
        in_specs=(
            P(("section", "mp"), "groups", None),
            P("groups", None, None),
            P("groups", None, None),
            P("groups", None),
            P("groups", None),
            P("groups", "section"),
            P("section", None, "mp"),
            P("section", None, "mp"),
            P("section", None, "mp"),
            P("section", "mp", None),
        ),
        out_specs=(P("section", "groups", None, "mp"), P(("section", "mp"), "groups", None)),
        check_vma=False,
    )
```

profile of v0, /device:TPU:0, one launch (start us, length us, event | category | flops | bytes accessed | tf_op | source)
XLA Modules:
  0.0 866.3 jit_solution(16907695326962325958)
XLA Ops:
  8.0 24.9 %all_gather.3 = bf16[16,4,4096]{2,1,0:T(4,128)(2,1)S(1)} all-gather(bf16[1,4,4096]{2,1,0:T(4,128)(2,1)} %param.14), channel_id=1, replica_groups=mesh['groups'=2,'section'=4,'mp'=4] {'section','mp'}, dimensions={0}, use_global_device_ids=true | all-gather | bytes 557056 | tf_op jit(solution)/shard_map/all_gather | solution.py:70
  32.9 3.1 fusion.100
  37.6 352.3 %while.35 = (s32[]{:T(128)}, bf16[32,4096]{1,0:T(8,128)(2,1)S(1)}, bf16[4,32,4096]{2,1,0:T(8,128)(2,1)S(1)}, bf16[4,32,4096]{2,1,0:T(8,128)(2,1)S(1)}, pred[]{:T...) while((s32[]{:T(128)}, bf16[32,4096]{1,0:T(8,128)(2,1)S(1)}, ...), condition=%wide.region_6.7_spmd, body=%wide.region_2.6_spmd.sunk | while | flops 272668704 | bytes 14527445 | solution.py:135
  42.2 3.7 convolution_convert_fusion.15
  47.1 28.3 %all-reduce.7.cloned.1.call-done = bf16[32,4096]{1,0:T(8,128)(2,1)} async-done(((bf16[32,4096]{1,0:T(8,128)(2,1)}), bf16[32,4096]{1,0:T(8,128)(2,1)}) %all-reduce.7.cloned.1.call-update) | async-done | bytes 262160 | tf_op jit(solution)/shard_map/while/body/eval_jaxpr/psum | solution.py:53
  76.8 3.4 collective-permute-start
  80.2 4.4 collective-permute-done
  85.8 3.0 convolution_convert_fusion.14
  89.1 3.7 convolution_convert_fusion.15
  94.1 32.2 %all-reduce.7.cloned.1.call-done = bf16[32,4096]{1,0:T(8,128)(2,1)} async-done(((bf16[32,4096]{1,0:T(8,128)(2,1)}), bf16[32,4096]{1,0:T(8,128)(2,1)}) %all-reduce.7.cloned.1.call-update) | async-done | bytes 262160 | tf_op jit(solution)/shard_map/while/body/eval_jaxpr/psum | solution.py:53
  127.7 3.4 collective-permute-start
  131.1 4.4 collective-permute-done
  140.0 3.7 convolution_convert_fusion.15
  144.9 32.2 %all-reduce.7.cloned.1.call-done = bf16[32,4096]{1,0:T(8,128)(2,1)} async-done(((bf16[32,4096]{1,0:T(8,128)(2,1)}), bf16[32,4096]{1,0:T(8,128)(2,1)}) %all-reduce.7.cloned.1.call-update) | async-done | bytes 262160 | tf_op jit(solution)/shard_map/while/body/eval_jaxpr/psum | solution.py:53
  178.6 3.4 collective-permute-start
  182.0 4.4 collective-permute-done
  190.9 3.7 convolution_convert_fusion.15
  195.8 32.2 %all-reduce.7.cloned.1.call-done = bf16[32,4096]{1,0:T(8,128)(2,1)} async-done(((bf16[32,4096]{1,0:T(8,128)(2,1)}), bf16[32,4096]{1,0:T(8,128)(2,1)}) %all-reduce.7.cloned.1.call-update) | async-done | bytes 262160 | tf_op jit(solution)/shard_map/while/body/eval_jaxpr/psum | solution.py:53
  229.5 3.4 collective-permute-start
  232.9 4.4 collective-permute-done
  238.4 3.0 convolution_convert_fusion.14
  241.8 3.7 convolution_convert_fusion.15
  246.7 32.2 %all-reduce.7.cloned.1.call-done = bf16[32,4096]{1,0:T(8,128)(2,1)} async-done(((bf16[32,4096]{1,0:T(8,128)(2,1)}), bf16[32,4096]{1,0:T(8,128)(2,1)}) %all-reduce.7.cloned.1.call-update) | async-done | bytes 262160 | tf_op jit(solution)/shard_map/while/body/eval_jaxpr/psum | solution.py:53
  280.4 3.4 collective-permute-start
  283.8 4.4 collective-permute-done
  292.7 3.7 convolution_convert_fusion.15
  297.6 32.2 %all-reduce.7.cloned.1.call-done = bf16[32,4096]{1,0:T(8,128)(2,1)} async-done(((bf16[32,4096]{1,0:T(8,128)(2,1)}), bf16[32,4096]{1,0:T(8,128)(2,1)}) %all-reduce.7.cloned.1.call-update) | async-done | bytes 262160 | tf_op jit(solution)/shard_map/while/body/eval_jaxpr/psum | solution.py:53
  331.2 3.4 collective-permute-start
  334.7 4.4 collective-permute-done
  343.6 3.7 convolution_convert_fusion.15
  348.5 32.2 %all-reduce.7.cloned.1.call-done = bf16[32,4096]{1,0:T(8,128)(2,1)} async-done(((bf16[32,4096]{1,0:T(8,128)(2,1)}), bf16[32,4096]{1,0:T(8,128)(2,1)}) %all-reduce.7.cloned.1.call-update) | async-done | bytes 262160 | tf_op jit(solution)/shard_map/while/body/eval_jaxpr/psum | solution.py:53
  382.1 3.4 collective-permute-start
  385.5 4.4 collective-permute-done
  390.0 367.4 %while.36 = (s32[]{:T(128)}, bf16[32,4096]{1,0:T(8,128)(2,1)S(1)}, bf16[16,4,1024]{2,0,1:T(8,128)(2,1)S(1)}, pred[]{:T(512)}, s32[]{:T(128)}, /*index=5*/bf16[4,...) while((s32[]{:T(128)}, bf16[32,4096]{1,0:T(8,128)(2,1)S(1)}, ...), condition=%wide.region_12.13_spmd, body=%wide.region_7.12_spmd.sunk | while | flops 408719520 | bytes 34816112 | solution.py:189
  391.6 3.7 convolution_convert_fusion.16
  396.6 4.2 convolution_convert_fusion.18
  400.9 33.4 %all-reduce.9.cloned.1.call-done = bf16[32,4096]{1,0:T(8,128)(2,1)} async-done(((bf16[32,4096]{1,0:T(8,128)(2,1)}), bf16[32,4096]{1,0:T(8,128)(2,1)}) %all-reduce.9.cloned.1.call-update) | async-done | bytes 262160 | tf_op jit(solution)/shard_map/while/body/eval_jaxpr/psum | solution.py:53
  437.0 7.0 collective-permute-done.1
  445.5 3.7 convolution_convert_fusion.16
  450.5 4.2 convolution_convert_fusion.18
  454.8 31.7 %all-reduce.9.cloned.1.call-done = bf16[32,4096]{1,0:T(8,128)(2,1)} async-done(((bf16[32,4096]{1,0:T(8,128)(2,1)}), bf16[32,4096]{1,0:T(8,128)(2,1)}) %all-reduce.9.cloned.1.call-update) | async-done | bytes 262160 | tf_op jit(solution)/shard_map/while/body/eval_jaxpr/psum | solution.py:53
  489.3 7.0 collective-permute-done.1
  497.8 3.7 convolution_convert_fusion.16
  502.8 4.2 convolution_convert_fusion.18
  507.0 31.8 %all-reduce.9.cloned.1.call-done = bf16[32,4096]{1,0:T(8,128)(2,1)} async-done(((bf16[32,4096]{1,0:T(8,128)(2,1)}), bf16[32,4096]{1,0:T(8,128)(2,1)}) %all-reduce.9.cloned.1.call-update) | async-done | bytes 262160 | tf_op jit(solution)/shard_map/while/body/eval_jaxpr/psum | solution.py:53
  541.5 7.0 collective-permute-done.1
  550.0 3.7 convolution_convert_fusion.16
  555.0 4.2 convolution_convert_fusion.18
  559.3 31.7 %all-reduce.9.cloned.1.call-done = bf16[32,4096]{1,0:T(8,128)(2,1)} async-done(((bf16[32,4096]{1,0:T(8,128)(2,1)}), bf16[32,4096]{1,0:T(8,128)(2,1)}) %all-reduce.9.cloned.1.call-update) | async-done | bytes 262160 | tf_op jit(solution)/shard_map/while/body/eval_jaxpr/psum | solution.py:53
  593.7 7.0 collective-permute-done.1
  602.3 3.7 convolution_convert_fusion.16
  607.3 4.2 convolution_convert_fusion.18
  611.5 31.8 %all-reduce.9.cloned.1.call-done = bf16[32,4096]{1,0:T(8,128)(2,1)} async-done(((bf16[32,4096]{1,0:T(8,128)(2,1)}), bf16[32,4096]{1,0:T(8,128)(2,1)}) %all-reduce.9.cloned.1.call-update) | async-done | bytes 262160 | tf_op jit(solution)/shard_map/while/body/eval_jaxpr/psum | solution.py:53
  646.0 7.0 collective-permute-done.1
  654.5 3.7 convolution_convert_fusion.16
  659.5 4.2 convolution_convert_fusion.18
  663.7 31.7 %all-reduce.9.cloned.1.call-done = bf16[32,4096]{1,0:T(8,128)(2,1)} async-done(((bf16[32,4096]{1,0:T(8,128)(2,1)}), bf16[32,4096]{1,0:T(8,128)(2,1)}) %all-reduce.9.cloned.1.call-update) | async-done | bytes 262160 | tf_op jit(solution)/shard_map/while/body/eval_jaxpr/psum | solution.py:53
  698.2 7.0 collective-permute-done.1
  706.7 3.7 convolution_convert_fusion.16
  711.7 4.2 convolution_convert_fusion.18
  716.0 31.8 %all-reduce.9.cloned.1.call-done = bf16[32,4096]{1,0:T(8,128)(2,1)} async-done(((bf16[32,4096]{1,0:T(8,128)(2,1)}), bf16[32,4096]{1,0:T(8,128)(2,1)}) %all-reduce.9.cloned.1.call-update) | async-done | bytes 262160 | tf_op jit(solution)/shard_map/while/body/eval_jaxpr/psum | solution.py:53
  750.5 7.0 collective-permute-done.1
  757.4 3.7 fusion.93
  765.6 91.4 %all-reduce.5.cloned.1.call-done = f32[16,4,4096]{2,1,0:T(4,128)} async-done(((f32[16,4,4096]{2,1,0:T(4,128)}), f32[16,4,4096]{2,1,0:T(4,128)}) %all-reduce.5.cloned.1.call-update) | async-done | bytes 1048592
  (265 shorter events, 80.1 us)
Async XLA Ops:
  8.0 28.1 %copy-start.2 = (bf16[1,4096,512]{2,1,0:T(8,128)(2,1)S(1)}, bf16[1,4096,512]{2,1,0:T(8,128)(2,1)}, u32[]{:S(2)}) copy-start(bf16[1,4096,512]{2,1,0:T(8,128)(2,1)} %param.21) | copy-start | bytes 12582916
  36.1 0.9 copy-start.3
  36.1 1.2 copy-start.4
  36.1 1.5 copy-start.5
  37.7 37.8 %all-reduce.7.cloned.1.call-start = ((), (), s32[]{:S(2)}) async-start(), calls=%async_computation.1 | async-start | bytes 524288 | tf_op jit(solution)/shard_map/while/body/eval_jaxpr/psum | solution.py:53
  76.8 7.8 collective-permute-start
  84.6 41.7 %all-reduce.7.cloned.1.call-start = ((), (), s32[]{:S(2)}) async-start(), calls=%async_computation.1 | async-start | bytes 524288 | tf_op jit(solution)/shard_map/while/body/eval_jaxpr/psum | solution.py:53
  127.7 7.8 collective-permute-start
  135.5 41.7 %all-reduce.7.cloned.1.call-start = ((), (), s32[]{:S(2)}) async-start(), calls=%async_computation.1 | async-start | bytes 524288 | tf_op jit(solution)/shard_map/while/body/eval_jaxpr/psum | solution.py:53
  178.6 7.8 collective-permute-start
  186.4 41.6 %all-reduce.7.cloned.1.call-start = ((), (), s32[]{:S(2)}) async-start(), calls=%async_computation.1 | async-start | bytes 524288 | tf_op jit(solution)/shard_map/while/body/eval_jaxpr/psum | solution.py:53
  229.5 7.8 collective-permute-start
  237.3 41.7 %all-reduce.7.cloned.1.call-start = ((), (), s32[]{:S(2)}) async-start(), calls=%async_computation.1 | async-start | bytes 524288 | tf_op jit(solution)/shard_map/while/body/eval_jaxpr/psum | solution.py:53
  280.4 7.8 collective-permute-start
  288.2 41.7 %all-reduce.7.cloned.1.call-start = ((), (), s32[]{:S(2)}) async-start(), calls=%async_computation.1 | async-start | bytes 524288 | tf_op jit(solution)/shard_map/while/body/eval_jaxpr/psum | solution.py:53
  331.2 7.8 collective-permute-start
  339.1 41.6 %all-reduce.7.cloned.1.call-start = ((), (), s32[]{:S(2)}) async-start(), calls=%async_computation.1 | async-start | bytes 524288 | tf_op jit(solution)/shard_map/while/body/eval_jaxpr/psum | solution.py:53
  382.1 7.8 collective-permute-start
  390.0 44.3 %all-reduce.9.cloned.1.call-start = ((), (), s32[]{:S(2)}) async-start(), calls=%async_computation.2 | async-start | bytes 524288 | tf_op jit(solution)/shard_map/while/body/eval_jaxpr/psum | solution.py:53
  390.1 5.3 copy-start
  435.4 8.6 collective-permute-start.1
  444.0 42.5 %all-reduce.9.cloned.1.call-start = ((), (), s32[]{:S(2)}) async-start(), calls=%async_computation.2 | async-start | bytes 524288 | tf_op jit(solution)/shard_map/while/body/eval_jaxpr/psum | solution.py:53
  444.0 5.3 copy-start
  487.7 8.6 collective-permute-start.1
  496.2 42.6 %all-reduce.9.cloned.1.call-start = ((), (), s32[]{:S(2)}) async-start(), calls=%async_computation.2 | async-start | bytes 524288 | tf_op jit(solution)/shard_map/while/body/eval_jaxpr/psum | solution.py:53
  496.2 5.3 copy-start
  539.9 8.6 collective-permute-start.1
  548.5 42.5 %all-reduce.9.cloned.1.call-start = ((), (), s32[]{:S(2)}) async-start(), calls=%async_computation.2 | async-start | bytes 524288 | tf_op jit(solution)/shard_map/while/body/eval_jaxpr/psum | solution.py:53
  548.5 5.3 copy-start
  592.1 8.6 collective-permute-start.1
  600.7 42.6 %all-reduce.9.cloned.1.call-start = ((), (), s32[]{:S(2)}) async-start(), calls=%async_computation.2 | async-start | bytes 524288 | tf_op jit(solution)/shard_map/while/body/eval_jaxpr/psum | solution.py:53
  600.7 5.3 copy-start
  644.4 8.6 collective-permute-start.1
  653.0 42.5 %all-reduce.9.cloned.1.call-start = ((), (), s32[]{:S(2)}) async-start(), calls=%async_computation.2 | async-start | bytes 524288 | tf_op jit(solution)/shard_map/while/body/eval_jaxpr/psum | solution.py:53
  653.0 5.3 copy-start
  696.6 8.6 collective-permute-start.1
  705.2 42.6 %all-reduce.9.cloned.1.call-start = ((), (), s32[]{:S(2)}) async-start(), calls=%async_computation.2 | async-start | bytes 524288 | tf_op jit(solution)/shard_map/while/body/eval_jaxpr/psum | solution.py:53
  705.2 5.3 copy-start
  748.9 8.6 collective-permute-start.1
  757.4 99.6 %all-reduce.5.cloned.1.call-start = ((), (), s32[]{:S(2)}) async-start(), calls=%async_computation | async-start | bytes 2097152
  757.4 3.7 copy-start.1
  761.2 3.1 copy-start.6
Sparse Core Ops, SparseCore 0:
  46.1 29.2 all-reduce.6
  93.0 33.2 all-reduce.6
  143.9 33.2 all-reduce.6
  194.8 33.2 all-reduce.6
  245.7 33.2 all-reduce.6
  296.5 33.2 all-reduce.6
  347.4 33.2 all-reduce.6
  401.0 33.2 all-reduce.8
  454.9 31.5 all-reduce.8
  507.1 31.5 all-reduce.8
  559.4 31.5 all-reduce.8
  611.6 31.5 all-reduce.8
  663.9 31.5 all-reduce.8
  716.1 31.5 all-reduce.8
Sparse Core Ops, SparseCore 1:
  764.4 92.6 all-reduce.4
where the time goes:
time: 868 us; the launch traced here: 866 us
  waiting for transfers between devices  617 us (71%)
  matrix products  125 us (14%)
  starting transfers between devices  33 us (4%)
  other arithmetic  25.8 us (3%)
  blocking collectives  24.9 us (3%)
  between operations  15.3 us (2%)
  local copies, waits for them, and re-layouts  14.1 us (2%)
  loops' own time  11.5 us (1%)
    psum x14, waiting for transfers between devices, head_sum(): return lax.psum(head_terms.astype(jnp.bfloat16), 'mp').astype(jnp.float32)  446 us
    unnamed x2, waiting for transfers between devices  91.5 us
    ppermute x14, waiting for transfers between devices, from_behind(): return lax.ppermute(array, axis, pairs)  79.6 us
    ppermute x14, starting transfers between devices, from_behind(): return lax.ppermute(array, axis, pairs)  32.9 us
    dot_general x7, matrix products, backward_step(): jnp.einsum('tk,dk->td', d_query, wq_local, preferred_element_type=jnp.flo...  29.6 us
    dot_general x7, matrix products, forward_step(): jnp.dot(attended.reshape(tgt_rows, local_cols), wo_local, preferred_eleme...  26.1 us
    dot_general x7, matrix products, backward_step(): jnp.einsum('td,kd->tk', d_out, wo_local, preferred_element_type=jnp.float32)  25.6 us
    all_gather x1, blocking collectives, per_device(): row_piece = lax.all_gather(memory, ('section', 'mp'), axis=0, tiled=True)  24.9 us
  transfers between devices with their start and end apart: 29, of which 29 were waited for; matrix products, arithmetic and copies ran while one was open for 1% of the time, Pallas kernels for 0%

commit v1 on v0

v1 whole, which is shorter than its diff:
```python
import math

import jax
import jax.numpy as jnp
from jax import lax
from jax.sharding import PartitionSpec as P

HD = 256
NEG_FILL = -1e30
KEEP_SCALE = 8.0 / 7.0
BF = jnp.bfloat16
F32 = jnp.float32


def shifted_right(source_bits, amount):
    return lax.shift_right_logical(source_bits, jnp.full(source_bits.shape, amount, jnp.int32))


def keep_factor(seed_value, first_row, row_count, col_count):
    position = (
        (first_row + jnp.arange(row_count, dtype=jnp.int32))[:, None] * col_count
        + jnp.arange(col_count, dtype=jnp.int32)[None, :]
    )
    hashed = position ^ seed_value * 1640531527
    hashed = hashed ^ shifted_right(hashed, 16)
    hashed = hashed * 2146121005
    hashed = hashed ^ shifted_right(hashed, 15)
    hashed = hashed * 1911520717
    hashed = hashed ^ shifted_right(hashed, 16)
    is_kept = shifted_right(hashed, 8) & 7 != 0
    return jnp.where(is_kept, KEEP_SCALE, 0.0).astype(F32)


def swap(array, axis, k):
    size = lax.axis_size(axis)
    return lax.ppermute(array, axis, [(i, i ^ k) for i in range(size)])


def gather_swaps(array, axis, ks):
    return [array if k == 0 else swap(array, axis, k) for k in ks]


def dot_f32(spec, left, right):
    return jnp.einsum(spec, left, right, preferred_element_type=F32)


def softmax_rows(scores, allowed):
    scores = jnp.where(allowed, scores, NEG_FILL)
    exp_terms = jnp.exp(scores - jnp.max(scores, axis=-1, keepdims=True))
    return exp_terms / jnp.sum(exp_terms, axis=-1, keepdims=True)


def per_device(
    memory, decoder_in, cotangent, src_lengths, tgt_segments, seeds, w_query, w_key, w_value, w_out
):
    micro_count, tgt_rows, dim = decoder_in.shape
    local_cols = w_query.shape[2]
    heads = local_cols // HD
    scale = 1.0 / math.sqrt(HD)
    sections = lax.axis_size("section")
    n_mp = lax.axis_size("mp")
    section = lax.axis_index("section")
    me = lax.axis_index("mp")
    share = n_mp // micro_count
    rows = tgt_rows // share
    src = sections * n_mp
    wq, wk, wv, wo = w_query[0], w_key[0], w_value[0], w_out[0]

    over_z = jnp.concatenate(gather_swaps(memory, "section", range(sections)), axis=0)
    over_x = jnp.stack(gather_swaps(over_z, "mp", range(0, n_mp, 2)), axis=1)
    over_core = jnp.stack(gather_swaps(over_x, "mp", range(2)), axis=2)
    mem_rows = over_core.reshape(src, micro_count, dim)

    def row_ids(device):
        a = jnp.arange(sections, dtype=jnp.int32)[:, None]
        j = jnp.arange(n_mp, dtype=jnp.int32)[None, :]
        return ((section ^ a) * n_mp + (device ^ j)).reshape(src)

    doc_ends = jnp.cumsum(src_lengths, axis=1)

    def allowed_of(owner, heads_owner):
        micro = owner // share
        ends = lax.dynamic_index_in_dim(doc_ends, micro, 0, keepdims=False)
        segments = lax.dynamic_index_in_dim(tgt_segments, micro, 0, keepdims=False)
        segments = lax.dynamic_slice_in_dim(segments, (owner % share) * rows, rows, 0)
        ids = row_ids(heads_owner)
        docs = jnp.sum((ends[None, :] <= ids[:, None]).astype(jnp.int32), axis=1)
        return segments[:, None] == docs[None, :]

    keys = dot_f32("rbd,dk->brk", mem_rows, wk).astype(BF)
    values = dot_f32("rbd,dk->brk", mem_rows, wv).astype(BF)

    def by_owner(array):
        return jnp.stack(
            [
                lax.dynamic_index_in_dim(array, (me ^ j) // share, 0, keepdims=False)
                for j in range(n_mp)
            ]
        )

    keys = by_owner(keys).reshape(n_mp, src, heads, HD)
    values = by_owner(values).reshape(n_mp, src, heads, HD)
    out_fold = jnp.stack(
        [
            dot_f32("jsk,kd->jsd", values[:, :, h], wo[h * HD : (h + 1) * HD]).astype(BF)
            for h in range(heads)
        ],
        axis=1,
    )
    query_fold = jnp.stack(
        [
            dot_f32("jsk,dk->jsd", keys[:, :, h], wq[:, h * HD : (h + 1) * HD]).astype(BF)
            for h in range(heads)
        ],
        axis=1,
    )

    def to_owners(fold):
        blocks = [fold[j] if j == 0 else swap(fold[j], "mp", j) for j in range(n_mp)]
        return jnp.stack(blocks).reshape(n_mp * heads * src, dim)

    out_fold = to_owners(out_fold)
    query_fold = to_owners(query_fold)
    allowed = jnp.stack([allowed_of(me, me ^ k) for k in range(n_mp)], axis=1)
    allowed = jnp.broadcast_to(allowed[:, :, None, :], (rows, n_mp, heads, src))

    my_micro = me // share
    my_first = (me % share) * rows

    def mine(array):
        part = lax.dynamic_index_in_dim(array, my_micro, 0, keepdims=False)
        return lax.dynamic_slice_in_dim(part, my_first, rows, 0)

    factor = keep_factor(seeds[my_micro, 0], my_first, rows, dim)

    def probs(current):
        scores = dot_f32("td,kd->tk", current, query_fold) * scale
        return softmax_rows(scores.reshape(rows, n_mp, heads, src), allowed)

    def layer(current):
        weights = probs(current).astype(BF).reshape(rows, n_mp * heads * src)
        summed = dot_f32("tk,kd->td", weights, out_fold)
        return (current.astype(F32) + factor * summed).astype(BF)

    current = mine(decoder_in)
    for step in range(sections - 1):
        came = lax.ppermute(layer(current), "section", [(step, step + 1)])
        current = jnp.where(section == step + 1, came, current)
    following = layer(current)
    prob_rows = probs(current)

    grad = mine(cotangent)

    def dropped(grad):
        return (grad.astype(F32) * factor).astype(BF)

    for step in range(sections - 1, 0, -1):
        d_probs = dot_f32("td,kd->tk", dropped(grad), out_fold).reshape(prob_rows.shape)
        inner = jnp.sum(prob_rows * d_probs, axis=-1, keepdims=True)
        d_scores = (prob_rows * (d_probs - inner) * scale).astype(BF)
        back = dot_f32("tk,kd->td", d_scores.reshape(rows, -1), query_fold)
        before = (grad.astype(F32) + back).astype(BF)
        came = lax.ppermute(before, "section", [(step, step - 1)])
        grad = jnp.where(section == step - 1, came, grad)

    def all_tokens(array):
        over_x = jnp.stack(gather_swaps(array, "mp", range(0, n_mp, 2)))
        return jnp.stack(gather_swaps(over_x, "mp", range(2)), axis=1).reshape(n_mp * rows, dim)

    every_x = all_tokens(current)
    every_d_out = all_tokens(dropped(grad))
    query = jnp.dot(every_x, wq, preferred_element_type=F32).astype(BF)
    query = query.reshape(n_mp, rows, heads, HD)
    d_att = dot_f32("td,kd->tk", every_d_out, wo).astype(BF).reshape(n_mp, rows, heads, HD)
    own_allowed = jnp.stack([allowed_of(me ^ j, me) for j in range(n_mp)])[:, None]
    own_probs = softmax_rows(dot_f32("jthk,jshk->jhts", query, keys) * scale, own_allowed)
    d_probs = dot_f32("jthk,jshk->jhts", d_att, values)
    inner = jnp.sum(own_probs * d_probs, axis=-1, keepdims=True)
    d_scores = (own_probs * (d_probs - inner) * scale).astype(BF)
    d_keys = dot_f32("jhts,jthk->jshk", d_scores, query).reshape(n_mp, src, local_cols)
    d_values = dot_f32("jhts,jthk->jshk", own_probs.astype(BF), d_att)
    d_values = d_values.reshape(n_mp, src, local_cols)

    def by_micro(array):
        parts = []
        for micro in range(micro_count):
            total = 0.0
            for q in range(share):
                owner = me ^ (micro * share + q)
                total = total + lax.dynamic_index_in_dim(array, owner, 0, keepdims=False)
            parts.append(total.astype(BF))
        return jnp.stack(parts, axis=1)

    terms = dot_f32("rbk,dk->rbd", by_micro(d_keys), wk) + dot_f32(
        "rbk,dk->rbd", by_micro(d_values), wv
    )
    terms = terms.reshape(sections, n_mp // 2, 2, micro_count, dim)
    half = terms[:, :, 0] + swap(terms[:, :, 1].astype(BF), "mp", 1).astype(F32)
    total = half[:, 0]
    for j in range(1, n_mp // 2):
        total = total + swap(half[:, j].astype(BF), "mp", 2 * j).astype(F32)
    mem_grad = total[0]
    for a in range(1, sections):
        mem_grad = mem_grad + swap(total[a].astype(BF), "section", a).astype(F32)

    out_cols = dim // n_mp
    following = following.reshape(rows, n_mp, out_cols)
    blocks = []
    for j in range(n_mp):
        part = lax.dynamic_index_in_dim(following, me ^ j, 1, keepdims=False)
        blocks.append(part if j == 0 else swap(part, "mp", j))
    stacked = jnp.stack(blocks)
    ordered = [
        lax.dynamic_index_in_dim(stacked, me ^ owner, 0, keepdims=False) for owner in range(n_mp)
    ]
    section_out = jnp.stack(ordered).reshape(1, micro_count, tgt_rows, out_cols)
    return (section_out, mem_grad[None])


def solution(mesh):
    return jax.shard_map(
        per_device,
        mesh=mesh,
        in_specs=(
            P(("section", "mp"), "groups", None),
            P("groups", None, None),
            P("groups", None, None),
            P("groups", None),
            P("groups", None),
            P("groups", "section"),
            P("section", None, "mp"),
            P("section", None, "mp"),
            P("section", None, "mp"),
            P("section", "mp", None),
        ),
        out_specs=(P("section", "groups", None, "mp"), P(("section", "mp"), "groups", None)),
        check_vma=False,
    )
```

time: 868 us -> 154 us (0.18)
  waiting for transfers between devices: 617 us -> 64.5 us
  matrix products: 125 us -> 40 us
  blocking collectives: 24.9 us -> 0 us
  other arithmetic: 25.8 us -> 10.2 us
  between operations: 15.3 us -> 1.35 us
  loops' own time: 11.5 us -> 0 us
    psum x14 -> x0, waiting for transfers between devices: 446 us -> none  [head_sum(): return lax.psum(head_terms.astype(jnp.bfloat16), 'mp').astype(jnp.float32)]
    unnamed x2 -> x0, waiting for transfers between devices: 91.5 us -> none
    dot_general x74 -> x27, matrix products: 122 us -> 39.8 us  [the longest x26 39.1 us: dot_f32(): return jnp.einsum(spec, left, right, preferred_element_type=F32)]
    all_gather x1 -> x0, blocking collectives: 24.9 us -> none  [per_device(): row_piece = lax.all_gather(memory, ('section', 'mp'), axis=0, tiled=True)]
    select_n x21 -> x5, other arithmetic: 17.5 us -> 0.15 us  [the longest x3 0.09 us: per_device(): current = jnp.where(section == step + 1, came, current)]
    ppermute x14 -> x29, waiting for transfers between devices: 79.6 us -> 64.5 us  [the longest x23 32.3 us: swap(): return lax.ppermute(array, axis, [(i, i ^ k) for i in range(size)])]
    another operation x2 -> x0, loops' own time: 11.5 us -> none  [the longest x1 7.05 us: per_device(): lax.fori_loop(0, step_count, backward_step, (zero_rows, grads_init))]
    ppermute x14 -> x29, starting transfers between devices: 32.9 us -> 29.2 us  [the longest x23 23.3 us: swap(): return lax.ppermute(array, axis, [(i, i ^ k) for i in range(size)])]
  transfers between devices with their start and end apart: 29 -> 29, of which waited for: 29 -> 16; matrix products, arithmetic and copies ran while one was open for 1% -> 16% of each run, Pallas kernels for 0% -> 0%
where the time goes in v1:
time: 154 us; the launch traced here: 153 us
  waiting for transfers between devices  64.5 us (42%)
  matrix products  40 us (26%)
  starting transfers between devices  29.2 us (19%)
  other arithmetic  10.2 us (7%)
  local copies, waits for them, and re-layouts  7.75 us (5%)
    dot_general x26, matrix products, dot_f32(): return jnp.einsum(spec, left, right, preferred_element_type=F32)  39.1 us
    ppermute x23, waiting for transfers between devices, swap(): return lax.ppermute(array, axis, [(i, i ^ k) for i in range(size)])  32.3 us
    ppermute x3, waiting for transfers between devices, per_device(): came = lax.ppermute(before, 'section', [(step, step - 1)])  26.6 us
    ppermute x23, starting transfers between devices, swap(): return lax.ppermute(array, axis, [(i, i ^ k) for i in range(size)])  23.3 us
    ppermute x3, waiting for transfers between devices, per_device(): came = lax.ppermute(layer(current), 'section', [(step, step + 1)])  5.65 us
    ppermute x3, starting transfers between devices, per_device(): came = lax.ppermute(before, 'section', [(step, step - 1)])  3.09 us
  transfers between devices with their start and end apart: 29, of which 16 were waited for; matrix products, arithmetic and copies ran while one was open for 16% of the time, Pallas kernels for 0%

profile of v1, /device:TPU:0, one launch (start us, length us, event | category | flops | bytes accessed | tf_op | source)
XLA Modules:
  0.0 152.9 jit_solution(518502400387656206)
XLA Ops:
  0.6 3.1 %collective-permute-start = (bf16[1,4,4096]{2,1,0:T(4,128)(2,1)}, bf16[1,4,4096]{2,1,0:T(4,128)(2,1)S(1)}, u32[]{:S(2)}, u32[]{:S(2)}) collective-permute-start(bf16[1,4,4096]{2,1,0:T(4,128)(2,1)} %param.10), channel_id=1, source_target_pairs={{0,4},{4,0},{8,12},{12,8},{1,5},{5,1},{9,13},{13,9},{2,6},{6,2},{1... | collective-permute-start | bytes 98312 | tf_op jit(solution)/shard_map/ppermute | solution.py:36
  3.7 2.6 %collective-permute-start.1 = (bf16[1,4,4096]{2,1,0:T(4,128)(2,1)}, bf16[1,4,4096]{2,1,0:T(4,128)(2,1)S(1)}, u32[]{:S(2)}, u32[]{:S(2)}) collective-permute-start(bf16[1,4,4096]{2,1,0:T(4,128)(2,1)} %param.10), channel_id=1, source_target_pairs={{0,8},{4,12},{8,0},{12,4},{1,9},{5,13},{9,1},{13,5},{2,10},{6,14},... | collective-permute-start | bytes 98312 | tf_op jit(solution)/shard_map/ppermute | solution.py:36
  6.3 0.8 constant_dynamic-update-slice_fusion.3
  7.3 0.8 fusion.226
  8.2 0.9 reduce_window_sum.11
  9.3 2.9 %collective-permute-done.2 = bf16[1,4,4096]{2,1,0:T(4,128)(2,1)S(1)} collective-permute-done((bf16[1,4,4096]{2,1,0:T(4,128)(2,1)}, bf16[1,4,4096]{2,1,0:T(4,128)(2,1)S(1)}, u32[]{:S(2)}, u32[]{:S(2)}) %collective-permute-start.2) | collective-permute-done | bytes 32800 | tf_op jit(solution)/shard_map/ppermute | solution.py:36
  12.3 1.6 %collective-permute-start.3 = (bf16[4,4,4096]{2,1,0:T(4,128)(2,1)S(1)}, bf16[4,4,4096]{2,1,0:T(4,128)(2,1)S(1)}, u32[]{:S(2)}, u32[]{:S(2)}) collective-permute-start(bf16[4,4,4096]{2,1,0:T(4,128)(2,1)S(1)} %constant_dynamic-update-slice_fusion), channel_id=1, source_target_pairs={{0,2},{1,3},{2,0},{3,1},{4,6},{5,7},{6,4},{7,5},{8,10},{9,11},{10,... | collective-permute-start | bytes 393224 | tf_op jit(solution)/shard_map/ppermute | solution.py:36
  14.3 3.0 %collective-permute-done.3 = bf16[4,4,4096]{2,1,0:T(4,128)(2,1)S(1)} collective-permute-done((bf16[4,4,4096]{2,1,0:T(4,128)(2,1)S(1)}, bf16[4,4,4096]{2,1,0:T(4,128)(2,1)S(1)}, u32[]{:S(2)}, u32[]{:S(2)}) %collective-permute-start.3) | collective-permute-done | bytes 131104 | tf_op jit(solution)/shard_map/ppermute | solution.py:36
  17.7 1.2 fusion.281
  20.2 3.0 %fusion.41 = bf16[16,4,512]{2,0,1:T(8,128)(2,1)S(1)} fusion(bf16[16,4,4096]{2,0,1:T(8,128)(2,1)S(1)} %reshape.750, bf16[1,4096,512]{2,1,0:T(8,128)(2,1)} %param.17), kind=kOutput, calls=%fused_computation.71 | convolution fusion | flops 268468224 | bytes 4784128 | tf_op jit(solution)/shard_map/rbd,dk->brk/dot_general | solution.py:44
  23.4 2.5 %fusion.9 = bf16[4,1,16,4096]{3,2,0,1:T(8,128)(2,1)S(1)} fusion(bf16[4096,512]{1,0:T(8,128)(2,1)} %bitcast.335, bf16[4,16,1,256]{3,2,1,0:T(2,128)(2,1)S(1)} %get-tuple-element.50), kind=kOutput, calls=%fused_computation.14 | convolution fusion | flops 134479872 | bytes 2654208 | tf_op jit(solution)/shard_map/jsk,dk->jsd/dot_general | solution.py:44
  25.9 2.3 %fusion.10 = bf16[4,1,16,4096]{3,2,0,1:T(8,128)(2,1)S(1)} fusion(bf16[4096,512]{1,0:T(8,128)(2,1)} %bitcast.336, bf16[4,16,1,256]{3,2,1,0:T(2,128)(2,1)S(1)} %get-tuple-element.51), kind=kOutput, calls=%fused_computation.15 | convolution fusion | flops 134479872 | bytes 2654208 | tf_op jit(solution)/shard_map/jsk,dk->jsd/dot_general | solution.py:44
  28.3 0.9 fusion.107
  29.2 1.4 collective-permute-start.7
  31.1 0.8 fusion.44
  32.2 2.2 %fusion.11 = bf16[4,1,16,4096]{3,2,0,1:T(8,128)(2,1)S(1)} fusion(bf16[1,512,4096]{2,1,0:T(8,128)(2,1)} %param.19, bf16[4,16,1,256]{3,2,1,0:T(2,128)(2,1)S(1)} %get-tuple-element.44), kind=kOutput, calls=%fused_computation.16 | convolution fusion | flops 134479872 | bytes 2654208 | tf_op jit(solution)/shard_map/jsk,kd->jsd/dot_general | solution.py:44
  34.3 2.1 %fusion.12 = bf16[4,1,16,4096]{3,2,0,1:T(8,128)(2,1)S(1)} fusion(bf16[1,512,4096]{2,1,0:T(8,128)(2,1)} %param.19, bf16[4,16,1,256]{3,2,1,0:T(2,128)(2,1)S(1)} %get-tuple-element.45), kind=kOutput, calls=%fused_computation.17 | convolution fusion | flops 134479872 | bytes 2654208 | tf_op jit(solution)/shard_map/jsk,kd->jsd/dot_general | solution.py:44
  36.4 0.9 fusion.101
  37.3 1.6 %collective-permute-start.10 = (bf16[2,16,4096]{2,1,0:T(8,128)(2,1)}, bf16[2,16,4096]{2,1,0:T(8,128)(2,1)}, u32[]{:S(2)}, u32[]{:S(2)}) collective-permute-start(bf16[2,16,4096]{2,1,0:T(8,128)(2,1)} %get-tuple-element.13), channel_id=1, source_target_pairs={{0,3},{1,2},{2,1},{3,0},{4,7},{5,6},{6,5},{7,4},{8,11},{9,10},{10,... | collective-permute-start | bytes 786440 | tf_op jit(solution)/shard_map/ppermute | solution.py:36
  39.5 4.7 %collective-permute-done.6 = bf16[2,16,4096]{2,1,0:T(8,128)(2,1)} collective-permute-done((bf16[2,16,4096]{2,1,0:T(8,128)(2,1)}, bf16[2,16,4096]{2,1,0:T(8,128)(2,1)}, u32[]{:S(2)}, u32[]{:S(2)}) %collective-permute-start.6) | collective-permute-done | bytes 262176 | tf_op jit(solution)/shard_map/ppermute | solution.py:36
  44.1 1.2 pad_maximum_fusion
  45.9 2.9 %collective-permute-done.10 = bf16[2,16,4096]{2,1,0:T(8,128)(2,1)} collective-permute-done((bf16[2,16,4096]{2,1,0:T(8,128)(2,1)}, bf16[2,16,4096]{2,1,0:T(8,128)(2,1)}, u32[]{:S(2)}, u32[]{:S(2)}) %collective-permute-start.10) | collective-permute-done | bytes 262176 | tf_op jit(solution)/shard_map/ppermute | solution.py:36
  48.9 6.1 %collective-permute-done.9 = bf16[2,16,4096]{2,1,0:T(8,128)(2,1)} collective-permute-done((bf16[2,16,4096]{2,1,0:T(8,128)(2,1)}, bf16[2,16,4096]{2,1,0:T(8,128)(2,1)}, u32[]{:S(2)}, u32[]{:S(2)}) %collective-permute-start.9) | collective-permute-done | bytes 262176 | tf_op jit(solution)/shard_map/ppermute | solution.py:36
  54.9 2.3 %fusion.21 = bf16[32,4096]{1,0:T(8,128)(2,1)S(1)} fusion(s32[]{:T(128)} %bitcast.1, s32[32]{0:T(128)S(1)} %iota_multiply_fusion, bf16[4,32,4096]{2,1,0:T(8,128)(2,1)S(1)} %copy-done.4, s32[]{:T(128)S(6)} %select_n.175, f32[32,4,2]{0,2,1:T(2,128)S(1)} %fusion.282, f32[32,4,2,16]{0,3,2,1:T(8,128)S(1)} %bitcast.361, pred[32,4,16]{0,2,1:T(8,128)(4,1)S(1)} %pad_add_fusion, ...), kind=kOutput, calls=%fused_computation.33 | convolution fusion | flops 37503248 | bytes 1592456 | tf_op jit(solution)/shard_map/tk,kd->td/dot_general | solution.py:44
  57.2 1.3 collective-permute-start.11
  58.6 5.6 %collective-permute-done.11 = bf16[32,4096]{1,0:T(8,128)(2,1)S(1)} collective-permute-done((bf16[32,4096]{1,0:T(8,128)(2,1)S(1)}, bf16[32,4096]{1,0:T(8,128)(2,1)S(1)}, u32[]{:S(2)}, u32[]{:S(2)}) %collective-permute-start.11) | collective-permute-done | bytes 262176 | tf_op jit(solution)/shard_map/ppermute | solution.py:147
  64.9 2.3 %add_convert_fusion.2 = bf16[32,4096]{1,0:T(8,128)(2,1)S(1)} fusion(bf16[32,4096]{1,0:T(8,128)(2,1)S(1)} %bitcast_select_fusion.1, s32[]{:T(128)} %bitcast.1, s32[32]{0:T(128)S(1)} %iota_multiply_fusion, f32[32,4,2]{0,2,1:T(2,128)S(1)} %fusion.283, f32[32,4,2,16]{0,3,2,1:T(8,128)S(1)} %bitcast.363, pred[32,4,16]{0,2,1:T(8,128)(4,1)S(1)} %pad_add_fusion, ...), kind=kOutput, calls=%fused_computation.137 | convolution fusion | flops 37503248 | bytes 1592452 | tf_op jit(solution)/shard_map/tk,kd->td/dot_general | solution.py:44
  67.2 0.8 collective-permute-start.12
  68.7 2.3 %add_convert_fusion.1 = bf16[32,4096]{1,0:T(8,128)(2,1)S(1)} fusion(bf16[32,4096]{1,0:T(8,128)(2,1)S(1)} %broadcast_select_fusion.1, s32[]{:T(128)} %bitcast.1, s32[32]{0:T(128)S(1)} %iota_multiply_fusion, f32[32,4,2]{0,2,1:T(2,128)S(1)} %fusion.284, f32[32,4,2,16]{0,3,2,1:T(8,128)S(1)} %bitcast.365, pred[32,4,16]{0,2,1:T(8,128)(4,1)S(1)} %pad_add_fusion, ...), kind=kOutput, calls=%fused_computation.136 | convolution fusion | flops 37503248 | bytes 1592452 | tf_op jit(solution)/shard_map/tk,kd->td/dot_general | solution.py:44
  71.0 0.7 collective-permute-start.13
  71.7 2.4 %fusion.89 = f32[32,4,2,16]{0,3,2,1:T(8,128)S(1)} fusion(s32[]{:T(128)} %bitcast.1, s32[32]{0:T(128)S(1)} %iota_multiply_fusion, bf16[4,32,4096]{2,1,0:T(8,128)(2,1)S(1)} %copy-done.5, s32[]{:T(128)S(6)} %select_n.175, bf16[1,2,16,4096]{3,2,1,0:T(8,128)(2,1)} %bitcast.48, bf16[1,2,16,4096]{3,2,1,0:T(8,128)(2,1)} %bitcast.46, ...), kind=kOutput, calls=%fused_computation.139 | convolution fusion | flops 39976960 | bytes 1327624 | tf_op jit(solution)/shard_map/td,kd->tk/dot_general | solution.py:44
  75.3 0.7 collective-permute-start.19
  76.2 2.4 %fusion.96 = f32[32,4,2,16]{0,3,2,1:T(8,128)S(1)} fusion(bf16[32,4096]{1,0:T(8,128)(2,1)S(1)} %bitcast_select_fusion, s32[]{:T(128)} %bitcast.1, s32[32]{0:T(128)S(1)} %iota_multiply_fusion, bf16[1,2,16,4096]{3,2,1,0:T(8,128)(2,1)} %bitcast.48, bf16[1,2,16,4096]{3,2,1,0:T(8,128)(2,1)} %bitcast.46, bf16[1,2,16,4096]{3,2,1,0:T(8,128)(2,1)} %bitcast.44, ...), kind=kOutput, calls=%fused_computation.144 | convolution fusion | flops 39976960 | bytes 1327236 | tf_op jit(solution)/shard_map/td,kd->tk/dot_general | solution.py:44
  78.9 0.7 collective-permute-start.20
  79.7 1.6 %collective-permute-start.17 = (bf16[32,4096]{1,0:T(8,128)(2,1)S(1)}, bf16[32,4096]{1,0:T(8,128)(2,1)S(1)}, u32[]{:S(2)}, u32[]{:S(2)}) collective-permute-start(bf16[32,4096]{1,0:T(8,128)(2,1)S(1)} %broadcast_select_fusion.2), channel_id=1, source_target_pairs={{0,2},{1,3},{2,0},{3,1},{4,6},{5,7},{6,4},{7,5},{8,10},{9,11},{10,... | collective-permute-start | bytes 786440 | tf_op jit(solution)/shard_map/ppermute | solution.py:36
  81.3 2.4 %fusion.93 = f32[32,4,2,16]{0,3,2,1:T(8,128)S(1)} fusion(bf16[32,4096]{1,0:T(8,128)(2,1)S(1)} %broadcast_select_fusion, s32[]{:T(128)} %bitcast.1, s32[32]{0:T(128)S(1)} %iota_multiply_fusion, bf16[1,2,16,4096]{3,2,1,0:T(8,128)(2,1)} %bitcast.48, bf16[1,2,16,4096]{3,2,1,0:T(8,128)(2,1)} %bitcast.46, bf16[1,2,16,4096]{3,2,1,0:T(8,128)(2,1)} %bitcast.44, ...), kind=kOutput, calls=%fused_computation.142 | convolution fusion | flops 39976960 | bytes 1327236 | tf_op jit(solution)/shard_map/td,kd->tk/dot_general | solution.py:44
  84.0 1.7 %collective-permute-start.21 = (bf16[32,4096]{1,0:T(8,128)(2,1)S(1)}, bf16[32,4096]{1,0:T(8,128)(2,1)S(1)}, u32[]{:S(2)}, u32[]{:S(2)}) collective-permute-start(bf16[32,4096]{1,0:T(8,128)(2,1)S(1)} %fusion.24), channel_id=1, source_target_pairs={{4,0},{5,1},{6,2},{7,3},{20,16},{21,17},{22,18},{23,19}} | collective-permute-start | bytes 786440 | tf_op jit(solution)/shard_map/ppermute | solution.py:163
  85.7 1.3 collective-permute-done.17
  87.2 26.6 %collective-permute-done.21 = bf16[32,4096]{1,0:T(8,128)(2,1)S(1)} collective-permute-done((bf16[32,4096]{1,0:T(8,128)(2,1)S(1)}, bf16[32,4096]{1,0:T(8,128)(2,1)S(1)}, u32[]{:S(2)}, u32[]{:S(2)}) %collective-permute-start.21) | collective-permute-done | bytes 262176 | tf_op jit(solution)/shard_map/ppermute | solution.py:163
  113.8 1.0 fusion.86
  114.8 1.6 %collective-permute-start.22 = (bf16[32,4096]{1,0:T(8,128)(2,1)S(1)}, bf16[32,4096]{1,0:T(8,128)(2,1)S(1)}, u32[]{:S(2)}, u32[]{:S(2)}) collective-permute-start(bf16[32,4096]{1,0:T(8,128)(2,1)S(1)} %fusion.86), channel_id=1, source_target_pairs={{0,2},{1,3},{2,0},{3,1},{4,6},{5,7},{6,4},{7,5},{8,10},{9,11},{10,... | collective-permute-start | bytes 786440 | tf_op jit(solution)/shard_map/ppermute | solution.py:36
  116.6 4.7 %collective-permute-done.22 = bf16[32,4096]{1,0:T(8,128)(2,1)S(1)} collective-permute-done((bf16[32,4096]{1,0:T(8,128)(2,1)S(1)}, bf16[32,4096]{1,0:T(8,128)(2,1)S(1)}, u32[]{:S(2)}, u32[]{:S(2)}) %collective-permute-start.22) | collective-permute-done | bytes 262176 | tf_op jit(solution)/shard_map/ppermute | solution.py:36
  121.4 0.7 convolution_convert_fusion.4
  122.4 0.9 collective-permute-done.23
  123.5 1.1 copy-done.3
  124.6 1.5 fusion.38
  126.7 3.7 %fusion.30 = f32[16,4,4096]{2,0,1:T(8,128)S(1)} fusion(bf16[1,4096,512]{2,1,0:T(8,128)(2,1)} %param.17, bf16[16,1,512]{2,0,1:T(8,128)(2,1)S(1)} %get-tuple-element.41, bf16[16,1,512]{2,0,1:T(8,128)(2,1)S(1)} %get-tuple-element.42, bf16[16,1,512]{2,0,1:T(8,128)(2,1)S(1)} %get-tuple-element.43, bf16[16,1,512]{2,0,1:T(8,128)(2,1)S(1)} %get-tuple-element.40), kind=kOutput, calls=%fused_computation.42 | convolution fusion | flops 268533760 | bytes 5308416 | tf_op jit(solution)/shard_map/rbk,dk->rbd/dot_general | solution.py:44
  130.4 1.4 convolution_add_fusion
  131.8 0.6 reshape.766
  132.4 0.6 slice.128
  133.4 0.6 collective-permute-start.24
  133.9 2.3 %add_convert_fusion = bf16[32,4096]{1,0:T(8,128)(2,1)S(1)} fusion(bf16[32,4096]{1,0:T(8,128)(2,1)S(1)} %broadcast_select_fusion.2, s32[]{:T(128)} %bitcast.1, s32[32]{0:T(128)S(1)} %iota_multiply_fusion, f32[32,4,2]{0,2,1:T(2,128)S(1)} %get-tuple-element.72, f32[32,4,2,16]{0,3,2,1:T(8,128)S(1)} %bitcast.345, pred[32,4,16]{0,2,1:T(8,128)(4,1)S(1)} %pad_add_fusion, ...), kind=kOutput, calls=%fused_computation.135 | convolution fusion | flops 37503248 | bytes 1592452 | tf_op jit(solution)/shard_map/tk,kd->td/dot_general | solution.py:44
  136.4 0.6 constant_dynamic-slice_fusion.13
  137.0 1.2 collective-permute-start.16
  138.2 0.6 collective-permute-start.15
  140.0 1.6 %collective-permute-start.25 = (bf16[4,4,4096]{2,1,0:T(4,128)(2,1)S(1)}, bf16[4,4,4096]{2,1,0:T(4,128)(2,1)S(1)}, u32[]{:S(2)}, u32[]{:S(2)}) collective-permute-start(bf16[4,4,4096]{2,1,0:T(4,128)(2,1)S(1)} %fusion.133), channel_id=1, source_target_pairs={{0,2},{1,3},{2,0},{3,1},{4,6},{5,7},{6,4},{7,5},{8,10},{9,11},{10,... | collective-permute-start | bytes 393224 | tf_op jit(solution)/shard_map/ppermute | solution.py:36
  141.6 1.3 collective-permute-done.15
  142.9 2.8 %collective-permute-done.25 = bf16[4,4,4096]{2,1,0:T(4,128)(2,1)S(1)} collective-permute-done((bf16[4,4,4096]{2,1,0:T(4,128)(2,1)S(1)}, bf16[4,4,4096]{2,1,0:T(4,128)(2,1)S(1)}, u32[]{:S(2)}, u32[]{:S(2)}) %collective-permute-start.25) | collective-permute-done | bytes 131104 | tf_op jit(solution)/shard_map/ppermute | solution.py:36
  146.0 1.0 collective-permute-start.27
  147.0 3.4 %collective-permute-start.26 = (bf16[4,4096]{1,0:T(4,128)(2,1)S(1)}, bf16[4,4096]{1,0:T(4,128)(2,1)S(1)}, u32[]{:S(2)}, u32[]{:S(2)}) collective-permute-start(bf16[4,4096]{1,0:T(4,128)(2,1)S(1)} %get-tuple-element.33), channel_id=1, source_target_pairs={{0,4},{4,0},{8,12},{12,8},{1,5},{5,1},{9,13},{13,9},{2,6},{6,2},{1... | collective-permute-start | bytes 98312 | tf_op jit(solution)/shard_map/ppermute | solution.py:36
  150.4 0.7 maximum_bitcast_fusion
  151.1 0.6 collective-permute-done.28
  151.7 0.6 collective-permute-done.26
  152.3 0.7 fusion.146
  (119 shorter events, 11.5 us)
Async XLA Ops:
  0.6 8.4 %collective-permute-start = (bf16[1,4,4096]{2,1,0:T(4,128)(2,1)}, bf16[1,4,4096]{2,1,0:T(4,128)(2,1)S(1)}, u32[]{:S(2)}, u32[]{:S(2)}) collective-permute-start(bf16[1,4,4096]{2,1,0:T(4,128)(2,1)} %param.10), channel_id=1, source_target_pairs={{0,4},{4,0},{8,12},{12,8},{1,5},{5,1},{9,13},{13,9},{2,6},{6,2},{1... | collective-permute-start | bytes 98312 | tf_op jit(solution)/shard_map/ppermute | solution.py:36
  3.7 5.6 %collective-permute-start.1 = (bf16[1,4,4096]{2,1,0:T(4,128)(2,1)}, bf16[1,4,4096]{2,1,0:T(4,128)(2,1)S(1)}, u32[]{:S(2)}, u32[]{:S(2)}) collective-permute-start(bf16[1,4,4096]{2,1,0:T(4,128)(2,1)} %param.10), channel_id=1, source_target_pairs={{0,8},{4,12},{8,0},{12,4},{1,9},{5,13},{9,1},{13,5},{2,10},{6,14},... | collective-permute-start | bytes 98312 | tf_op jit(solution)/shard_map/ppermute | solution.py:36
  6.3 5.9 %collective-permute-start.2 = (bf16[1,4,4096]{2,1,0:T(4,128)(2,1)}, bf16[1,4,4096]{2,1,0:T(4,128)(2,1)S(1)}, u32[]{:S(2)}, u32[]{:S(2)}) collective-permute-start(bf16[1,4,4096]{2,1,0:T(4,128)(2,1)} %param.10), channel_id=1, source_target_pairs={{0,12},{4,8},{8,4},{12,0},{1,13},{5,9},{9,5},{13,1},{2,14},{6,10},... | collective-permute-start | bytes 98312 | tf_op jit(solution)/shard_map/ppermute | solution.py:36
  12.3 5.0 %collective-permute-start.3 = (bf16[4,4,4096]{2,1,0:T(4,128)(2,1)S(1)}, bf16[4,4,4096]{2,1,0:T(4,128)(2,1)S(1)}, u32[]{:S(2)}, u32[]{:S(2)}) collective-permute-start(bf16[4,4,4096]{2,1,0:T(4,128)(2,1)S(1)} %constant_dynamic-update-slice_fusion), channel_id=1, source_target_pairs={{0,2},{1,3},{2,0},{3,1},{4,6},{5,7},{6,4},{7,5},{8,10},{9,11},{10,... | collective-permute-start | bytes 393224 | tf_op jit(solution)/shard_map/ppermute | solution.py:36
  17.5 1.6 %collective-permute-start.4 = (bf16[4,2,4,4096]{3,2,0,1:T(4,128)(2,1)S(1)}, bf16[4,2,4,4096]{3,2,0,1:T(4,128)(2,1)S(1)}, u32[]{:S(2)}, u32[]{:S(2)}) collective-permute-start(bf16[4,2,4,4096]{3,2,0,1:T(4,128)(2,1)S(1)} %get-tuple-element.32), channel_id=1, source_target_pairs={{0,1},{1,0},{2,3},{3,2},{4,5},{5,4},{6,7},{7,6},{8,9},{9,8},{10,11... | collective-permute-start | bytes 786440 | tf_op jit(solution)/shard_map/ppermute | solution.py:36
  23.3 7.8 %copy-start = (bf16[1,4096,512]{2,1,0:T(8,128)(2,1)S(1)}, bf16[1,4096,512]{2,1,0:T(8,128)(2,1)}, u32[]{:S(2)}) copy-start(bf16[1,4096,512]{2,1,0:T(8,128)(2,1)} %param.18) | copy-start | bytes 12582916
  29.2 10.3 %collective-permute-start.7 = (bf16[2,16,4096]{2,1,0:T(8,128)(2,1)}, bf16[2,16,4096]{2,1,0:T(8,128)(2,1)S(1)}, u32[]{:S(2)}, u32[]{:S(2)}) collective-permute-start(bf16[2,16,4096]{2,1,0:T(8,128)(2,1)} %get-tuple-element.17), channel_id=1, source_target_pairs={{0,3},{1,2},{2,1},{3,0},{4,7},{5,6},{6,5},{7,4},{8,11},{9,10},{10,... | collective-permute-start | bytes 786440 | tf_op jit(solution)/shard_map/ppermute | solution.py:36
  30.6 13.6 %collective-permute-start.6 = (bf16[2,16,4096]{2,1,0:T(8,128)(2,1)}, bf16[2,16,4096]{2,1,0:T(8,128)(2,1)}, u32[]{:S(2)}, u32[]{:S(2)}) collective-permute-start(bf16[2,16,4096]{2,1,0:T(8,128)(2,1)} %get-tuple-element.18), channel_id=1, source_target_pairs={{0,2},{1,3},{2,0},{3,1},{4,6},{5,7},{6,4},{7,5},{8,10},{9,11},{10,... | collective-permute-start | bytes 786440 | tf_op jit(solution)/shard_map/ppermute | solution.py:36
  31.1 13.0 %collective-permute-start.5 = (bf16[2,16,4096]{2,1,0:T(8,128)(2,1)S(1)}, bf16[2,16,4096]{2,1,0:T(8,128)(2,1)}, u32[]{:S(2)}, u32[]{:S(2)}) collective-permute-start(bf16[2,16,4096]{2,1,0:T(8,128)(2,1)S(1)} %get-tuple-element.16), channel_id=1, source_target_pairs={{0,1},{1,0},{2,3},{3,2},{4,5},{5,4},{6,7},{7,6},{8,9},{9,8},{10,11... | collective-permute-start | bytes 786440 | tf_op jit(solution)/shard_map/ppermute | solution.py:36
  32.2 13.2 %copy-start.4 = (bf16[4,32,4096]{2,1,0:T(8,128)(2,1)S(1)}, bf16[4,32,4096]{2,1,0:T(8,128)(2,1)}, u32[]{:S(2)}) copy-start(bf16[4,32,4096]{2,1,0:T(8,128)(2,1)} %param.11) | copy-start | bytes 3145732
  37.3 11.5 %collective-permute-start.10 = (bf16[2,16,4096]{2,1,0:T(8,128)(2,1)}, bf16[2,16,4096]{2,1,0:T(8,128)(2,1)}, u32[]{:S(2)}, u32[]{:S(2)}) collective-permute-start(bf16[2,16,4096]{2,1,0:T(8,128)(2,1)} %get-tuple-element.13), channel_id=1, source_target_pairs={{0,3},{1,2},{2,1},{3,0},{4,7},{5,6},{6,5},{7,4},{8,11},{9,10},{10,... | collective-permute-start | bytes 786440 | tf_op jit(solution)/shard_map/ppermute | solution.py:36
  38.9 16.0 %collective-permute-start.9 = (bf16[2,16,4096]{2,1,0:T(8,128)(2,1)}, bf16[2,16,4096]{2,1,0:T(8,128)(2,1)}, u32[]{:S(2)}, u32[]{:S(2)}) collective-permute-start(bf16[2,16,4096]{2,1,0:T(8,128)(2,1)} %get-tuple-element.14), channel_id=1, source_target_pairs={{0,2},{1,3},{2,0},{3,1},{4,6},{5,7},{6,4},{7,5},{8,10},{9,11},{10,... | collective-permute-start | bytes 786440 | tf_op jit(solution)/shard_map/ppermute | solution.py:36
  39.5 15.5 %collective-permute-start.8 = (bf16[2,16,4096]{2,1,0:T(8,128)(2,1)}, bf16[2,16,4096]{2,1,0:T(8,128)(2,1)}, u32[]{:S(2)}, u32[]{:S(2)}) collective-permute-start(bf16[2,16,4096]{2,1,0:T(8,128)(2,1)} %get-tuple-element.12), channel_id=1, source_target_pairs={{0,1},{1,0},{2,3},{3,2},{4,5},{5,4},{6,7},{7,6},{8,9},{9,8},{10,11... | collective-permute-start | bytes 786440 | tf_op jit(solution)/shard_map/ppermute | solution.py:36
  57.2 7.0 %collective-permute-start.11 = (bf16[32,4096]{1,0:T(8,128)(2,1)S(1)}, bf16[32,4096]{1,0:T(8,128)(2,1)S(1)}, u32[]{:S(2)}, u32[]{:S(2)}) collective-permute-start(bf16[32,4096]{1,0:T(8,128)(2,1)S(1)} %fusion.21), channel_id=1, source_target_pairs={{0,4},{1,5},{2,6},{3,7},{16,20},{17,21},{18,22},{19,23}} | collective-permute-start | bytes 786440 | tf_op jit(solution)/shard_map/ppermute | solution.py:147
  67.1 4.6 %copy-start.5 = (bf16[4,32,4096]{2,1,0:T(8,128)(2,1)S(1)}, bf16[4,32,4096]{2,1,0:T(8,128)(2,1)}, u32[]{:S(2)}) copy-start(bf16[4,32,4096]{2,1,0:T(8,128)(2,1)} %param.12) | copy-start | bytes 3145732
  67.2 0.9 collective-permute-start.12
  71.0 3.1 %collective-permute-start.13 = (bf16[32,4096]{1,0:T(8,128)(2,1)S(1)}, bf16[32,4096]{1,0:T(8,128)(2,1)S(1)}, u32[]{:S(2)}, u32[]{:S(2)}) collective-permute-start(bf16[32,4096]{1,0:T(8,128)(2,1)S(1)} %add_convert_fusion.1), channel_id=1, source_target_pairs={{8,12},{9,13},{10,14},{11,15},{24,28},{25,29},{26,30},{27,31}} | collective-permute-start | bytes 786440 | tf_op jit(solution)/shard_map/ppermute | solution.py:147
  75.3 0.8 collective-permute-start.19
  78.9 2.3 %collective-permute-start.20 = (bf16[32,4096]{1,0:T(8,128)(2,1)S(1)}, bf16[32,4096]{1,0:T(8,128)(2,1)S(1)}, u32[]{:S(2)}, u32[]{:S(2)}) collective-permute-start(bf16[32,4096]{1,0:T(8,128)(2,1)S(1)} %fusion.23), channel_id=1, source_target_pairs={{8,4},{9,5},{10,6},{11,7},{24,20},{25,21},{26,22},{27,23}} | collective-permute-start | bytes 786440 | tf_op jit(solution)/shard_map/ppermute | solution.py:163
  79.7 7.4 %collective-permute-start.17 = (bf16[32,4096]{1,0:T(8,128)(2,1)S(1)}, bf16[32,4096]{1,0:T(8,128)(2,1)S(1)}, u32[]{:S(2)}, u32[]{:S(2)}) collective-permute-start(bf16[32,4096]{1,0:T(8,128)(2,1)S(1)} %broadcast_select_fusion.2), channel_id=1, source_target_pairs={{0,2},{1,3},{2,0},{3,1},{4,6},{5,7},{6,4},{7,5},{8,10},{9,11},{10,... | collective-permute-start | bytes 786440 | tf_op jit(solution)/shard_map/ppermute | solution.py:36
  84.0 37.5 %copy-start.2 = (bf16[1,4096,512]{2,1,0:T(8,128)(2,1)S(1)}, bf16[1,4096,512]{2,1,0:T(8,128)(2,1)}, u32[]{:S(2)}) copy-start(bf16[1,4096,512]{2,1,0:T(8,128)(2,1)} %param.16) | copy-start | bytes 12582916
  84.0 29.8 %collective-permute-start.21 = (bf16[32,4096]{1,0:T(8,128)(2,1)S(1)}, bf16[32,4096]{1,0:T(8,128)(2,1)S(1)}, u32[]{:S(2)}, u32[]{:S(2)}) collective-permute-start(bf16[32,4096]{1,0:T(8,128)(2,1)S(1)} %fusion.24), channel_id=1, source_target_pairs={{4,0},{5,1},{6,2},{7,3},{20,16},{21,17},{22,18},{23,19}} | collective-permute-start | bytes 786440 | tf_op jit(solution)/shard_map/ppermute | solution.py:163
  87.1 29.3 %collective-permute-start.18 = (bf16[2,32,4096]{2,1,0:T(8,128)(2,1)S(1)}, bf16[2,32,4096]{2,1,0:T(8,128)(2,1)S(1)}, u32[]{:S(2)}, u32[]{:S(2)}) collective-permute-start(bf16[2,32,4096]{2,1,0:T(8,128)(2,1)S(1)} %get-tuple-element.20), channel_id=1, source_target_pairs={{0,1},{1,0},{2,3},{3,2},{4,5},{5,4},{6,7},{7,6},{8,9},{9,8},{10,11... | collective-permute-start | bytes 1572872 | tf_op jit(solution)/shard_map/ppermute | solution.py:36
  114.8 6.4 %collective-permute-start.22 = (bf16[32,4096]{1,0:T(8,128)(2,1)S(1)}, bf16[32,4096]{1,0:T(8,128)(2,1)S(1)}, u32[]{:S(2)}, u32[]{:S(2)}) collective-permute-start(bf16[32,4096]{1,0:T(8,128)(2,1)S(1)} %fusion.86), channel_id=1, source_target_pairs={{0,2},{1,3},{2,0},{3,1},{4,6},{5,7},{6,4},{7,5},{8,10},{9,11},{10,... | collective-permute-start | bytes 786440 | tf_op jit(solution)/shard_map/ppermute | solution.py:36
  121.3 2.0 %collective-permute-start.23 = (bf16[2,32,4096]{2,1,0:T(8,128)(2,1)S(1)}, bf16[2,32,4096]{2,1,0:T(8,128)(2,1)S(1)}, u32[]{:S(2)}, u32[]{:S(2)}) collective-permute-start(bf16[2,32,4096]{2,1,0:T(8,128)(2,1)S(1)} %get-tuple-element.22), channel_id=1, source_target_pairs={{0,1},{1,0},{2,3},{3,2},{4,5},{5,4},{6,7},{7,6},{8,9},{9,8},{10,11... | collective-permute-start | bytes 1572872 | tf_op jit(solution)/shard_map/ppermute | solution.py:36
  122.4 2.2 %copy-start.3 = (bf16[1,512,4096]{2,1,0:T(8,128)(2,1)S(1)}, bf16[1,512,4096]{2,1,0:T(8,128)(2,1)}, u32[]{:S(2)}) copy-start(bf16[1,512,4096]{2,1,0:T(8,128)(2,1)} %param.19) | copy-start | bytes 12582916
  126.7 3.8 %copy-start.1 = (bf16[1,4096,512]{2,1,0:T(8,128)(2,1)S(1)}, bf16[1,4096,512]{2,1,0:T(8,128)(2,1)}, u32[]{:S(2)}) copy-start(bf16[1,4096,512]{2,1,0:T(8,128)(2,1)} %param.18) | copy-start | bytes 12582916
  133.4 6.2 %collective-permute-start.24 = (bf16[4,2,4,4096]{3,2,0,1:T(4,128)(2,1)S(1)}, bf16[4,2,4,4096]{3,2,0,1:T(4,128)(2,1)S(1)}, u32[]{:S(2)}, u32[]{:S(2)}) collective-permute-start(bf16[4,2,4,4096]{3,2,0,1:T(4,128)(2,1)S(1)} %bitcast.343), channel_id=1, source_target_pairs={{0,1},{1,0},{2,3},{3,2},{4,5},{5,4},{6,7},{7,6},{8,9},{9,8},{10,11... | collective-permute-start | bytes 786440 | tf_op jit(solution)/shard_map/ppermute | solution.py:36
  137.0 4.6 %collective-permute-start.16 = (bf16[32,1024]{1,0:T(8,128)(2,1)S(1)}, bf16[32,1024]{1,0:T(8,128)(2,1)S(1)}, u32[]{:S(2)}, u32[]{:S(2)}) collective-permute-start(bf16[32,1024]{1,0:T(8,128)(2,1)S(1)} %bitcast.357), channel_id=1, source_target_pairs={{0,3},{1,2},{2,1},{3,0},{4,7},{5,6},{6,5},{7,4},{8,11},{9,10},{10,... | collective-permute-start | bytes 196616 | tf_op jit(solution)/shard_map/ppermute | solution.py:36
  138.2 4.7 %collective-permute-start.15 = (bf16[32,1024]{1,0:T(8,128)(2,1)S(1)}, bf16[32,1024]{1,0:T(8,128)(2,1)S(1)}, u32[]{:S(2)}, u32[]{:S(2)}) collective-permute-start(bf16[32,1024]{1,0:T(8,128)(2,1)S(1)} %bitcast.358), channel_id=1, source_target_pairs={{0,2},{1,3},{2,0},{3,1},{4,6},{5,7},{6,4},{7,5},{8,10},{9,11},{10,... | collective-permute-start | bytes 196616 | tf_op jit(solution)/shard_map/ppermute | solution.py:36
  138.8 4.0 %collective-permute-start.14 = (bf16[32,1024]{1,0:T(8,128)(2,1)S(1)}, bf16[32,1024]{1,0:T(8,128)(2,1)S(1)}, u32[]{:S(2)}, u32[]{:S(2)}) collective-permute-start(bf16[32,1024]{1,0:T(8,128)(2,1)S(1)} %bitcast.359), channel_id=1, source_target_pairs={{0,1},{1,0},{2,3},{3,2},{4,5},{5,4},{6,7},{7,6},{8,9},{9,8},{10,11... | collective-permute-start | bytes 196616 | tf_op jit(solution)/shard_map/ppermute | solution.py:36
  140.0 5.8 %collective-permute-start.25 = (bf16[4,4,4096]{2,1,0:T(4,128)(2,1)S(1)}, bf16[4,4,4096]{2,1,0:T(4,128)(2,1)S(1)}, u32[]{:S(2)}, u32[]{:S(2)}) collective-permute-start(bf16[4,4,4096]{2,1,0:T(4,128)(2,1)S(1)} %fusion.133), channel_id=1, source_target_pairs={{0,2},{1,3},{2,0},{3,1},{4,6},{5,7},{6,4},{7,5},{8,10},{9,11},{10,... | collective-permute-start | bytes 393224 | tf_op jit(solution)/shard_map/ppermute | solution.py:36
  145.9 5.8 %collective-permute-start.28 = (bf16[4,4096]{1,0:T(4,128)(2,1)S(1)}, bf16[4,4096]{1,0:T(4,128)(2,1)S(1)}, u32[]{:S(2)}, u32[]{:S(2)}) collective-permute-start(bf16[4,4096]{1,0:T(4,128)(2,1)S(1)} %get-tuple-element.34), channel_id=1, source_target_pairs={{0,12},{4,8},{8,4},{12,0},{1,13},{5,9},{9,5},{13,1},{2,14},{6,10},... | collective-permute-start | bytes 98312 | tf_op jit(solution)/shard_map/ppermute | solution.py:36
  146.0 5.7 %collective-permute-start.27 = (bf16[4,4096]{1,0:T(4,128)(2,1)S(1)}, bf16[4,4096]{1,0:T(4,128)(2,1)S(1)}, u32[]{:S(2)}, u32[]{:S(2)}) collective-permute-start(bf16[4,4096]{1,0:T(4,128)(2,1)S(1)} %get-tuple-element.35), channel_id=1, source_target_pairs={{0,8},{4,12},{8,0},{12,4},{1,9},{5,13},{9,1},{13,5},{2,10},{6,14},... | collective-permute-start | bytes 98312 | tf_op jit(solution)/shard_map/ppermute | solution.py:36
  147.0 5.3 %collective-permute-start.26 = (bf16[4,4096]{1,0:T(4,128)(2,1)S(1)}, bf16[4,4096]{1,0:T(4,128)(2,1)S(1)}, u32[]{:S(2)}, u32[]{:S(2)}) collective-permute-start(bf16[4,4096]{1,0:T(4,128)(2,1)S(1)} %get-tuple-element.33), channel_id=1, source_target_pairs={{0,4},{4,0},{8,12},{12,8},{1,5},{5,1},{9,13},{13,9},{2,6},{6,2},{1... | collective-permute-start | bytes 98312 | tf_op jit(solution)/shard_map/ppermute | solution.py:36

commit v2 on v1

--- a/solution.py
+++ b/solution.py
@@ -1,8 +1,11 @@
+import functools
 import math
 
 import jax
 import jax.numpy as jnp
 from jax import lax
+from jax.experimental import pallas as pl
+from jax.experimental.pallas import tpu as pltpu
 from jax.sharding import PartitionSpec as P
 
 HD = 256
@@ -48,6 +51,97 @@
     scores = jnp.where(allowed, scores, NEG_FILL)
     exp_terms = jnp.exp(scores - jnp.max(scores, axis=-1, keepdims=True))
     return exp_terms / jnp.sum(exp_terms, axis=-1, keepdims=True)
+
+TRANSPOSED = (((1,), (1,)), ((), ()))
+FIRST = (((0,), (0,)), ((), ()))
+MEBI = 1024 * 1024
+
+
+def product(left, right, dims):
+    return lax.dot_general(left, right, dims, preferred_element_type=F32)
+
+
+def scores_of(folds, tokens):
+    return jnp.concatenate([product(fold[...], tokens, TRANSPOSED) for fold in folds], axis=0)
+
+
+def spread(weights, folds):
+    size = weights.shape[0] // len(folds)
+    turned = jnp.transpose(weights)
+    total = None
+    for k, fold in enumerate(folds):
+        part = product(turned[:, k * size : (k + 1) * size].astype(BF), fold[...], PLAIN)
+        total = part if total is None else total + part
+    return total
+
+
+PLAIN = (((1,), (0,)), ((), ()))
+
+
+def probs_of(query_folds, tokens, allowed, scale, src):
+    scores = scores_of(query_folds, tokens) * scale
+    scores = jnp.where(allowed != 0, scores, NEG_FILL)
+    scores = scores.reshape(-1, src, scores.shape[1])
+    exp_terms = jnp.exp(scores - jnp.max(scores, axis=1, keepdims=True))
+    probs = exp_terms / jnp.sum(exp_terms, axis=1, keepdims=True)
+    return probs.reshape(allowed.shape)
+
+
+def d_scores_of(probs, d_probs, scale, src):
+    shape = probs.shape
+    probs = probs.reshape(-1, src, shape[1])
+    d_probs = d_probs.reshape(probs.shape)
+    inner = jnp.sum(probs * d_probs, axis=1, keepdims=True)
+    return (probs * (d_probs - inner) * scale).reshape(shape)
+
+
+def picked(take, came, held):
+    return jnp.where(take[0] != 0, came[...], held[...])
+
+
+def forward_kernel(n, scale, src, take, came, held, allowed, factor, *refs):
+    query_folds, out_folds, (current, following) = refs[:n], refs[n : 2 * n], refs[2 * n :]
+    tokens = picked(take, came, held)
+    current[...] = tokens
+    probs = probs_of(query_folds, tokens, allowed[...], scale, src)
+    summed = spread(probs, out_folds)
+    following[...] = (tokens.astype(F32) + factor[...] * summed).astype(BF)
+
+
+def backward(probs, grad, factor, query_folds, out_folds, scale, src):
+    d_out = (grad.astype(F32) * factor[...]).astype(BF)
+    d_scores = d_scores_of(probs, scores_of(out_folds, d_out), scale, src)
+    return (grad.astype(F32) + spread(d_scores, query_folds)).astype(BF)
+
+
+def turn_kernel(n, scale, src, take, came, held, allowed, factor, grad, *refs):
+    query_folds, out_folds, (current, kept, before) = refs[:n], refs[n : 2 * n], refs[2 * n :]
+    tokens = picked(take, came, held)
+    current[...] = tokens
+    probs = probs_of(query_folds, tokens, allowed[...], scale, src)
+    kept[...] = probs
+    before[...] = backward(probs, grad[...], factor, query_folds, out_folds, scale, src)
+
+
+def backward_kernel(n, scale, src, take, came, held, probs, factor, *refs):
+    query_folds, out_folds, (current, before) = refs[:n], refs[n : 2 * n], refs[2 * n :]
+    grad = picked(take, came, held)
+    current[...] = grad
+    before[...] = backward(probs[...], grad, factor, query_folds, out_folds, scale, src)
+
+
+def on_chip(body, outs, first, *args):
+    vmem = pl.BlockSpec(memory_space=pltpu.VMEM)
+    size = sum(math.prod(a.shape) * a.dtype.itemsize for a in args)
+    flops = 8 * args[0].shape[0] * sum(math.prod(a.shape) for a in args[-8:])
+    return pl.pallas_call(
+        body,
+        out_shape=[jax.ShapeDtypeStruct(*out) for out in outs],
+        in_specs=[pl.BlockSpec(memory_space=pltpu.SMEM)] + [vmem] * len(args),
+        out_specs=[vmem] * len(outs),
+        compiler_params=pltpu.CompilerParams(vmem_limit_bytes=2 * size + 4 * MEBI),
+        cost_estimate=pl.CostEstimate(flops=flops, bytes_accessed=size, transcendentals=0),
+    )(first, *args)
 
 
 def per_device(
@@ -116,13 +210,14 @@
     )
 
     def to_owners(fold):
-        blocks = [fold[j] if j == 0 else swap(fold[j], "mp", j) for j in range(n_mp)]
-        return jnp.stack(blocks).reshape(n_mp * heads * src, dim)
-
-    out_fold = to_owners(out_fold)
-    query_fold = to_owners(query_fold)
-    allowed = jnp.stack([allowed_of(me, me ^ k) for k in range(n_mp)], axis=1)
-    allowed = jnp.broadcast_to(allowed[:, :, None, :], (rows, n_mp, heads, src))
+        fold = fold.reshape(n_mp, heads * src, dim)
+        return [fold[j] if j == 0 else swap(fold[j], "mp", j) for j in range(n_mp)]
+
+    out_folds = to_owners(out_fold)
+    query_folds = to_owners(query_fold)
+    allowed = jnp.stack([allowed_of(me, me ^ k).T for k in range(n_mp)])[:, None]
+    allowed = jnp.broadcast_to(allowed, (n_mp, heads, src, rows)).astype(jnp.int32)
+    allowed = allowed.reshape(n_mp * heads * src, rows)
 
     my_micro = me // share
     my_first = (me % share) * rows
@@ -132,76 +227,35 @@
         return lax.dynamic_slice_in_dim(part, my_first, rows, 0)
 
     factor = keep_factor(seeds[my_micro, 0], my_first, rows, dim)
-
-    def probs(current):
-        scores = dot_f32("td,kd->tk", current, query_fold) * scale
-        return softmax_rows(scores.reshape(rows, n_mp, heads, src), allowed)
-
-    def layer(current):
-        weights = probs(current).astype(BF).reshape(rows, n_mp * heads * src)
-        summed = dot_f32("tk,kd->td", weights, out_fold)
-        return (current.astype(F32) + factor * summed).astype(BF)
-
-    current = mine(decoder_in)
+    folds = (*query_folds, *out_folds)
+    wide = ((rows, dim), BF)
+
+    def at(step):
+        return (section == step).astype(jnp.int32)[None]
+
+    held = mine(decoder_in)
+    factor, held, allowed = lax.optimization_barrier((factor, held, allowed))
+    came = held
     for step in range(sections - 1):
-        came = lax.ppermute(layer(current), "section", [(step, step + 1)])
-        current = jnp.where(section == step + 1, came, current)
-    following = layer(current)
-    prob_rows = probs(current)
-
+        body = functools.partial(forward_kernel, n_mp, scale, src)
+        held, following = on_chip(
+            body, [wide, wide], at(step), came, held, allowed, factor, *folds
+        )
+        came = lax.ppermute(following, "section", [(step, step + 1)])
+    step = sections - 1
+    body = functools.partial(turn_kernel, n_mp, scale, src)
     grad = mine(cotangent)
-
-    def dropped(grad):
-        return (grad.astype(F32) * factor).astype(BF)
-
-    for step in range(sections - 1, 0, -1):
-        d_probs = dot_f32("td,kd->tk", dropped(grad), out_fold).reshape(prob_rows.shape)
-        inner = jnp.sum(prob_rows * d_probs, axis=-1, keepdims=True)
-        d_scores = (prob_rows * (d_probs - inner) * scale).astype(BF)
-        back = dot_f32("tk,kd->td", d_scores.reshape(rows, -1), query_fold)
-        before = (grad.astype(F32) + back).astype(BF)
-        came = lax.ppermute(before, "section", [(step, step - 1)])
-        grad = jnp.where(section == step - 1, came, grad)
+    current, probs, before = on_chip(
+        body, [wide, (allowed.shape, F32), wide], at(step), came, held, allowed, factor, grad, *folds
+    )
+    body = functools.partial(forward_kernel, n_mp, scale, src)
+    _, following = on_chip(
+        body, [wide, wide], at(step), current, current, allowed, factor, *folds
+    )
 
     def all_tokens(array):
         over_x = jnp.stack(gather_swaps(array, "mp", range(0, n_mp, 2)))
         return jnp.stack(gather_swaps(over_x, "mp", range(2)), axis=1).reshape(n_mp * rows, dim)
-
-    every_x = all_tokens(current)
-    every_d_out = all_tokens(dropped(grad))
-    query = jnp.dot(every_x, wq, preferred_element_type=F32).astype(BF)
-    query = query.reshape(n_mp, rows, heads, HD)
-    d_att = dot_f32("td,kd->tk", every_d_out, wo).astype(BF).reshape(n_mp, rows, heads, HD)
-    own_allowed = jnp.stack([allowed_of(me ^ j, me) for j in range(n_mp)])[:, None]
-    own_probs = softmax_rows(dot_f32("jthk,jshk->jhts", query, keys) * scale, own_allowed)
-    d_probs = dot_f32("jthk,jshk->jhts", d_att, values)
-    inner = jnp.sum(own_probs * d_probs, axis=-1, keepdims=True)
-    d_scores = (own_probs * (d_probs - inner) * scale).astype(BF)
-    d_keys = dot_f32("jhts,jthk->jshk", d_scores, query).reshape(n_mp, src, local_cols)
-    d_values = dot_f32("jhts,jthk->jshk", own_probs.astype(BF), d_att)
-    d_values = d_values.reshape(n_mp, src, local_cols)
-
-    def by_micro(array):
-        parts = []
-        for micro in range(micro_count):
-            total = 0.0
-            for q in range(share):
-                owner = me ^ (micro * share + q)
-                total = total + lax.dynamic_index_in_dim(array, owner, 0, keepdims=False)
-            parts.append(total.astype(BF))
-        return jnp.stack(parts, axis=1)
-
-    terms = dot_f32("rbk,dk->rbd", by_micro(d_keys), wk) + dot_f32(
-        "rbk,dk->rbd", by_micro(d_values), wv
-    )
-    terms = terms.reshape(sections, n_mp // 2, 2, micro_count, dim)
-    half = terms[:, :, 0] + swap(terms[:, :, 1].astype(BF), "mp", 1).astype(F32)
-    total = half[:, 0]
-    for j in range(1, n_mp // 2):
-        total = total + swap(half[:, j].astype(BF), "mp", 2 * j).astype(F32)
-    mem_grad = total[0]
-    for a in range(1, sections):
-        mem_grad = mem_grad + swap(total[a].astype(BF), "section", a).astype(F32)
 
     out_cols = dim // n_mp
     following = following.reshape(rows, n_mp, out_cols)
@@ -214,6 +268,59 @@
         lax.dynamic_index_in_dim(stacked, me ^ owner, 0, keepdims=False) for owner in range(n_mp)
     ]
     section_out = jnp.stack(ordered).reshape(1, micro_count, tgt_rows, out_cols)
+
+    every_x = all_tokens(current)
+    query = jnp.dot(every_x, wq, preferred_element_type=F32).astype(BF)
+    query = query.reshape(n_mp, rows, heads, HD)
+    own_allowed = jnp.stack([allowed_of(me ^ j, me) for j in range(n_mp)])[:, None]
+    own_probs = softmax_rows(dot_f32("jthk,jshk->jhts", query, keys) * scale, own_allowed)
+
+    for step in range(sections - 1, 0, -1):
+        came = lax.ppermute(before, "section", [(step, step - 1)])
+        if step == 1:
+            break
+        if step == 2:
+            came, section_out, query, own_probs = lax.optimization_barrier(
+                (came, section_out, query, own_probs)
+            )
+        body = functools.partial(backward_kernel, n_mp, scale, src)
+        grad, before = on_chip(
+            body, [wide, wide], at(step - 1), came, grad, probs, factor, *folds
+        )
+    grad = jnp.where(section == 0, came, grad)
+    d_out = (grad.astype(F32) * factor).astype(BF)
+
+    every_d_out = all_tokens(d_out)
+    d_att = dot_f32("td,kd->tk", every_d_out, wo).astype(BF).reshape(n_mp, rows, heads, HD)
+    d_probs = dot_f32("jthk,jshk->jhts", d_att, values)
+    inner = jnp.sum(own_probs * d_probs, axis=-1, keepdims=True)
+    d_scores = (own_probs * (d_probs - inner) * scale).astype(BF)
+    d_keys = dot_f32("jhts,jthk->jshk", d_scores, query).reshape(n_mp, src, local_cols)
+    d_values = dot_f32("jhts,jthk->jshk", own_probs.astype(BF), d_att)
+    d_values = d_values.reshape(n_mp, src, local_cols)
+
+    def by_micro(array):
+        parts = []
+        for micro in range(micro_count):
+            total = 0.0
+            for q in range(share):
+                owner = me ^ (micro * share + q)
+                total = total + lax.dynamic_index_in_dim(array, owner, 0, keepdims=False)
+            parts.append(total.astype(BF))
+        return jnp.stack(parts, axis=1)
+
+    terms = dot_f32("rbk,dk->rbd", by_micro(d_keys), wk) + dot_f32(
+        "rbk,dk->rbd", by_micro(d_values), wv
+    )
+    terms = terms.reshape(sections, n_mp // 2, 2, micro_count, dim)
+    half = terms[:, :, 0] + swap(terms[:, :, 1].astype(BF), "mp", 1).astype(F32)
+    total = half[:, 0]
+    for j in range(1, n_mp // 2):
+        total = total + swap(half[:, j].astype(BF), "mp", 2 * j).astype(F32)
+    mem_grad = total[0]
+    for a in range(1, sections):
+        mem_grad = mem_grad + swap(total[a].astype(BF), "section", a).astype(F32)
+
     return (section_out, mem_grad[None])
 
 

time: 154 us -> 186 us (1.21)
  local copies, waits for them, and re-layouts: 7.75 us -> 30.2 us
  matrix products: 40 us -> 23 us
  Pallas kernels: 0 us -> 13.8 us
  waiting for transfers between devices: 64.5 us -> 74.3 us
  other arithmetic: 10.2 us -> 12.5 us
    dot_general x26 -> x12, matrix products: 39.1 us -> 19.9 us  [dot_f32(): return jnp.einsum(spec, left, right, preferred_element_type=F32)]
    pallas_call x0 -> x7, Pallas kernels: none -> 13.8 us  [on_chip(): pl.pallas_call(body, out_shape=[jax.ShapeDtypeStruct(*out) for out in out...]
    unnamed x20 -> x68, local copies, waits for them, and re-layouts: 2.44 us -> 14.4 us
    ppermute x23, waiting for transfers between devices: 32.3 us -> 37.9 us  [swap(): return lax.ppermute(array, axis, [(i, i ^ k) for i in range(size)])]
    ppermute x3, waiting for transfers between devices: 26.6 us -> 30.2 us  [per_device(): came = lax.ppermute(before, 'section', [(step, step - 1)])]
    slice x2, local copies, waits for them, and re-layouts: 0.94 us -> 3.39 us  [per_device(): half = terms[:, :, 0] + swap(terms[:, :, 1].astype(BF), 'mp', 1).astype(F32)]
    eq x5, other arithmetic: 0.38 us -> 2.81 us  [allowed_of(): return segments[:, None] == docs[None, :]]
    squeeze x0 -> x2, local copies, waits for them, and re-layouts: none -> 2.39 us  [mine(): part = lax.dynamic_index_in_dim(array, my_micro, 0, keepdims=False)]
  transfers between devices with their start and end apart: 29 -> 29, of which waited for: 16 -> 15; matrix products, arithmetic and copies ran while one was open for 16% -> 16% of each run, Pallas kernels for 0% -> 2%
where the time goes in v2:
time: 186 us; the launch traced here: 184 us
  waiting for transfers between devices  74.3 us (40%)
  local copies, waits for them, and re-layouts  30.2 us (16%)
  starting transfers between devices  29.2 us (16%)
  matrix products  23 us (12%)
  Pallas kernels  13.8 us (7%)
  other arithmetic  12.5 us (7%)
    ppermute x23, waiting for transfers between devices, swap(): return lax.ppermute(array, axis, [(i, i ^ k) for i in range(size)])  37.9 us
    ppermute x3, waiting for transfers between devices, per_device(): came = lax.ppermute(before, 'section', [(step, step - 1)])  30.2 us
    ppermute x23, starting transfers between devices, swap(): return lax.ppermute(array, axis, [(i, i ^ k) for i in range(size)])  21.5 us
    dot_general x12, matrix products, dot_f32(): return jnp.einsum(spec, left, right, preferred_element_type=F32)  19.9 us
    unnamed x68, local copies, waits for them, and re-layouts  14.4 us
    pallas_call x7, Pallas kernels, on_chip(): pl.pallas_call(body, out_shape=[jax.ShapeDtypeStruct(*out) for out in out...  13.8 us
    ppermute x3, waiting for transfers between devices, per_device(): came = lax.ppermute(following, 'section', [(step, step + 1)])  6.23 us
    ppermute x3, starting transfers between devices, per_device(): came = lax.ppermute(following, 'section', [(step, step + 1)])  4.17 us
  transfers between devices with their start and end apart: 29, of which 15 were waited for; matrix products, arithmetic and copies ran while one was open for 16% of the time, Pallas kernels for 2%

profile of v2, /device:TPU:0, one launch (start us, length us, event | category | flops | bytes accessed | tf_op | source)
XLA Modules:
  0.0 184.4 jit_solution(3890117337351246086)
XLA Ops:
  0.6 3.1 %collective-permute-start = (bf16[1,4,4096]{2,1,0:T(4,128)(2,1)}, bf16[1,4,4096]{2,1,0:T(4,128)(2,1)S(1)}, u32[]{:S(2)}, u32[]{:S(2)}) collective-permute-start(bf16[1,4,4096]{2,1,0:T(4,128)(2,1)} %param.10), channel_id=1, source_target_pairs={{0,4},{4,0},{8,12},{12,8},{1,5},{5,1},{9,13},{13,9},{2,6},{6,2},{1... | collective-permute-start | bytes 98312 | tf_op jit(solution)/shard_map/ppermute | solution.py:39
  3.7 2.6 %collective-permute-start.1 = (bf16[1,4,4096]{2,1,0:T(4,128)(2,1)}, bf16[1,4,4096]{2,1,0:T(4,128)(2,1)S(1)}, u32[]{:S(2)}, u32[]{:S(2)}) collective-permute-start(bf16[1,4,4096]{2,1,0:T(4,128)(2,1)} %param.10), channel_id=1, source_target_pairs={{0,8},{4,12},{8,0},{12,4},{1,9},{5,13},{9,1},{13,5},{2,10},{6,14},... | collective-permute-start | bytes 98312 | tf_op jit(solution)/shard_map/ppermute | solution.py:39
  7.2 1.2 fusion.113
  9.2 1.0 fusion.43.factor
  10.2 2.0 %collective-permute-done.2 = bf16[1,4,4096]{2,1,0:T(4,128)(2,1)S(1)} collective-permute-done((bf16[1,4,4096]{2,1,0:T(4,128)(2,1)}, bf16[1,4,4096]{2,1,0:T(4,128)(2,1)S(1)}, u32[]{:S(2)}, u32[]{:S(2)}) %collective-permute-start.2) | collective-permute-done | bytes 32800 | tf_op jit(solution)/shard_map/ppermute | solution.py:39
  12.3 1.6 collective-permute-start.3
  13.9 3.4 %collective-permute-done.3 = bf16[4,4,4096]{2,1,0:T(4,128)(2,1)S(1)} collective-permute-done((bf16[4,4,4096]{2,1,0:T(4,128)(2,1)S(1)}, bf16[4,4,4096]{2,1,0:T(4,128)(2,1)S(1)}, u32[]{:S(2)}, u32[]{:S(2)}) %collective-permute-start.3) | collective-permute-done | bytes 131104 | tf_op jit(solution)/shard_map/ppermute | solution.py:39
  17.6 1.4 fusion.94
  22.0 3.0 %fusion.23 = bf16[16,4,512]{2,0,1:T(8,128)(2,1)S(1)} fusion(bf16[16,4,4096]{2,0,1:T(8,128)(2,1)S(1)} %reshape.643, bf16[1,4096,512]{2,1,0:T(8,128)(2,1)} %param.17), kind=kOutput, calls=%fused_computation.43 | convolution fusion | flops 268468224 | bytes 4784128 | tf_op jit(solution)/shard_map/rbd,dk->brk/dot_general | solution.py:47
  25.2 2.5 %fusion.4 = bf16[4,1,16,4096]{3,2,0,1:T(8,128)(2,1)S(1)} fusion(bf16[4096,512]{1,0:T(8,128)(2,1)} %bitcast.237, bf16[4,16,1,256]{3,2,1,0:T(2,128)(2,1)S(1)} %get-tuple-element.92), kind=kOutput, calls=%fused_computation.9 | convolution fusion | flops 134479872 | bytes 2654208 | tf_op jit(solution)/shard_map/jsk,dk->jsd/dot_general | solution.py:47
  27.7 2.3 %fusion.3 = bf16[4,1,16,4096]{3,2,0,1:T(8,128)(2,1)S(1)} fusion(bf16[4096,512]{1,0:T(8,128)(2,1)} %bitcast.238, bf16[4,16,1,256]{3,2,1,0:T(2,128)(2,1)S(1)} %get-tuple-element.93), kind=kOutput, calls=%fused_computation.8 | convolution fusion | flops 134479872 | bytes 2654208 | tf_op jit(solution)/shard_map/jsk,dk->jsd/dot_general | solution.py:47
  31.5 1.5 collective-permute-start.6
  34.0 2.1 %fusion.6 = bf16[4,1,16,4096]{3,2,0,1:T(8,128)(2,1)S(1)} fusion(bf16[1,512,4096]{2,1,0:T(8,128)(2,1)} %param.19, bf16[4,16,1,256]{3,2,1,0:T(2,128)(2,1)S(1)} %get-tuple-element.86), kind=kOutput, calls=%fused_computation.11 | convolution fusion | flops 134479872 | bytes 2654208 | tf_op jit(solution)/shard_map/jsk,kd->jsd/dot_general | solution.py:47
  36.1 2.1 %fusion.5 = bf16[4,1,16,4096]{3,2,0,1:T(8,128)(2,1)S(1)} fusion(bf16[1,512,4096]{2,1,0:T(8,128)(2,1)} %param.19, bf16[4,16,1,256]{3,2,1,0:T(2,128)(2,1)S(1)} %get-tuple-element.87), kind=kOutput, calls=%fused_computation.10 | convolution fusion | flops 134479872 | bytes 2654208 | tf_op jit(solution)/shard_map/jsk,kd->jsd/dot_general | solution.py:47
  39.0 1.5 collective-permute-start.9
  40.9 4.7 %collective-permute-done.7.refs_3_ = bf16[32,4096]{1,0:T(8,128)(2,1)S(1)} collective-permute-done((bf16[32,4096]{1,0:T(8,128)(2,1)}, bf16[32,4096]{1,0:T(8,128)(2,1)S(1)}, u32[]{:S(2)}, u32[]{:S(2)}) %collective-permute-start.7) | collective-permute-done | bytes 262176 | tf_op jit(solution)/shard_map/ppermute | solution.py:39
  45.6 6.5 %collective-permute-done.9.refs_6_ = bf16[32,4096]{1,0:T(8,128)(2,1)S(1)} collective-permute-done((bf16[32,4096]{1,0:T(8,128)(2,1)S(1)}, bf16[32,4096]{1,0:T(8,128)(2,1)S(1)}, u32[]{:S(2)}, u32[]{:S(2)}) %collective-permute-start.9) | collective-permute-done | bytes 262176 | tf_op jit(solution)/shard_map/ppermute | solution.py:39
  52.1 3.7 %collective-permute-done.10.refs_7_ = bf16[32,4096]{1,0:T(8,128)(2,1)S(1)} collective-permute-done((bf16[32,4096]{1,0:T(8,128)(2,1)S(1)}, bf16[32,4096]{1,0:T(8,128)(2,1)S(1)}, u32[]{:S(2)}, u32[]{:S(2)}) %collective-permute-start.10) | collective-permute-done | bytes 262176 | tf_op jit(solution)/shard_map/ppermute | solution.py:39
  55.9 0.9 copy-done.10
  56.8 1.7 shard_map.113
  60.0 2.1 %collective-permute-start.11 = (bf16[32,4096]{1,0:T(8,128)(2,1)}, bf16[32,4096]{1,0:T(8,128)(2,1)}, u32[]{:S(2)}, u32[]{:S(2)}) collective-permute-start(bf16[32,4096]{1,0:T(8,128)(2,1)} %get-tuple-element.26), channel_id=1, source_target_pairs={{0,4},{1,5},{2,6},{3,7},{16,20},{17,21},{18,22},{19,23}} | collective-permute-start | bytes 786440 | tf_op jit(solution)/shard_map/ppermute | solution.py:244
  62.1 6.2 %collective-permute-done.11.came = bf16[32,4096]{1,0:T(8,128)(2,1)} collective-permute-done((bf16[32,4096]{1,0:T(8,128)(2,1)}, bf16[32,4096]{1,0:T(8,128)(2,1)}, u32[]{:S(2)}, u32[]{:S(2)}) %collective-permute-start.11) | collective-permute-done | bytes 262176 | tf_op jit(solution)/shard_map/ppermute | solution.py:244
  68.3 0.9 copy-done.2
  69.2 0.9 copy-done.17
  70.2 1.9 %shard_map.114 = (bf16[32,4096]{1,0:T(8,128)(2,1)S(1)}, bf16[32,4096]{1,0:T(8,128)(2,1)S(1)}) custom-call(s32[1]{0:T(128)} %bitcast.2.take, bf16[32,4096]{1,0:T(8,128)(2,1)} %collective-permute-done.11.came, bf16[32,4096]{1,0:T(8,128)(2,1)S(1)} %copy-done.17, s32[128,32]{1,0:T(8,128)S(1)} %bitcast.233, f32[32,4096]{1,0:T(8,128)S(1)} %fusion.43.factor, ...), custom_call_target="tpu_custom_call" | custom-call | flops 268435456 | bytes 3162112 | tf_op jit(solution)/shard_map/pallas_call | solution.py:137
  72.8 1.7 dynamic-slice_bitcast_fusion.grad.held
  74.5 0.9 copy-done.3
  75.5 1.7 shard_map.115
  77.9 1.4 collective-permute-start.13
  80.3 0.9 copy-done.8
  81.3 0.9 copy-done.12
  82.2 2.8 %shard_map.116 = (bf16[32,4096]{1,0:T(8,128)(2,1)}, f32[128,32]{1,0:T(8,128)S(1)}, bf16[32,4096]{1,0:T(8,128)(2,1)S(1)}) custom-call(s32[1]{0:T(128)} %bitcast.1.take, bf16[32,4096]{1,0:T(8,128)(2,1)} %collective-permute-done.13.came, bf16[32,4096]{1,0:T(8,128)(2,1)S(1)} %copy-done.12, s32[128,32]{1,0:T(8,128)S(1)} %bitcast.235, ...), custom_call_target="tpu_custom_call" | custom-call | flops 268435456 | bytes 3424256 | tf_op jit(solution)/shard_map/pallas_call | solution.py:137
  85.0 1.5 collective-permute-start.19
  86.5 1.3 broadcast_compare_fusion.1
  87.8 1.2 broadcast_compare_fusion.2
  89.1 0.9 copy-done.5
  90.0 2.1 %shard_map.118 = (bf16[32,4096]{1,0:T(8,128)(2,1)}, bf16[32,4096]{1,0:T(8,128)(2,1)S(1)}) custom-call(s32[1]{0:T(128)} %bitcast.1.take, bf16[32,4096]{1,0:T(8,128)(2,1)} %get-tuple-element.35.came.held, bf16[32,4096]{1,0:T(8,128)(2,1)} %get-tuple-element.35.came.held, s32[128,32]{1,0:T(8,128)S(1)} %bitcast.236, f32[32,4096]{1,0:T(8,128)S(1)} %fusion.43.factor, ...), custom_call_target="tpu_custom_call" | custom-call | flops 268435456 | bytes 3162112 | tf_op jit(solution)/shard_map/pallas_call | solution.py:137
  92.8 1.8 reshape.646
  94.7 1.2 fusion.108
  95.9 1.9 %constant_dynamic-slice_fusion.13 = (bf16[32,1,1024]{2,1,0:T(2,128)(2,1)S(1)}, bf16[32,1,1024]{2,1,0:T(2,128)(2,1)S(1)}, bf16[32,1,1024]{2,1,0:T(2,128)(2,1)S(1)}, bf16[32,1,1024]{2,1,0:T(2,128)(2,1)S(1)}) fusion(bf16[32,4,1024]{2,1,0:T(4,128)(2,1)} %reshape.646, s32[]{:T(128)S(6)} %select_n.123, s32[]{:T(128)S(6)} %select_n.126, s32[]{:T(128)S(6)} %select_n.125, ...), kind=kLoop, calls=%fused_computation.178 | loop fusion | bytes 524304 | tf_op jit(solution)/shard_map/jit(dynamic_index_in_dim)/dynamic_slice | solution.py:264
  98.6 1.5 collective-permute-start.17
  101.7 2.0 %collective-permute-done.17 = bf16[32,1024]{1,0:T(8,128)(2,1)S(1)} collective-permute-done((bf16[32,1024]{1,0:T(8,128)(2,1)S(1)}, bf16[32,1024]{1,0:T(8,128)(2,1)S(1)}, u32[]{:S(2)}, u32[]{:S(2)}) %collective-permute-start.17) | collective-permute-done | bytes 65568 | tf_op jit(solution)/shard_map/ppermute | solution.py:39
  104.5 1.7 shard_map.117
  106.9 1.4 collective-permute-start.15
  108.5 1.4 convolution_convert_fusion.4
  109.9 1.6 reshape.649
  111.5 1.7 fusion.30
  113.2 0.9 copy-done.7
  114.2 0.9 copy-done.15
  115.1 1.9 %shard_map.119 = (bf16[32,4096]{1,0:T(8,128)(2,1)S(1)}, bf16[32,4096]{1,0:T(8,128)(2,1)S(1)}) custom-call(s32[1]{0:T(128)} %bitcast.2.take, bf16[32,4096]{1,0:T(8,128)(2,1)} %collective-permute-done.15.came, bf16[32,4096]{1,0:T(8,128)(2,1)S(1)} %copy-done.15, f32[128,32]{1,0:T(8,128)S(1)} %get-tuple-element.33.probs, f32[32,4096]{1,0:T(8,128)S(1)} %fusion.43.factor, ...), custom_call_target="tpu_custom_call" | custom-call | flops 268435456 | bytes 3162112 | tf_op jit(solution)/shard_map/pallas_call | solution.py:137
  117.1 1.6 collective-permute-start.21
  118.6 30.2 %collective-permute-done.21 = bf16[32,4096]{1,0:T(8,128)(2,1)S(1)} collective-permute-done((bf16[32,4096]{1,0:T(8,128)(2,1)S(1)}, bf16[32,4096]{1,0:T(8,128)(2,1)S(1)}, u32[]{:S(2)}, u32[]{:S(2)}) %collective-permute-start.21) | collective-permute-done | bytes 262176 | tf_op jit(solution)/shard_map/ppermute | solution.py:279
  149.6 6.2 %collective-permute-done.22 = bf16[32,4096]{1,0:T(8,128)(2,1)S(1)} collective-permute-done((bf16[32,4096]{1,0:T(8,128)(2,1)S(1)}, bf16[32,4096]{1,0:T(8,128)(2,1)S(1)}, u32[]{:S(2)}, u32[]{:S(2)}) %collective-permute-start.22) | collective-permute-done | bytes 262176 | tf_op jit(solution)/shard_map/ppermute | solution.py:39
  156.0 1.9 %collective-permute-done.23 = bf16[2,32,4096]{2,1,0:T(8,128)(2,1)S(1)} collective-permute-done((bf16[2,32,4096]{2,1,0:T(8,128)(2,1)S(1)}, bf16[2,32,4096]{2,1,0:T(8,128)(2,1)S(1)}, u32[]{:S(2)}, u32[]{:S(2)}) %collective-permute-start.23) | collective-permute-done | bytes 524320 | tf_op jit(solution)/shard_map/ppermute | solution.py:39
  158.1 1.5 fusion.20
  160.2 3.7 %fusion.12 = f32[16,4,4096]{2,0,1:T(8,128)S(1)} fusion(bf16[1,4096,512]{2,1,0:T(8,128)(2,1)} %param.17, bf16[16,1,512]{2,0,1:T(8,128)(2,1)S(1)} %get-tuple-element.83, bf16[16,1,512]{2,0,1:T(8,128)(2,1)S(1)} %get-tuple-element.84, bf16[16,1,512]{2,0,1:T(8,128)(2,1)S(1)} %get-tuple-element.85, bf16[16,1,512]{2,0,1:T(8,128)(2,1)S(1)} %get-tuple-element.82), kind=kOutput, calls=%fused_computation.17 | convolution fusion | flops 268533760 | bytes 5308416 | tf_op jit(solution)/shard_map/rbk,dk->rbd/dot_general | solution.py:47
  164.0 1.4 convolution_add_fusion
  165.3 1.6 reshape.654
  167.0 1.8 slice.136
  169.3 1.6 slice.135
  172.1 5.1 %collective-permute-done.25 = bf16[4,4,4096]{2,1,0:T(4,128)(2,1)S(1)} collective-permute-done((bf16[4,4,4096]{2,1,0:T(4,128)(2,1)S(1)}, bf16[4,4,4096]{2,1,0:T(4,128)(2,1)S(1)}, u32[]{:S(2)}, u32[]{:S(2)}) %collective-permute-start.25) | collective-permute-done | bytes 131104 | tf_op jit(solution)/shard_map/ppermute | solution.py:39
  177.5 1.0 collective-permute-start.27
  178.5 3.4 %collective-permute-start.26 = (bf16[4,4096]{1,0:T(4,128)(2,1)S(1)}, bf16[4,4096]{1,0:T(4,128)(2,1)S(1)}, u32[]{:S(2)}, u32[]{:S(2)}) collective-permute-start(bf16[4,4096]{1,0:T(4,128)(2,1)S(1)} %get-tuple-element.75), channel_id=1, source_target_pairs={{0,4},{4,0},{8,12},{12,8},{1,5},{5,1},{9,13},{13,9},{2,6},{6,2},{1... | collective-permute-start | bytes 98312 | tf_op jit(solution)/shard_map/ppermute | solution.py:39
  181.9 1.3 collective-permute-done.28
  (150 shorter events, 22.3 us)
Async XLA Ops:
  0.6 7.8 %copy-start = (bf16[4,32,4096]{2,1,0:T(8,128)(2,1)S(1)}, bf16[4,32,4096]{2,1,0:T(8,128)(2,1)}, u32[]{:S(2)}) copy-start(bf16[4,32,4096]{2,1,0:T(8,128)(2,1)} %param.11) | copy-start | bytes 3145732
  0.6 9.5 %collective-permute-start = (bf16[1,4,4096]{2,1,0:T(4,128)(2,1)}, bf16[1,4,4096]{2,1,0:T(4,128)(2,1)S(1)}, u32[]{:S(2)}, u32[]{:S(2)}) collective-permute-start(bf16[1,4,4096]{2,1,0:T(4,128)(2,1)} %param.10), channel_id=1, source_target_pairs={{0,4},{4,0},{8,12},{12,8},{1,5},{5,1},{9,13},{13,9},{2,6},{6,2},{1... | collective-permute-start | bytes 98312 | tf_op jit(solution)/shard_map/ppermute | solution.py:39
  3.7 6.5 %collective-permute-start.1 = (bf16[1,4,4096]{2,1,0:T(4,128)(2,1)}, bf16[1,4,4096]{2,1,0:T(4,128)(2,1)S(1)}, u32[]{:S(2)}, u32[]{:S(2)}) collective-permute-start(bf16[1,4,4096]{2,1,0:T(4,128)(2,1)} %param.10), channel_id=1, source_target_pairs={{0,8},{4,12},{8,0},{12,4},{1,9},{5,13},{9,1},{13,5},{2,10},{6,14},... | collective-permute-start | bytes 98312 | tf_op jit(solution)/shard_map/ppermute | solution.py:39
  6.3 5.9 %collective-permute-start.2 = (bf16[1,4,4096]{2,1,0:T(4,128)(2,1)}, bf16[1,4,4096]{2,1,0:T(4,128)(2,1)S(1)}, u32[]{:S(2)}, u32[]{:S(2)}) collective-permute-start(bf16[1,4,4096]{2,1,0:T(4,128)(2,1)} %param.10), channel_id=1, source_target_pairs={{0,12},{4,8},{8,4},{12,0},{1,13},{5,9},{9,5},{13,1},{2,14},{6,10},... | collective-permute-start | bytes 98312 | tf_op jit(solution)/shard_map/ppermute | solution.py:39
  12.3 5.0 %collective-permute-start.3 = (bf16[4,4,4096]{2,1,0:T(4,128)(2,1)S(1)}, bf16[4,4,4096]{2,1,0:T(4,128)(2,1)S(1)}, u32[]{:S(2)}, u32[]{:S(2)}) collective-permute-start(bf16[4,4,4096]{2,1,0:T(4,128)(2,1)S(1)} %constant_dynamic-update-slice_fusion), channel_id=1, source_target_pairs={{0,2},{1,3},{2,0},{3,1},{4,6},{5,7},{6,4},{7,5},{8,10},{9,11},{10,... | collective-permute-start | bytes 393224 | tf_op jit(solution)/shard_map/ppermute | solution.py:39
  17.5 3.4 %collective-permute-start.4 = (bf16[4,2,4,4096]{3,2,0,1:T(4,128)(2,1)S(1)}, bf16[4,2,4,4096]{3,2,0,1:T(4,128)(2,1)S(1)}, u32[]{:S(2)}, u32[]{:S(2)}) collective-permute-start(bf16[4,2,4,4096]{3,2,0,1:T(4,128)(2,1)S(1)} %get-tuple-element.74), channel_id=1, source_target_pairs={{0,1},{1,0},{2,3},{3,2},{4,5},{5,4},{6,7},{7,6},{8,9},{9,8},{10,11... | collective-permute-start | bytes 786440 | tf_op jit(solution)/shard_map/ppermute | solution.py:39
  25.1 2.6 %copy-start.26 = (bf16[4,16,512]{2,1,0:T(8,128)(2,1)}, bf16[4,16,512]{2,1,0:T(8,128)(2,1)S(1)}, u32[]{:S(2)}) copy-start(bf16[4,16,512]{2,1,0:T(8,128)(2,1)S(1)} %pad_maximum_fusion.9) | copy-start | bytes 196612
  25.1 7.9 %copy-start.19 = (bf16[1,4096,512]{2,1,0:T(8,128)(2,1)S(1)}, bf16[1,4096,512]{2,1,0:T(8,128)(2,1)}, u32[]{:S(2)}) copy-start(bf16[1,4096,512]{2,1,0:T(8,128)(2,1)} %param.18) | copy-start | bytes 12582916
  31.0 9.5 %collective-permute-start.5 = (bf16[32,4096]{1,0:T(8,128)(2,1)}, bf16[32,4096]{1,0:T(8,128)(2,1)S(1)}, u32[]{:S(2)}, u32[]{:S(2)}) collective-permute-start(bf16[32,4096]{1,0:T(8,128)(2,1)} %bitcast.27), channel_id=1, source_target_pairs={{0,1},{1,0},{2,3},{3,2},{4,5},{5,4},{6,7},{7,6},{8,9},{9,8},{10,11... | collective-permute-start | bytes 786440 | tf_op jit(solution)/shard_map/ppermute | solution.py:39
  31.5 9.4 %collective-permute-start.6 = (bf16[32,4096]{1,0:T(8,128)(2,1)}, bf16[32,4096]{1,0:T(8,128)(2,1)S(1)}, u32[]{:S(2)}, u32[]{:S(2)}) collective-permute-start(bf16[32,4096]{1,0:T(8,128)(2,1)} %bitcast.28), channel_id=1, source_target_pairs={{0,2},{1,3},{2,0},{3,1},{4,6},{5,7},{6,4},{7,5},{8,10},{9,11},{10,... | collective-permute-start | bytes 786440 | tf_op jit(solution)/shard_map/ppermute | solution.py:39
  33.0 12.6 %collective-permute-start.7 = (bf16[32,4096]{1,0:T(8,128)(2,1)}, bf16[32,4096]{1,0:T(8,128)(2,1)S(1)}, u32[]{:S(2)}, u32[]{:S(2)}) collective-permute-start(bf16[32,4096]{1,0:T(8,128)(2,1)} %bitcast.29), channel_id=1, source_target_pairs={{0,3},{1,2},{2,1},{3,0},{4,7},{5,6},{6,5},{7,4},{8,11},{9,10},{10,... | collective-permute-start | bytes 786440 | tf_op jit(solution)/shard_map/ppermute | solution.py:39
  33.9 2.2 %copy-start.24 = (bf16[4,16,512]{2,1,0:T(8,128)(2,1)}, bf16[4,16,512]{2,1,0:T(8,128)(2,1)S(1)}, u32[]{:S(2)}) copy-start(bf16[4,16,512]{2,1,0:T(8,128)(2,1)S(1)} %pad_maximum_fusion.10) | copy-start | bytes 196612
  38.3 7.3 %collective-permute-start.8 = (bf16[32,4096]{1,0:T(8,128)(2,1)S(1)}, bf16[32,4096]{1,0:T(8,128)(2,1)S(1)}, u32[]{:S(2)}, u32[]{:S(2)}) collective-permute-start(bf16[32,4096]{1,0:T(8,128)(2,1)S(1)} %bitcast.254), channel_id=1, source_target_pairs={{0,1},{1,0},{2,3},{3,2},{4,5},{5,4},{6,7},{7,6},{8,9},{9,8},{10,11... | collective-permute-start | bytes 786440 | tf_op jit(solution)/shard_map/ppermute | solution.py:39
  39.0 13.1 %collective-permute-start.9 = (bf16[32,4096]{1,0:T(8,128)(2,1)S(1)}, bf16[32,4096]{1,0:T(8,128)(2,1)S(1)}, u32[]{:S(2)}, u32[]{:S(2)}) collective-permute-start(bf16[32,4096]{1,0:T(8,128)(2,1)S(1)} %bitcast.253), channel_id=1, source_target_pairs={{0,2},{1,3},{2,0},{3,1},{4,6},{5,7},{6,4},{7,5},{8,10},{9,11},{10,... | collective-permute-start | bytes 786440 | tf_op jit(solution)/shard_map/ppermute | solution.py:39
  40.5 15.4 %collective-permute-start.10 = (bf16[32,4096]{1,0:T(8,128)(2,1)S(1)}, bf16[32,4096]{1,0:T(8,128)(2,1)S(1)}, u32[]{:S(2)}, u32[]{:S(2)}) collective-permute-start(bf16[32,4096]{1,0:T(8,128)(2,1)S(1)} %bitcast.252), channel_id=1, source_target_pairs={{0,3},{1,2},{2,1},{3,0},{4,7},{5,6},{6,5},{7,4},{8,11},{9,10},{10,... | collective-permute-start | bytes 786440 | tf_op jit(solution)/shard_map/ppermute | solution.py:39
  55.9 1.0 copy-start.10
  58.5 0.7 copy-start.1
  59.2 0.7 copy-start.16
  60.0 19.4 %copy-start.29 = (s32[16]{0:T(128)S(1)}, s32[16]{0:T(128)}, u32[]{:S(2)}) copy-start(s32[16]{0:T(128)} %get-tuple-element.46) | copy-start | bytes 196
  60.0 8.3 %collective-permute-start.11 = (bf16[32,4096]{1,0:T(8,128)(2,1)}, bf16[32,4096]{1,0:T(8,128)(2,1)}, u32[]{:S(2)}, u32[]{:S(2)}) collective-permute-start(bf16[32,4096]{1,0:T(8,128)(2,1)} %get-tuple-element.26), channel_id=1, source_target_pairs={{0,4},{1,5},{2,6},{3,7},{16,20},{17,21},{18,22},{19,23}} | collective-permute-start | bytes 786440 | tf_op jit(solution)/shard_map/ppermute | solution.py:244
  68.3 0.9 copy-start.2
  69.2 0.9 copy-start.17
  72.1 2.4 %collective-permute-start.12 = (bf16[32,4096]{1,0:T(8,128)(2,1)S(1)}, bf16[32,4096]{1,0:T(8,128)(2,1)S(1)}, u32[]{:S(2)}, u32[]{:S(2)}) collective-permute-start(bf16[32,4096]{1,0:T(8,128)(2,1)S(1)} %get-tuple-element.28), channel_id=1, source_target_pairs={{4,8},{5,9},{6,10},{7,11},{20,24},{21,25},{22,26},{23,27}} | collective-permute-start | bytes 786440 | tf_op jit(solution)/shard_map/ppermute | solution.py:244
  74.5 1.0 copy-start.3
  77.2 0.7 copy-start.11
  77.9 1.5 collective-permute-start.13
  79.4 1.0 copy-start.4
  80.3 0.9 copy-start.8
  81.3 0.9 copy-start.12
  85.0 7.1 %copy-start.18 = (bf16[32,4096]{1,0:T(8,128)(2,1)}, bf16[32,4096]{1,0:T(8,128)(2,1)S(1)}, u32[]{:S(2)}) copy-start(bf16[32,4096]{1,0:T(8,128)(2,1)S(1)} %get-tuple-element.32) | copy-start | bytes 786436
  85.0 9.7 %collective-permute-start.19 = (bf16[32,4096]{1,0:T(8,128)(2,1)}, bf16[32,4096]{1,0:T(8,128)(2,1)}, u32[]{:S(2)}, u32[]{:S(2)}) collective-permute-start(bf16[32,4096]{1,0:T(8,128)(2,1)} %get-tuple-element.35.came.held), channel_id=1, source_target_pairs={{0,2},{1,3},{2,0},{3,1},{4,6},{5,7},{6,4},{7,5},{8,10},{9,11},{10,... | collective-permute-start | bytes 786440 | tf_op jit(solution)/shard_map/ppermute | solution.py:39
  89.1 0.9 copy-start.5
  92.1 0.7 copy-start.13
  94.7 9.9 %copy-start.6 = (bf16[32,4096]{1,0:T(8,128)(2,1)S(1)}, bf16[32,4096]{1,0:T(8,128)(2,1)}, u32[]{:S(2)}) copy-start(bf16[32,4096]{1,0:T(8,128)(2,1)} %copy-done.1) | copy-start | bytes 786436
  94.7 9.9 %copy-start.9 = (bf16[32,4096]{1,0:T(8,128)(2,1)S(1)}, bf16[32,4096]{1,0:T(8,128)(2,1)}, u32[]{:S(2)}) copy-start(bf16[32,4096]{1,0:T(8,128)(2,1)} %dynamic-slice_bitcast_fusion.grad.held) | copy-start | bytes 786436
  95.8 12.5 %collective-permute-start.20 = (bf16[2,32,4096]{2,1,0:T(8,128)(2,1)S(1)}, bf16[2,32,4096]{2,1,0:T(8,128)(2,1)S(1)}, u32[]{:S(2)}, u32[]{:S(2)}) collective-permute-start(bf16[2,32,4096]{2,1,0:T(8,128)(2,1)S(1)} %get-tuple-element.64), channel_id=1, source_target_pairs={{0,1},{1,0},{2,3},{3,2},{4,5},{5,4},{6,7},{7,6},{8,9},{9,8},{10,11... | collective-permute-start | bytes 1572872 | tf_op jit(solution)/shard_map/ppermute | solution.py:39
  97.8 3.8 %collective-permute-start.18 = (bf16[32,1024]{1,0:T(8,128)(2,1)S(1)}, bf16[32,1024]{1,0:T(8,128)(2,1)S(1)}, u32[]{:S(2)}, u32[]{:S(2)}) collective-permute-start(bf16[32,1024]{1,0:T(8,128)(2,1)S(1)} %bitcast.257), channel_id=1, source_target_pairs={{0,3},{1,2},{2,1},{3,0},{4,7},{5,6},{6,5},{7,4},{8,11},{9,10},{10,... | collective-permute-start | bytes 196616 | tf_op jit(solution)/shard_map/ppermute | solution.py:39
  98.6 5.1 %collective-permute-start.17 = (bf16[32,1024]{1,0:T(8,128)(2,1)S(1)}, bf16[32,1024]{1,0:T(8,128)(2,1)S(1)}, u32[]{:S(2)}, u32[]{:S(2)}) collective-permute-start(bf16[32,1024]{1,0:T(8,128)(2,1)S(1)} %bitcast.258), channel_id=1, source_target_pairs={{0,2},{1,3},{2,0},{3,1},{4,6},{5,7},{6,4},{7,5},{8,10},{9,11},{10,... | collective-permute-start | bytes 196616 | tf_op jit(solution)/shard_map/ppermute | solution.py:39
  100.1 3.6 %collective-permute-start.16 = (bf16[32,1024]{1,0:T(8,128)(2,1)S(1)}, bf16[32,1024]{1,0:T(8,128)(2,1)S(1)}, u32[]{:S(2)}, u32[]{:S(2)}) collective-permute-start(bf16[32,1024]{1,0:T(8,128)(2,1)S(1)} %bitcast.259), channel_id=1, source_target_pairs={{0,1},{1,0},{2,3},{3,2},{4,5},{5,4},{6,7},{7,6},{8,9},{9,8},{10,11... | collective-permute-start | bytes 196616 | tf_op jit(solution)/shard_map/ppermute | solution.py:39
  100.9 3.6 %collective-permute-start.14 = (bf16[32,4096]{1,0:T(8,128)(2,1)}, bf16[32,4096]{1,0:T(8,128)(2,1)S(1)}, u32[]{:S(2)}, u32[]{:S(2)}) collective-permute-start(bf16[32,4096]{1,0:T(8,128)(2,1)} %copy-done.18), channel_id=1, source_target_pairs={{12,8},{13,9},{14,10},{15,11},{28,24},{29,25},{30,26},{31,27}} | collective-permute-start | bytes 786440 | tf_op jit(solution)/shard_map/ppermute | solution.py:279
  103.7 4.8 %copy-start.21 = (bf16[1,4096,512]{2,1,0:T(8,128)(2,1)S(1)}, bf16[1,4096,512]{2,1,0:T(8,128)(2,1)}, u32[]{:S(2)}) copy-start(bf16[1,4096,512]{2,1,0:T(8,128)(2,1)} %param.16) | copy-start | bytes 12582916
  106.2 0.7 copy-start.14
  106.9 6.3 %collective-permute-start.15 = (bf16[32,4096]{1,0:T(8,128)(2,1)}, bf16[32,4096]{1,0:T(8,128)(2,1)}, u32[]{:S(2)}, u32[]{:S(2)}) collective-permute-start(bf16[32,4096]{1,0:T(8,128)(2,1)} %get-tuple-element.34), channel_id=1, source_target_pairs={{8,4},{9,5},{10,6},{11,7},{24,20},{25,21},{26,22},{27,23}} | collective-permute-start | bytes 786440 | tf_op jit(solution)/shard_map/ppermute | solution.py:279
  108.4 3.1 %copy-start.27 = (bf16[4,16,512]{2,1,0:T(8,128)(2,1)S(1)}, bf16[4,16,512]{2,1,0:T(8,128)(2,1)}, u32[]{:S(2)}) copy-start(bf16[4,16,512]{2,1,0:T(8,128)(2,1)} %copy-done.26) | copy-start | bytes 196612
  113.2 1.0 copy-start.7
  114.2 0.9 copy-start.15
  117.1 41.0 %copy-start.22 = (bf16[1,512,4096]{2,1,0:T(8,128)(2,1)S(1)}, bf16[1,512,4096]{2,1,0:T(8,128)(2,1)}, u32[]{:S(2)}) copy-start(bf16[1,512,4096]{2,1,0:T(8,128)(2,1)} %param.19) | copy-start | bytes 12582916
  117.1 31.8 %collective-permute-start.21 = (bf16[32,4096]{1,0:T(8,128)(2,1)S(1)}, bf16[32,4096]{1,0:T(8,128)(2,1)S(1)}, u32[]{:S(2)}, u32[]{:S(2)}) collective-permute-start(bf16[32,4096]{1,0:T(8,128)(2,1)S(1)} %get-tuple-element.42), channel_id=1, source_target_pairs={{4,0},{5,1},{6,2},{7,3},{20,16},{21,17},{22,18},{23,19}} | collective-permute-start | bytes 786440 | tf_op jit(solution)/shard_map/ppermute | solution.py:279
  148.9 6.9 %collective-permute-start.22 = (bf16[32,4096]{1,0:T(8,128)(2,1)S(1)}, bf16[32,4096]{1,0:T(8,128)(2,1)S(1)}, u32[]{:S(2)}, u32[]{:S(2)}) collective-permute-start(bf16[32,4096]{1,0:T(8,128)(2,1)S(1)} %multiply_convert_fusion), channel_id=1, source_target_pairs={{0,2},{1,3},{2,0},{3,1},{4,6},{5,7},{6,4},{7,5},{8,10},{9,11},{10,... | collective-permute-start | bytes 786440 | tf_op jit(solution)/shard_map/ppermute | solution.py:39
  155.9 2.0 %collective-permute-start.23 = (bf16[2,32,4096]{2,1,0:T(8,128)(2,1)S(1)}, bf16[2,32,4096]{2,1,0:T(8,128)(2,1)S(1)}, u32[]{:S(2)}, u32[]{:S(2)}) collective-permute-start(bf16[2,32,4096]{2,1,0:T(8,128)(2,1)S(1)} %get-tuple-element.62), channel_id=1, source_target_pairs={{0,1},{1,0},{2,3},{3,2},{4,5},{5,4},{6,7},{7,6},{8,9},{9,8},{10,11... | collective-permute-start | bytes 1572872 | tf_op jit(solution)/shard_map/ppermute | solution.py:39
  158.0 1.7 copy-start.25
  158.0 1.8 copy-start.28
  158.0 2.0 %copy-start.23 = (bf16[4,32,2,256]{3,2,1,0:T(2,128)(2,1)S(1)}, bf16[4,32,2,256]{3,2,1,0:T(2,128)(2,1)}, u32[]{:S(2)}) copy-start(bf16[4,32,2,256]{3,2,1,0:T(2,128)(2,1)} %reshape.649) | copy-start | bytes 393220
  160.2 3.8 %copy-start.20 = (bf16[1,4096,512]{2,1,0:T(8,128)(2,1)S(1)}, bf16[1,4096,512]{2,1,0:T(8,128)(2,1)}, u32[]{:S(2)}) copy-start(bf16[1,4096,512]{2,1,0:T(8,128)(2,1)} %param.18) | copy-start | bytes 12582916
  169.1 1.8 collective-permute-start.24
  171.4 5.8 %collective-permute-start.25 = (bf16[4,4,4096]{2,1,0:T(4,128)(2,1)S(1)}, bf16[4,4,4096]{2,1,0:T(4,128)(2,1)S(1)}, u32[]{:S(2)}, u32[]{:S(2)}) collective-permute-start(bf16[4,4,4096]{2,1,0:T(4,128)(2,1)S(1)} %fusion.52), channel_id=1, source_target_pairs={{0,2},{1,3},{2,0},{3,1},{4,6},{5,7},{6,4},{7,5},{8,10},{9,11},{10,... | collective-permute-start | bytes 393224 | tf_op jit(solution)/shard_map/ppermute | solution.py:39
  177.4 5.8 %collective-permute-start.28 = (bf16[4,4096]{1,0:T(4,128)(2,1)S(1)}, bf16[4,4096]{1,0:T(4,128)(2,1)S(1)}, u32[]{:S(2)}, u32[]{:S(2)}) collective-permute-start(bf16[4,4096]{1,0:T(4,128)(2,1)S(1)} %get-tuple-element.76), channel_id=1, source_target_pairs={{0,12},{4,8},{8,4},{12,0},{1,13},{5,9},{9,5},{13,1},{2,14},{6,10},... | collective-permute-start | bytes 98312 | tf_op jit(solution)/shard_map/ppermute | solution.py:39
  177.5 5.7 %collective-permute-start.27 = (bf16[4,4096]{1,0:T(4,128)(2,1)S(1)}, bf16[4,4096]{1,0:T(4,128)(2,1)S(1)}, u32[]{:S(2)}, u32[]{:S(2)}) collective-permute-start(bf16[4,4096]{1,0:T(4,128)(2,1)S(1)} %get-tuple-element.77), channel_id=1, source_target_pairs={{0,8},{4,12},{8,0},{12,4},{1,9},{5,13},{9,1},{13,5},{2,10},{6,14},... | collective-permute-start | bytes 98312 | tf_op jit(solution)/shard_map/ppermute | solution.py:39
  178.5 5.3 %collective-permute-start.26 = (bf16[4,4096]{1,0:T(4,128)(2,1)S(1)}, bf16[4,4096]{1,0:T(4,128)(2,1)S(1)}, u32[]{:S(2)}, u32[]{:S(2)}) collective-permute-start(bf16[4,4096]{1,0:T(4,128)(2,1)S(1)} %get-tuple-element.75), channel_id=1, source_target_pairs={{0,4},{4,0},{8,12},{12,8},{1,5},{5,1},{9,13},{13,9},{2,6},{6,2},{1... | collective-permute-start | bytes 98312 | tf_op jit(solution)/shard_map/ppermute | solution.py:39

commit v3 on v1

v3 whole, which is shorter than its diff:
```python
import functools
import math

import jax
import jax.numpy as jnp
from jax import lax
from jax.experimental import pallas as pl
from jax.experimental.pallas import tpu as pltpu
from jax.sharding import PartitionSpec as P

HD = 256
NEG_FILL = -1e30
KEEP_SCALE = 8.0 / 7.0
BF = jnp.bfloat16
F32 = jnp.float32
MEBI = 1024 * 1024
NN = (((1,), (0,)), ((), ()))
NT = (((1,), (1,)), ((), ()))
SCALE = 1.0 / math.sqrt(HD)


def shifted_right(source_bits, amount):
    return lax.shift_right_logical(source_bits, jnp.full(source_bits.shape, amount, jnp.int32))


def keep_factor(seed_value, first_row, row_count, col_count):
    position = (
        (first_row + jnp.arange(row_count, dtype=jnp.int32))[:, None] * col_count
        + jnp.arange(col_count, dtype=jnp.int32)[None, :]
    )
    hashed = position ^ seed_value * 1640531527
    hashed = hashed ^ shifted_right(hashed, 16)
    hashed = hashed * 2146121005
    hashed = hashed ^ shifted_right(hashed, 15)
    hashed = hashed * 1911520717
    hashed = hashed ^ shifted_right(hashed, 16)
    is_kept = shifted_right(hashed, 8) & 7 != 0
    return jnp.where(is_kept, KEEP_SCALE, 0.0).astype(F32)


def swap(array, axis, k):
    size = lax.axis_size(axis)
    return lax.ppermute(array, axis, [(i, i ^ k) for i in range(size)])


def over_mp(array):
    evens = [array]
    for k in range(2, lax.axis_size("mp"), 2):
        evens.append(swap(array, "mp", k))
    pieces = []
    for even in evens:
        pieces += [even, swap(even, "mp", 1)]
    return pieces


def product(left, right, dims):
    return lax.dot_general(left, right, dims, preferred_element_type=F32)


def softmax_down(scores, allowed, src):
    shape = scores.shape
    scores = jnp.where(allowed != 0, scores * SCALE, NEG_FILL).reshape(-1, src, shape[1])
    exp_terms = jnp.exp(scores - jnp.max(scores, axis=1, keepdims=True))
    return (exp_terms / jnp.sum(exp_terms, axis=1, keepdims=True)).reshape(shape)


def softmax_back(probs, d_probs, src):
    shape = probs.shape
    probs = probs.reshape(-1, src, shape[1])
    d_probs = d_probs.reshape(probs.shape)
    inner = jnp.sum(probs * d_probs, axis=1, keepdims=True)
    return (probs * (d_probs - inner) * SCALE).reshape(shape)


def spread(weights, fold):
    return product(jnp.transpose(weights).astype(BF), fold[...], NN)


def picked(where, step, came, held):
    return jnp.where(where[0] == step, came[...], held[...])


def keys_values_kernel(n, src, heads, where, *refs):
    pieces, (by_owner, wk, wv, wo, keys, values), folds = refs[:n], refs[n : n + 6], refs[n + 6 :]
    rows = jnp.concatenate([piece[...] for piece in pieces], axis=0)
    for weight, out in ((wv, values), (wk, keys)):
        flat = product(rows, weight[...], NN).astype(BF)
        out[...] = product(by_owner[...], flat, NN).astype(BF)
    fold_loop(n, src, heads, values, folds, lambda h, cols: wo[h * HD : (h + 1) * HD, cols], NN)


def fold_loop(n, src, heads, source, folds, weight, dims):
    dim = folds[0].shape[1]
    width = min(dim, 1024)
    for first in range(0, dim, width):
        cols = slice(first, first + width)
        for h in range(heads):
            part = product(source[:, h * HD : (h + 1) * HD], weight(h, cols), dims).astype(BF)
            for k in range(n):
                folds[k][h * src : (h + 1) * src, cols] = part[k * src : (k + 1) * src]


def query_fold_kernel(n, src, heads, where, keys, wq, *folds):
    fold_loop(n, src, heads, keys, folds, lambda h, cols: wq[cols, h * HD : (h + 1) * HD], NT)


def forward(tokens, allowed, factor, query_fold, out_fold, src):
    probs = softmax_down(product(query_fold[...], tokens, NT), allowed[...], src)
    return (tokens.astype(F32) + factor[...] * spread(probs, out_fold)).astype(BF)


def first_kernel(n, src, where, held, allowed, factor, *refs):
    blocks, (query_fold, out_fold, following) = refs[: 2 * n], refs[2 * n :]
    size = blocks[0].shape[0]
    for k in range(n):
        query_fold[k * size : (k + 1) * size] = blocks[k][...]
        out_fold[k * size : (k + 1) * size] = blocks[n + k][...]
    following[...] = forward(held[...], allowed, factor, query_fold, out_fold, src)


def forward_kernel(
    step, src, where, came, held, allowed, factor, query_fold, out_fold, current, following
):
    tokens = picked(where, step, came, held)
    current[...] = tokens
    following[...] = forward(tokens, allowed, factor, query_fold, out_fold, src)


def backward(probs, grad, factor, query_fold, out_fold, src):
    d_out = (grad.astype(F32) * factor[...]).astype(BF)
    d_scores = softmax_back(probs, product(out_fold[...], d_out, NT), src)
    return (grad.astype(F32) + spread(d_scores, query_fold)).astype(BF)


def turn_kernel(
    step, src, where, came, held, allowed, factor, query_fold, out_fold, grad, current, kept, before
):
    tokens = picked(where, step, came, held)
    current[...] = tokens
    probs = softmax_down(product(query_fold[...], tokens, NT), allowed[...], src)
    kept[...] = probs
    before[...] = backward(probs, grad[...], factor, query_fold, out_fold, src)


def backward_kernel(
    step, src, where, came, held, probs, factor, query_fold, out_fold, current, before
):
    grad = picked(where, step, came, held)
    current[...] = grad
    before[...] = backward(probs[...], grad, factor, query_fold, out_fold, src)


def dropped_kernel(step, where, came, held, factor, d_out):
    grad = picked(where, step, came, held)
    d_out[...] = (grad.astype(F32) * factor[...]).astype(BF)


def outputs_kernel(n, where, current, probs, factor, out_fold, *parts):
    width = parts[0].shape[1]
    turned = jnp.transpose(probs[...]).astype(BF)
    for j in range(n):
        cols = pl.ds(pl.multiple_of((where[1] ^ j) * width, width), width)
        summed = product(turned, out_fold[:, cols], NN)
        total = current[:, cols].astype(F32) + factor[:, cols] * summed
        parts[j][...] = total.astype(BF)


def order_kernel(n, where, *refs):
    for j in range(n):
        refs[n][where[1] ^ j] = refs[j][...]


def heads_of(n, heads, rows, src):
    for k in range(n):
        for h in range(heads):
            tile = slice((k * heads + h) * src, (k * heads + h + 1) * src)
            cols = slice(h * HD, (h + 1) * HD)
            yield tile, slice(k * rows, (k + 1) * rows), slice(k * src, (k + 1) * src), cols


def query_kernel(n, src, heads, where, keys, wq, allowed, *refs):
    pieces, (query, probs) = refs[:n], refs[n:]
    rows = pieces[0].shape[0]
    tokens = jnp.concatenate([piece[...] for piece in pieces], axis=0)
    query[...] = product(tokens, wq[...], NN).astype(BF)
    for tile, toks, srcs, cols in heads_of(n, heads, rows, src):
        scores = product(keys[srcs, cols], query[toks, cols], NT)
        probs[tile] = softmax_down(scores, allowed[tile], src)


def terms_kernel(n, src, heads, where, keys, values, query, probs, by_micro, wk, wv, wo, *refs):
    pieces, (kept, sent, d_att, d_keys, d_values) = refs[:n], refs[n:]
    rows = pieces[0].shape[0]
    grads = jnp.concatenate([piece[...] for piece in pieces], axis=0)
    d_att[...] = product(grads, wo[...], NT).astype(BF)
    for tile, toks, srcs, cols in heads_of(n, heads, rows, src):
        own = probs[tile]
        d_scores = softmax_back(own, product(values[srcs, cols], d_att[toks, cols], NT), src)
        d_keys[srcs, cols] = product(d_scores.astype(BF), query[toks, cols], NN).astype(BF)
        d_values[srcs, cols] = product(own.astype(BF), d_att[toks, cols], NN).astype(BF)
    key_rows = product(by_micro[...], d_keys[...], NN).astype(BF)
    value_rows = product(by_micro[...], d_values[...], NN).astype(BF)
    size = key_rows.shape[0] // n
    dim = kept.shape[1]
    width = min(dim, 1024)
    for first in range(0, dim, width):
        cols = slice(first, first + width)
        part = product(key_rows, wk[cols], NT) + product(value_rows, wv[cols], NT)
        for k in range(0, n, 2):
            to = slice(k // 2 * size, (k // 2 + 1) * size)
            kept[to, cols] = part[k * size : (k + 1) * size]
            sent[to, cols] = part[(k + 1) * size : (k + 2) * size].astype(BF)


def on_chip(body, outs, where, *args, scratch=()):
    vmem = pl.BlockSpec(memory_space=pltpu.VMEM)
    outs = [jax.ShapeDtypeStruct(*out) for out in outs]
    size = sum(math.prod(a.shape) * a.dtype.itemsize for a in (*args, *outs, *scratch))
    return pl.pallas_call(
        body,
        out_shape=outs,
        in_specs=[pl.BlockSpec(memory_space=pltpu.SMEM)] + [vmem] * len(args),
        out_specs=[vmem] * len(outs),
        scratch_shapes=[pltpu.VMEM(s.shape, s.dtype) for s in scratch],
        compiler_params=pltpu.CompilerParams(vmem_limit_bytes=size + size // 2 + 4 * MEBI),
        cost_estimate=pl.CostEstimate(
            flops=64 * size, bytes_accessed=size, transcendentals=0
        ),
    )(where, *args)


def per_device(
    memory, decoder_in, cotangent, src_lengths, tgt_segments, seeds, w_query, w_key, w_value, w_out
):
    micro_count, tgt_rows, dim = decoder_in.shape
    local_cols = w_query.shape[2]
    heads = local_cols // HD
    sections = lax.axis_size("section")
    n_mp = lax.axis_size("mp")
    section = lax.axis_index("section")
    me = lax.axis_index("mp")
    where = jnp.stack([section, me]).astype(jnp.int32)
    share = n_mp // micro_count
    rows = tgt_rows // share
    src = sections * n_mp
    fold_rows = heads * src
    wq, wk, wv, wo = w_query[0], w_key[0], w_value[0], w_out[0]

    own = memory.reshape(micro_count, dim)
    over_z = [own if a == 0 else swap(own, "section", a) for a in range(sections)]
    pieces = over_mp(jnp.concatenate(over_z, axis=0))

    def row_ids(device):
        j = jnp.arange(n_mp, dtype=jnp.int32)[:, None]
        a = jnp.arange(sections, dtype=jnp.int32)[None, :]
        return ((section ^ a) * n_mp + (device ^ j)).reshape(src)

    doc_ends = jnp.cumsum(src_lengths, axis=1)

    def allowed_of(owner, heads_owner):
        micro = owner // share
        ends = lax.dynamic_index_in_dim(doc_ends, micro, 0, keepdims=False)
        segments = lax.dynamic_index_in_dim(tgt_segments, micro, 0, keepdims=False)
        segments = lax.dynamic_slice_in_dim(segments, (owner % share) * rows, rows, 0)
        docs = jnp.sum((ends[None, :] <= row_ids(heads_owner)[:, None]).astype(jnp.int32), axis=1)
        return docs[:, None] == segments[None, :]

    def every_head(blocks):
        blocks = jnp.broadcast_to(jnp.stack(blocks)[:, None], (n_mp, heads, src, rows))
        return blocks.astype(jnp.int32).reshape(n_mp * fold_rows, rows)

    allowed = every_head([allowed_of(me, me ^ k) for k in range(n_mp)])
    own_allowed = every_head([allowed_of(me ^ j, me) for j in range(n_mp)])

    to_row = jnp.arange(n_mp * src, dtype=jnp.int32)[:, None]
    from_row = jnp.arange(src * micro_count, dtype=jnp.int32)[None, :]
    by_owner = (to_row % src == from_row // micro_count) & (
        (me ^ (to_row // src)) // share == from_row % micro_count
    )
    by_owner = by_owner.astype(BF)

    def mine(array):
        part = lax.dynamic_index_in_dim(array, me // share, 0, keepdims=False)
        return lax.dynamic_slice_in_dim(part, (me % share) * rows, rows, 0)

    factor = keep_factor(seeds[me // share, 0], (me % share) * rows, rows, dim)
    held = mine(decoder_in)
    grad = mine(cotangent)
    allowed, own_allowed, by_owner, by_micro, factor, held, grad = lax.optimization_barrier(
        (allowed, own_allowed, by_owner, by_owner.T, factor, held, grad)
    )

    wide = ((rows, dim), BF)
    stacked = ((n_mp * src, local_cols), BF)
    block = ((fold_rows, dim), BF)
    whole_fold = ((n_mp * fold_rows, dim), BF)
    keys, values, *out_blocks = on_chip(
        functools.partial(keys_values_kernel, n_mp, src, heads),
        [stacked, stacked] + [block] * n_mp,
        where,
        *pieces,
        by_owner,
        wk,
        wv,
        wo,
    )
    query_blocks = on_chip(
        functools.partial(query_fold_kernel, n_mp, src, heads), [block] * n_mp, where, keys, wq
    )

    def to_owners(blocks):
        return [part if j == 0 else swap(part, "mp", j) for j, part in enumerate(blocks)]

    out_blocks = to_owners(out_blocks)
    query_blocks = to_owners(query_blocks)
    query_fold, out_fold, following = on_chip(
        functools.partial(first_kernel, n_mp, src),
        [whole_fold, whole_fold, wide],
        where,
        held,
        allowed,
        factor,
        *query_blocks,
        *out_blocks,
    )
    folds = (query_fold, out_fold)
    for step in range(1, sections):
        came = lax.ppermute(following, "section", [(step - 1, step)])
        if step < sections - 1:
            held, following = on_chip(
                functools.partial(forward_kernel, step, src),
                [wide, wide],
                where,
                came,
                held,
                allowed,
                factor,
                *folds,
            )
    current, probs, before = on_chip(
        functools.partial(turn_kernel, sections - 1, src),
        [wide, (allowed.shape, F32), wide],
        where,
        came,
        held,
        allowed,
        factor,
        *folds,
        grad,
    )

    out_cols = dim // n_mp
    for step in range(sections - 1, 0, -1):
        came = lax.ppermute(before, "section", [(step, step - 1)])
        if step == 3:
            parts = on_chip(
                functools.partial(outputs_kernel, n_mp),
                [((rows, out_cols), BF)] * n_mp,
                where,
                current,
                probs,
                factor,
                out_fold,
            )
            came, parts = lax.optimization_barrier((came, parts))
        if step == 2:
            came, parts = lax.optimization_barrier((came, to_owners(parts)))
        if step == 1:
            (section_out,) = on_chip(
                functools.partial(order_kernel, n_mp),
                [((n_mp, rows, out_cols), BF)],
                where,
                *parts,
            )
            came, section_out, every_x = lax.optimization_barrier(
                (came, section_out, over_mp(current))
            )
            break
        grad, before = on_chip(
            functools.partial(backward_kernel, step - 1, src),
            [wide, wide],
            where,
            came,
            grad,
            probs,
            factor,
            *folds,
        )
    (d_out,) = on_chip(functools.partial(dropped_kernel, 0), [wide], where, came, grad, factor)

    query, own_probs = on_chip(
        functools.partial(query_kernel, n_mp, src, heads),
        [((n_mp * rows, local_cols), BF), (own_allowed.shape, F32)],
        where,
        keys,
        wq,
        own_allowed,
        *every_x,
    )
    half_rows = n_mp // 2 * sections * micro_count
    kept, sent = on_chip(
        functools.partial(terms_kernel, n_mp, src, heads),
        [((half_rows, dim), F32), ((half_rows, dim), BF)],
        where,
        keys,
        values,
        query,
        own_probs,
        by_micro,
        wk,
        wv,
        wo,
        *over_mp(d_out),
        scratch=[
            jax.ShapeDtypeStruct((n_mp * rows, local_cols), BF),
            jax.ShapeDtypeStruct(*stacked),
            jax.ShapeDtypeStruct(*stacked),
        ],
    )
    half = (kept + swap(sent, "mp", 1).astype(F32)).reshape(n_mp // 2, -1, dim)
    total = half[0]
    for j in range(1, n_mp // 2):
        total = total + swap(half[j].astype(BF), "mp", 2 * j).astype(F32)
    total = total.reshape(sections, micro_count, dim)
    mem_grad = total[0]
    for a in range(1, sections):
        mem_grad = mem_grad + swap(total[a].astype(BF), "section", a).astype(F32)
    return (section_out.reshape(1, micro_count, tgt_rows, out_cols), mem_grad[None])


def solution(mesh):
    return jax.shard_map(
        per_device,
        mesh=mesh,
        in_specs=(
            P(("section", "mp"), "groups", None),
            P("groups", None, None),
            P("groups", None, None),
            P("groups", None),
            P("groups", None),
            P("groups", "section"),
            P("section", None, "mp"),
            P("section", None, "mp"),
            P("section", None, "mp"),
            P("section", "mp", None),
        ),
        out_specs=(P("section", "groups", None, "mp"), P(("section", "mp"), "groups", None)),
        check_vma=False,
    )
```

time: 154 us -> 140 us (0.909)
  matrix products: 40 us -> 0 us
  Pallas kernels: 0 us -> 23.6 us
  waiting for transfers between devices: 64.5 us -> 70.4 us
  other arithmetic: 10.2 us -> 5.17 us
    dot_general x27 -> x0, matrix products: 39.8 us -> none  [the longest x26 39.1 us: dot_f32(): return jnp.einsum(spec, left, right, preferred_element_type=F32)]
    pallas_call x0 -> x13, Pallas kernels: none -> 23.6 us  [on_chip(): pl.pallas_call(body, out_shape=outs, in_specs=[pl.BlockSpec(memory_space=...]
    ppermute x23 -> x26, waiting for transfers between devices: 32.3 us -> 40 us  [swap(): return lax.ppermute(array, axis, [(i, i ^ k) for i in range(size)])]
    unnamed x20 -> x14, local copies, waits for them, and re-layouts: 2.44 us -> 6.58 us
    ppermute x3, waiting for transfers between devices: 26.6 us -> 24.4 us  [per_device(): came = lax.ppermute(before, 'section', [(step, step - 1)])]
    another operation x13 -> x2, other arithmetic: 2.25 us -> 0.11 us  [the longest x1 0.08 us: per_device(): where = jnp.stack([section, me]).astype(jnp.int32)]
    ppermute x3, starting transfers between devices: 2.79 us -> 4.69 us  [per_device(): came = lax.ppermute(following, 'section', [(step - 1, step)])]
    unnamed x2 -> x0, other arithmetic: 1.81 us -> none
  transfers between devices with their start and end apart: 29 -> 32, of which waited for: 16 -> 18; matrix products, arithmetic and copies ran while one was open for 16% -> 4% of each run, Pallas kernels for 0% -> 6%
where the time goes in v3:
time: 140 us
  waiting for transfers between devices  70.4 us (50%)
  starting transfers between devices  30.5 us (22%)
  Pallas kernels  23.6 us (17%)
  local copies, waits for them, and re-layouts  8.91 us (6%)
  other arithmetic  5.17 us (4%)
    ppermute x26, waiting for transfers between devices, swap(): return lax.ppermute(array, axis, [(i, i ^ k) for i in range(size)])  40 us
    ppermute x3, waiting for transfers between devices, per_device(): came = lax.ppermute(before, 'section', [(step, step - 1)])  24.4 us
    pallas_call x13, Pallas kernels, on_chip(): pl.pallas_call(body, out_shape=outs, in_specs=[pl.BlockSpec(memory_space=...  23.6 us
    ppermute x26, starting transfers between devices, swap(): return lax.ppermute(array, axis, [(i, i ^ k) for i in range(size)])  22.7 us
    unnamed x14, local copies, waits for them, and re-layouts  6.58 us
    ppermute x3, waiting for transfers between devices, per_device(): came = lax.ppermute(following, 'section', [(step - 1, step)])  6.06 us
    ppermute x3, starting transfers between devices, per_device(): came = lax.ppermute(following, 'section', [(step - 1, step)])  4.69 us
    ppermute x3, starting transfers between devices, per_device(): came = lax.ppermute(before, 'section', [(step, step - 1)])  3.09 us
  transfers between devices with their start and end apart: 32, of which 18 were waited for; matrix products, arithmetic and copies ran while one was open for 4% of the time, Pallas kernels for 6%

profile of v3, /device:TPU:0, one launch (start us, length us, event | category | flops | bytes accessed | tf_op | source)
XLA Modules:
  0.0 139.5 jit_solution(12521577831196927610)
XLA Ops:
  0.6 5.1 %collective-permute-start.2 = (bf16[4,4096]{1,0:T(4,128)(2,1)}, bf16[4,4096]{1,0:T(4,128)(2,1)S(1)}, u32[]{:S(2)}, u32[]{:S(2)}) collective-permute-start(bf16[4,4096]{1,0:T(4,128)(2,1)} %bitcast.47), channel_id=1, source_target_pairs={{0,12},{4,8},{8,4},{12,0},{1,13},{5,9},{9,5},{13,1},{2,14},{6,10},... | collective-permute-start | bytes 98312 | tf_op jit(solution)/shard_map/ppermute | solution.py:43
  5.7 0.6 collective-permute-start
  6.5 0.9 reduce_window_sum.11
  7.3 1.2 fusion.26
  8.6 0.8 fusion.18
  9.8 0.9 fusion.5.factor
  10.8 1.1 dynamic-slice_bitcast_fusion
  11.8 0.1 and_convert_fusion
  12.0 0.1 convert_reduce_fusion.2
  12.2 0.8 pad_maximum_fusion.refs_0_
  13.0 1.7 %collective-permute-start.4 = (bf16[16,4096]{1,0:T(8,128)(2,1)S(1)}, bf16[16,4096]{1,0:T(8,128)(2,1)S(1)}, u32[]{:S(2)}, u32[]{:S(2)}) collective-permute-start(bf16[16,4096]{1,0:T(8,128)(2,1)S(1)} %pad_maximum_fusion.refs_0_), channel_id=1, source_target_pairs={{0,2},{1,3},{2,0},{3,1},{4,6},{5,7},{6,4},{7,5},{8,10},{9,11},{10,... | collective-permute-start | bytes 393224 | tf_op jit(solution)/shard_map/ppermute | solution.py:43
  14.8 3.2 %collective-permute-done.4.refs_2_ = bf16[16,4096]{1,0:T(8,128)(2,1)S(1)} collective-permute-done((bf16[16,4096]{1,0:T(8,128)(2,1)S(1)}, bf16[16,4096]{1,0:T(8,128)(2,1)S(1)}, u32[]{:S(2)}, u32[]{:S(2)}) %collective-permute-start.4) | collective-permute-done | bytes 131104 | tf_op jit(solution)/shard_map/ppermute | solution.py:43
  18.2 1.2 collective-permute-done.5.refs_3_
  19.4 2.2 %copy-done = bf16[1,4096,512]{2,1,0:T(8,128)(2,1)S(1)} copy-done((bf16[1,4096,512]{2,1,0:T(8,128)(2,1)S(1)}, bf16[1,4096,512]{2,1,0:T(8,128)(2,1)}, u32[]{:S(2)}) %copy-start) | copy-done | bytes 4194328
  21.6 2.2 %copy-done.2 = bf16[1,4096,512]{2,1,0:T(8,128)(2,1)S(1)} copy-done((bf16[1,4096,512]{2,1,0:T(8,128)(2,1)S(1)}, bf16[1,4096,512]{2,1,0:T(8,128)(2,1)}, u32[]{:S(2)}) %copy-start.2) | copy-done | bytes 4194328
  23.8 2.2 %copy-done.4 = bf16[1,512,4096]{2,1,0:T(8,128)(2,1)S(1)} copy-done((bf16[1,512,4096]{2,1,0:T(8,128)(2,1)S(1)}, bf16[1,512,4096]{2,1,0:T(8,128)(2,1)}, u32[]{:S(2)}) %copy-start.4) | copy-done | bytes 4194328
  26.0 3.1 %shard_map.113 = (bf16[64,512]{1,0:T(8,128)(2,1)S(1)}, bf16[64,512]{1,0:T(8,128)(2,1)S(1)}, bf16[32,4096]{1,0:T(8,128)(2,1)S(1)}, bf16[32,4096]{1,0:T(8,128)(2,1...) custom-call(s32[2]{0:T(128)S(1)} %pad_add_fusion.2.where, ...), custom_call_target="tpu_custom_call" | custom-call | flops 914882560 | bytes 14295040 | tf_op jit(solution)/shard_map/pallas_call | solution.py:219
  29.1 0.2 collective-permute-start.9
  29.3 1.6 %collective-permute-start.10 = (bf16[32,4096]{1,0:T(8,128)(2,1)S(1)}, bf16[32,4096]{1,0:T(8,128)(2,1)S(1)}, u32[]{:S(2)}, u32[]{:S(2)}) collective-permute-start(bf16[32,4096]{1,0:T(8,128)(2,1)S(1)} %get-tuple-element.68), channel_id=1, source_target_pairs={{0,2},{1,3},{2,0},{3,1},{4,6},{5,7},{6,4},{7,5},{8,10},{9,11},{10,... | collective-permute-start | bytes 786440 | tf_op jit(solution)/shard_map/ppermute | solution.py:43
  31.0 1.9 %shard_map.114 = (bf16[32,4096]{1,0:T(8,128)(2,1)S(1)}, bf16[32,4096]{1,0:T(8,128)(2,1)S(1)}, bf16[32,4096]{1,0:T(8,128)(2,1)S(1)}, bf16[32,4096]{1,0:T(8,128)(2,1)S(1)}) custom-call(s32[2]{0:T(128)S(1)} %pad_add_fusion.2.where, bf16[64,512]{1,0:T(8,128)(2,1)S(1)} %get-tuple-element.61.keys, bf16[4096,512]{1,0:T(8,128)(2,1)S(1)} %bitcast.39), custom_call_target="tpu_custom_call" | custom-call | flops 339738624 | bytes 5308416 | tf_op jit(solution)/shard_map/pallas_call | solution.py:219
  32.9 0.5 collective-permute-start.6
  33.4 1.6 %collective-permute-start.7 = (bf16[32,4096]{1,0:T(8,128)(2,1)S(1)}, bf16[32,4096]{1,0:T(8,128)(2,1)S(1)}, u32[]{:S(2)}, u32[]{:S(2)}) collective-permute-start(bf16[32,4096]{1,0:T(8,128)(2,1)S(1)} %get-tuple-element.64), channel_id=1, source_target_pairs={{0,2},{1,3},{2,0},{3,1},{4,6},{5,7},{6,4},{7,5},{8,10},{9,11},{10,... | collective-permute-start | bytes 786440 | tf_op jit(solution)/shard_map/ppermute | solution.py:43
  35.1 3.4 %collective-permute-done.10.refs_6_ = bf16[32,4096]{1,0:T(8,128)(2,1)S(1)} collective-permute-done((bf16[32,4096]{1,0:T(8,128)(2,1)S(1)}, bf16[32,4096]{1,0:T(8,128)(2,1)S(1)}, u32[]{:S(2)}, u32[]{:S(2)}) %collective-permute-start.10) | collective-permute-done | bytes 262176 | tf_op jit(solution)/shard_map/ppermute | solution.py:43
  38.4 4.8 %collective-permute-done.11.refs_7_ = bf16[32,4096]{1,0:T(8,128)(2,1)S(1)} collective-permute-done((bf16[32,4096]{1,0:T(8,128)(2,1)S(1)}, bf16[32,4096]{1,0:T(8,128)(2,1)S(1)}, u32[]{:S(2)}, u32[]{:S(2)}) %collective-permute-start.11) | collective-permute-done | bytes 262176 | tf_op jit(solution)/shard_map/ppermute | solution.py:43
  43.2 6.5 %collective-permute-done.7.refs_2_ = bf16[32,4096]{1,0:T(8,128)(2,1)S(1)} collective-permute-done((bf16[32,4096]{1,0:T(8,128)(2,1)S(1)}, bf16[32,4096]{1,0:T(8,128)(2,1)S(1)}, u32[]{:S(2)}, u32[]{:S(2)}) %collective-permute-start.7) | collective-permute-done | bytes 262176 | tf_op jit(solution)/shard_map/ppermute | solution.py:43
  49.7 4.5 %collective-permute-done.8.refs_3_ = bf16[32,4096]{1,0:T(8,128)(2,1)S(1)} collective-permute-done((bf16[32,4096]{1,0:T(8,128)(2,1)S(1)}, bf16[32,4096]{1,0:T(8,128)(2,1)S(1)}, u32[]{:S(2)}, u32[]{:S(2)}) %collective-permute-start.8) | collective-permute-done | bytes 262176 | tf_op jit(solution)/shard_map/ppermute | solution.py:43
  54.1 1.5 %shard_map.115 = (bf16[128,4096]{1,0:T(8,128)(2,1)S(1)}, bf16[128,4096]{1,0:T(8,128)(2,1)S(1)}, bf16[32,4096]{1,0:T(8,128)(2,1)S(1)}) custom-call(s32[2]{0:T(128)S(1)} %pad_add_fusion.2.where, bf16[32,4096]{1,0:T(8,128)(2,1)S(1)} %get-tuple-element.57.held, s32[128,32]{1,0:T(8,128)S(1)} %bitcast.41, f32[32,4096]{1,0:T(8,128)S(1)} %fusion.5.factor, ...), custom_call_target="tpu_custom_call" | custom-call | flops 336592896 | bytes 5259264 | tf_op jit(solution)/shard_map/pallas_call | solution.py:219
  55.7 3.3 %collective-permute-start.12 = (bf16[32,4096]{1,0:T(8,128)(2,1)S(1)}, bf16[32,4096]{1,0:T(8,128)(2,1)S(1)}, u32[]{:S(2)}, u32[]{:S(2)}) collective-permute-start(bf16[32,4096]{1,0:T(8,128)(2,1)S(1)} %get-tuple-element.70), channel_id=1, source_target_pairs={{0,4},{1,5},{2,6},{3,7},{16,20},{17,21},{18,22},{19,23}} | collective-permute-start | bytes 786440 | tf_op jit(solution)/shard_map/ppermute | solution.py:328
  59.0 6.1 %collective-permute-done.12.came = bf16[32,4096]{1,0:T(8,128)(2,1)S(1)} collective-permute-done((bf16[32,4096]{1,0:T(8,128)(2,1)S(1)}, bf16[32,4096]{1,0:T(8,128)(2,1)S(1)}, u32[]{:S(2)}, u32[]{:S(2)}) %collective-permute-start.12) | collective-permute-done | bytes 262176 | tf_op jit(solution)/shard_map/ppermute | solution.py:328
  65.1 1.5 %shard_map.116 = (bf16[32,4096]{1,0:T(8,128)(2,1)S(1)}, bf16[32,4096]{1,0:T(8,128)(2,1)S(1)}) custom-call(s32[2]{0:T(128)S(1)} %pad_add_fusion.2.where, bf16[32,4096]{1,0:T(8,128)(2,1)S(1)} %collective-permute-done.12.came, bf16[32,4096]{1,0:T(8,128)(2,1)S(1)} %get-tuple-element.57.held, s32[128,32]{1,0:T(8,128)S(1)} %bitcast.42, ...), custom_call_target="tpu_custom_call" | custom-call | flops 235929600 | bytes 3686400 | tf_op jit(solution)/shard_map/pallas_call | solution.py:219
  66.6 0.7 collective-permute-start.13
  67.3 1.5 %shard_map.117 = (bf16[32,4096]{1,0:T(8,128)(2,1)S(1)}, bf16[32,4096]{1,0:T(8,128)(2,1)S(1)}) custom-call(s32[2]{0:T(128)S(1)} %pad_add_fusion.2.where, bf16[32,4096]{1,0:T(8,128)(2,1)S(1)} %collective-permute-done.13.came, bf16[32,4096]{1,0:T(8,128)(2,1)S(1)} %get-tuple-element.74.held, s32[128,32]{1,0:T(8,128)S(1)} %bitcast.43, ...), custom_call_target="tpu_custom_call" | custom-call | flops 235929600 | bytes 3686400 | tf_op jit(solution)/shard_map/pallas_call | solution.py:219
  68.8 0.7 collective-permute-start.14
  69.5 1.6 %shard_map.118 = (bf16[32,4096]{1,0:T(8,128)(2,1)S(1)}, f32[128,32]{1,0:T(8,128)S(1)}, bf16[32,4096]{1,0:T(8,128)(2,1)S(1)}) custom-call(s32[2]{0:T(128)S(1)} %pad_add_fusion.2.where, bf16[32,4096]{1,0:T(8,128)(2,1)S(1)} %collective-permute-done.14.came, bf16[32,4096]{1,0:T(8,128)(2,1)S(1)} %get-tuple-element.76.held, s32[128,32]{1,0:T(8,128)S(1)} %bitcast.44, ...), custom_call_target="tpu_custom_call" | custom-call | flops 253755392 | bytes 3964928 | tf_op jit(solution)/shard_map/pallas_call | solution.py:219
  71.1 0.7 collective-permute-start.15
  71.8 1.6 %collective-permute-start.22 = (bf16[32,4096]{1,0:T(8,128)(2,1)S(1)}, bf16[32,4096]{1,0:T(8,128)(2,1)S(1)}, u32[]{:S(2)}, u32[]{:S(2)}) collective-permute-start(bf16[32,4096]{1,0:T(8,128)(2,1)S(1)} %get-tuple-element.101.current.refs_0_), channel_id=1, source_target_pairs={{0,2},{1,3},{2,0},{3,1},{4,6},{5,7},{6,4},{7,5},{8,10},{9,11},{10,... | collective-permute-start | bytes 786440 | tf_op jit(solution)/shard_map/ppermute | solution.py:43
  73.4 0.9 shard_map.119
  74.3 1.5 %shard_map.120 = (bf16[32,4096]{1,0:T(8,128)(2,1)S(1)}, bf16[32,4096]{1,0:T(8,128)(2,1)S(1)}) custom-call(s32[2]{0:T(128)S(1)} %pad_add_fusion.2.where, bf16[32,4096]{1,0:T(8,128)(2,1)S(1)} %collective-permute-done.15.came, bf16[32,4096]{1,0:T(8,128)(2,1)S(1)} %get-tuple-element.77.grad.held, f32[128,32]{1,0:T(8,128)S(1)} %get-tuple-element.80.probs, ...), custom_call_target="tpu_custom_call" | custom-call | flops 235929600 | bytes 3686400 | tf_op jit(solution)/shard_map/pallas_call | solution.py:219
  75.8 0.7 collective-permute-start.16
  76.5 0.6 collective-permute-start.18
  77.2 1.3 collective-permute-start.19
  78.4 1.2 collective-permute-done.22.refs_2_
  79.7 0.5 collective-permute-start.23
  80.2 1.3 collective-permute-done.18.refs_2_
  81.5 0.5 collective-permute-done.19.refs_3_
  82.0 1.5 %shard_map.121 = (bf16[32,4096]{1,0:T(8,128)(2,1)S(1)}, bf16[32,4096]{1,0:T(8,128)(2,1)S(1)}) custom-call(s32[2]{0:T(128)S(1)} %pad_add_fusion.2.where, bf16[32,4096]{1,0:T(8,128)(2,1)S(1)} %collective-permute-done.16.came, bf16[32,4096]{1,0:T(8,128)(2,1)S(1)} %get-tuple-element.92.held, f32[128,32]{1,0:T(8,128)S(1)} %get-tuple-element.80.probs, ...), custom_call_target="tpu_custom_call" | custom-call | flops 235929600 | bytes 3686400 | tf_op jit(solution)/shard_map/pallas_call | solution.py:219
  83.5 1.7 %collective-permute-start.20 = (bf16[32,4096]{1,0:T(8,128)(2,1)S(1)}, bf16[32,4096]{1,0:T(8,128)(2,1)S(1)}, u32[]{:S(2)}, u32[]{:S(2)}) collective-permute-start(bf16[32,4096]{1,0:T(8,128)(2,1)S(1)} %get-tuple-element.93), channel_id=1, source_target_pairs={{4,0},{5,1},{6,2},{7,3},{20,16},{21,17},{22,18},{23,19}} | collective-permute-start | bytes 786440 | tf_op jit(solution)/shard_map/ppermute | solution.py:354
  85.3 1.3 shard_map.122
  86.6 24.4 %collective-permute-done.20.came = bf16[32,4096]{1,0:T(8,128)(2,1)S(1)} collective-permute-done((bf16[32,4096]{1,0:T(8,128)(2,1)S(1)}, bf16[32,4096]{1,0:T(8,128)(2,1)S(1)}, u32[]{:S(2)}, u32[]{:S(2)}) %collective-permute-start.20) | collective-permute-done | bytes 262176 | tf_op jit(solution)/shard_map/ppermute | solution.py:354
  110.9 0.6 shard_map.124.refs_0_
  111.5 1.6 %collective-permute-start.25 = (bf16[32,4096]{1,0:T(8,128)(2,1)S(1)}, bf16[32,4096]{1,0:T(8,128)(2,1)S(1)}, u32[]{:S(2)}, u32[]{:S(2)}) collective-permute-start(bf16[32,4096]{1,0:T(8,128)(2,1)S(1)} %shard_map.124.refs_0_), channel_id=1, source_target_pairs={{0,2},{1,3},{2,0},{3,1},{4,6},{5,7},{6,4},{7,5},{8,10},{9,11},{10,... | collective-permute-start | bytes 786440 | tf_op jit(solution)/shard_map/ppermute | solution.py:43
  113.1 4.9 %collective-permute-done.25.refs_2_ = bf16[32,4096]{1,0:T(8,128)(2,1)S(1)} collective-permute-done((bf16[32,4096]{1,0:T(8,128)(2,1)S(1)}, bf16[32,4096]{1,0:T(8,128)(2,1)S(1)}, u32[]{:S(2)}, u32[]{:S(2)}) %collective-permute-start.25) | collective-permute-done | bytes 262176 | tf_op jit(solution)/shard_map/ppermute | solution.py:43
  118.0 1.4 %shard_map.123 = (bf16[128,512]{1,0:T(8,128)(2,1)S(1)}, f32[128,32]{1,0:T(8,128)S(1)}) custom-call(s32[2]{0:T(128)S(1)} %pad_add_fusion.2.where, bf16[64,512]{1,0:T(8,128)(2,1)S(1)} %get-tuple-element.61.keys, bf16[4096,512]{1,0:T(8,128)(2,1)S(1)} %bitcast.40, s32[128,32]{1,0:T(8,128)S(1)} %bitcast.45, ...), custom_call_target="tpu_custom_call" | custom-call | flops 350224384 | bytes 5472256 | tf_op jit(solution)/shard_map/pallas_call | solution.py:219
  119.5 5.2 %shard_map.125 = (f32[32,4096]{1,0:T(8,128)S(1)}, bf16[32,4096]{1,0:T(8,128)(2,1)S(1)}) custom-call(s32[2]{0:T(128)S(1)} %pad_add_fusion.2.where, bf16[64,512]{1,0:T(8,128)(2,1)S(1)} %get-tuple-element.61.keys, bf16[64,512]{1,0:T(8,128)(2,1)S(1)} %get-tuple-element.99.values, bf16[128,512]{1,0:T(8,128)(2,1)S(1)} %get-tuple-element.105.query, ...), custom_call_target="tpu_custom_call" | custom-call | flops 957874176 | bytes 14966784 | tf_op jit(solution)/shard_map/pallas_call | solution.py:219
  124.7 0.5 collective-permute-start.27
  125.2 1.2 collective-permute-done.27
  126.4 1.6 %collective-permute-start.28 = (bf16[16,4096]{1,0:T(8,128)(2,1)S(1)}, bf16[16,4096]{1,0:T(8,128)(2,1)S(1)}, u32[]{:S(2)}, u32[]{:S(2)}) collective-permute-start(bf16[16,4096]{1,0:T(8,128)(2,1)S(1)} %slice.49), channel_id=1, source_target_pairs={{0,2},{1,3},{2,0},{3,1},{4,6},{5,7},{6,4},{7,5},{8,10},{9,11},{10,... | collective-permute-start | bytes 393224 | tf_op jit(solution)/shard_map/ppermute | solution.py:43
  128.0 4.3 %collective-permute-done.28 = bf16[16,4096]{1,0:T(8,128)(2,1)S(1)} collective-permute-done((bf16[16,4096]{1,0:T(8,128)(2,1)S(1)}, bf16[16,4096]{1,0:T(8,128)(2,1)S(1)}, u32[]{:S(2)}, u32[]{:S(2)}) %collective-permute-start.28) | collective-permute-done | bytes 131104 | tf_op jit(solution)/shard_map/ppermute | solution.py:43
  132.5 0.6 collective-permute-start.31
  133.1 2.8 %collective-permute-start.30 = (bf16[4,4096]{1,0:T(4,128)(2,1)S(1)}, bf16[4,4096]{1,0:T(4,128)(2,1)S(1)}, u32[]{:S(2)}, u32[]{:S(2)}) collective-permute-start(bf16[4,4096]{1,0:T(4,128)(2,1)S(1)} %get-tuple-element.123), channel_id=1, source_target_pairs={{0,8},{4,12},{8,0},{12,4},{1,9},{5,13},{9,1},{13,5},{2,10},{6,14},... | collective-permute-start | bytes 98312 | tf_op jit(solution)/shard_map/ppermute | solution.py:43
  135.9 1.1 collective-permute-done.29
  137.1 1.3 collective-permute-done.31
  138.3 0.5 collective-permute-done.30
  138.9 0.7 fusion.8
  (60 shorter events, 1.2 us)
Async XLA Ops:
  0.6 11.5 %collective-permute-start.2 = (bf16[4,4096]{1,0:T(4,128)(2,1)}, bf16[4,4096]{1,0:T(4,128)(2,1)S(1)}, u32[]{:S(2)}, u32[]{:S(2)}) collective-permute-start(bf16[4,4096]{1,0:T(4,128)(2,1)} %bitcast.47), channel_id=1, source_target_pairs={{0,12},{4,8},{8,4},{12,0},{1,13},{5,9},{9,5},{13,1},{2,14},{6,10},... | collective-permute-start | bytes 98312 | tf_op jit(solution)/shard_map/ppermute | solution.py:43
  5.7 6.4 %collective-permute-start.1 = (bf16[4,4096]{1,0:T(4,128)(2,1)}, bf16[4,4096]{1,0:T(4,128)(2,1)S(1)}, u32[]{:S(2)}, u32[]{:S(2)}) collective-permute-start(bf16[4,4096]{1,0:T(4,128)(2,1)} %bitcast.48), channel_id=1, source_target_pairs={{0,8},{4,12},{8,0},{12,4},{1,9},{5,13},{9,1},{13,5},{2,10},{6,14},... | collective-permute-start | bytes 98312 | tf_op jit(solution)/shard_map/ppermute | solution.py:43
  5.7 6.4 %collective-permute-start = (bf16[4,4096]{1,0:T(4,128)(2,1)}, bf16[4,4096]{1,0:T(4,128)(2,1)S(1)}, u32[]{:S(2)}, u32[]{:S(2)}) collective-permute-start(bf16[4,4096]{1,0:T(4,128)(2,1)} %bitcast.49), channel_id=1, source_target_pairs={{0,4},{4,0},{8,12},{12,8},{1,5},{5,1},{9,13},{13,9},{2,6},{6,2},{1... | collective-permute-start | bytes 98312 | tf_op jit(solution)/shard_map/ppermute | solution.py:43
  13.0 5.0 %collective-permute-start.4 = (bf16[16,4096]{1,0:T(8,128)(2,1)S(1)}, bf16[16,4096]{1,0:T(8,128)(2,1)S(1)}, u32[]{:S(2)}, u32[]{:S(2)}) collective-permute-start(bf16[16,4096]{1,0:T(8,128)(2,1)S(1)} %pad_maximum_fusion.refs_0_), channel_id=1, source_target_pairs={{0,2},{1,3},{2,0},{3,1},{4,6},{5,7},{6,4},{7,5},{8,10},{9,11},{10,... | collective-permute-start | bytes 393224 | tf_op jit(solution)/shard_map/ppermute | solution.py:43
  14.8 3.4 %collective-permute-start.3 = (bf16[16,4096]{1,0:T(8,128)(2,1)S(1)}, bf16[16,4096]{1,0:T(8,128)(2,1)S(1)}, u32[]{:S(2)}, u32[]{:S(2)}) collective-permute-start(bf16[16,4096]{1,0:T(8,128)(2,1)S(1)} %pad_maximum_fusion.refs_0_), channel_id=1, source_target_pairs={{0,1},{1,0},{2,3},{3,2},{4,5},{5,4},{6,7},{7,6},{8,9},{9,8},{10,11... | collective-permute-start | bytes 393224 | tf_op jit(solution)/shard_map/ppermute | solution.py:43
  18.0 1.3 collective-permute-start.5
  19.4 2.2 %copy-start = (bf16[1,4096,512]{2,1,0:T(8,128)(2,1)S(1)}, bf16[1,4096,512]{2,1,0:T(8,128)(2,1)}, u32[]{:S(2)}) copy-start(bf16[1,4096,512]{2,1,0:T(8,128)(2,1)} %param.17) | copy-start | bytes 12582916
  21.6 2.2 %copy-start.2 = (bf16[1,4096,512]{2,1,0:T(8,128)(2,1)S(1)}, bf16[1,4096,512]{2,1,0:T(8,128)(2,1)}, u32[]{:S(2)}) copy-start(bf16[1,4096,512]{2,1,0:T(8,128)(2,1)} %param.18) | copy-start | bytes 12582916
  23.8 2.2 %copy-start.4 = (bf16[1,512,4096]{2,1,0:T(8,128)(2,1)S(1)}, bf16[1,512,4096]{2,1,0:T(8,128)(2,1)}, u32[]{:S(2)}) copy-start(bf16[1,512,4096]{2,1,0:T(8,128)(2,1)} %param.19) | copy-start | bytes 12582916
  26.0 5.0 %copy-start.6 = (bf16[1,4096,512]{2,1,0:T(8,128)(2,1)S(1)}, bf16[1,4096,512]{2,1,0:T(8,128)(2,1)}, u32[]{:S(2)}) copy-start(bf16[1,4096,512]{2,1,0:T(8,128)(2,1)} %param.16) | copy-start | bytes 12582916
  29.1 6.0 %collective-permute-start.9 = (bf16[32,4096]{1,0:T(8,128)(2,1)S(1)}, bf16[32,4096]{1,0:T(8,128)(2,1)S(1)}, u32[]{:S(2)}, u32[]{:S(2)}) collective-permute-start(bf16[32,4096]{1,0:T(8,128)(2,1)S(1)} %get-tuple-element.67), channel_id=1, source_target_pairs={{0,1},{1,0},{2,3},{3,2},{4,5},{5,4},{6,7},{7,6},{8,9},{9,8},{10,11... | collective-permute-start | bytes 786440 | tf_op jit(solution)/shard_map/ppermute | solution.py:43
  29.3 9.1 %collective-permute-start.10 = (bf16[32,4096]{1,0:T(8,128)(2,1)S(1)}, bf16[32,4096]{1,0:T(8,128)(2,1)S(1)}, u32[]{:S(2)}, u32[]{:S(2)}) collective-permute-start(bf16[32,4096]{1,0:T(8,128)(2,1)S(1)} %get-tuple-element.68), channel_id=1, source_target_pairs={{0,2},{1,3},{2,0},{3,1},{4,6},{5,7},{6,4},{7,5},{8,10},{9,11},{10,... | collective-permute-start | bytes 786440 | tf_op jit(solution)/shard_map/ppermute | solution.py:43
  30.9 12.3 %collective-permute-start.11 = (bf16[32,4096]{1,0:T(8,128)(2,1)S(1)}, bf16[32,4096]{1,0:T(8,128)(2,1)S(1)}, u32[]{:S(2)}, u32[]{:S(2)}) collective-permute-start(bf16[32,4096]{1,0:T(8,128)(2,1)S(1)} %get-tuple-element.69), channel_id=1, source_target_pairs={{0,3},{1,2},{2,1},{3,0},{4,7},{5,6},{6,5},{7,4},{8,11},{9,10},{10,... | collective-permute-start | bytes 786440 | tf_op jit(solution)/shard_map/ppermute | solution.py:43
  32.9 10.3 %collective-permute-start.6 = (bf16[32,4096]{1,0:T(8,128)(2,1)S(1)}, bf16[32,4096]{1,0:T(8,128)(2,1)S(1)}, u32[]{:S(2)}, u32[]{:S(2)}) collective-permute-start(bf16[32,4096]{1,0:T(8,128)(2,1)S(1)} %get-tuple-element.63), channel_id=1, source_target_pairs={{0,1},{1,0},{2,3},{3,2},{4,5},{5,4},{6,7},{7,6},{8,9},{9,8},{10,11... | collective-permute-start | bytes 786440 | tf_op jit(solution)/shard_map/ppermute | solution.py:43
  33.4 16.2 %collective-permute-start.7 = (bf16[32,4096]{1,0:T(8,128)(2,1)S(1)}, bf16[32,4096]{1,0:T(8,128)(2,1)S(1)}, u32[]{:S(2)}, u32[]{:S(2)}) collective-permute-start(bf16[32,4096]{1,0:T(8,128)(2,1)S(1)} %get-tuple-element.64), channel_id=1, source_target_pairs={{0,2},{1,3},{2,0},{3,1},{4,6},{5,7},{6,4},{7,5},{8,10},{9,11},{10,... | collective-permute-start | bytes 786440 | tf_op jit(solution)/shard_map/ppermute | solution.py:43
  35.1 19.1 %collective-permute-start.8 = (bf16[32,4096]{1,0:T(8,128)(2,1)S(1)}, bf16[32,4096]{1,0:T(8,128)(2,1)S(1)}, u32[]{:S(2)}, u32[]{:S(2)}) collective-permute-start(bf16[32,4096]{1,0:T(8,128)(2,1)S(1)} %get-tuple-element.65), channel_id=1, source_target_pairs={{0,3},{1,2},{2,1},{3,0},{4,7},{5,6},{6,5},{7,4},{8,11},{9,10},{10,... | collective-permute-start | bytes 786440 | tf_op jit(solution)/shard_map/ppermute | solution.py:43
  55.7 9.4 %collective-permute-start.12 = (bf16[32,4096]{1,0:T(8,128)(2,1)S(1)}, bf16[32,4096]{1,0:T(8,128)(2,1)S(1)}, u32[]{:S(2)}, u32[]{:S(2)}) collective-permute-start(bf16[32,4096]{1,0:T(8,128)(2,1)S(1)} %get-tuple-element.70), channel_id=1, source_target_pairs={{0,4},{1,5},{2,6},{3,7},{16,20},{17,21},{18,22},{19,23}} | collective-permute-start | bytes 786440 | tf_op jit(solution)/shard_map/ppermute | solution.py:328
  66.6 0.7 collective-permute-start.13
  68.8 0.7 collective-permute-start.14
  71.1 3.1 %collective-permute-start.15 = (bf16[32,4096]{1,0:T(8,128)(2,1)S(1)}, bf16[32,4096]{1,0:T(8,128)(2,1)S(1)}, u32[]{:S(2)}, u32[]{:S(2)}) collective-permute-start(bf16[32,4096]{1,0:T(8,128)(2,1)S(1)} %get-tuple-element.78), channel_id=1, source_target_pairs={{12,8},{13,9},{14,10},{15,11},{28,24},{29,25},{30,26},{31,27}} | collective-permute-start | bytes 786440 | tf_op jit(solution)/shard_map/ppermute | solution.py:354
  71.8 7.8 %collective-permute-start.22 = (bf16[32,4096]{1,0:T(8,128)(2,1)S(1)}, bf16[32,4096]{1,0:T(8,128)(2,1)S(1)}, u32[]{:S(2)}, u32[]{:S(2)}) collective-permute-start(bf16[32,4096]{1,0:T(8,128)(2,1)S(1)} %get-tuple-element.101.current.refs_0_), channel_id=1, source_target_pairs={{0,2},{1,3},{2,0},{3,1},{4,6},{5,7},{6,4},{7,5},{8,10},{9,11},{10,... | collective-permute-start | bytes 786440 | tf_op jit(solution)/shard_map/ppermute | solution.py:43
  74.2 45.3 %copy-start.5 = (bf16[1,512,4096]{2,1,0:T(8,128)(2,1)S(1)}, bf16[1,512,4096]{2,1,0:T(8,128)(2,1)}, u32[]{:S(2)}) copy-start(bf16[1,512,4096]{2,1,0:T(8,128)(2,1)} %param.19) | copy-start | bytes 12582916
  75.8 6.2 %collective-permute-start.16 = (bf16[32,4096]{1,0:T(8,128)(2,1)S(1)}, bf16[32,4096]{1,0:T(8,128)(2,1)S(1)}, u32[]{:S(2)}, u32[]{:S(2)}) collective-permute-start(bf16[32,4096]{1,0:T(8,128)(2,1)S(1)} %get-tuple-element.86), channel_id=1, source_target_pairs={{8,4},{9,5},{10,6},{11,7},{24,20},{25,21},{26,22},{27,23}} | collective-permute-start | bytes 786440 | tf_op jit(solution)/shard_map/ppermute | solution.py:354
  76.5 3.2 %collective-permute-start.17 = (bf16[32,1024]{1,0:T(8,128)(2,1)S(1)}, bf16[32,1024]{1,0:T(8,128)(2,1)S(1)}, u32[]{:S(2)}, u32[]{:S(2)}) collective-permute-start(bf16[32,1024]{1,0:T(8,128)(2,1)S(1)} %get-tuple-element.88), channel_id=1, source_target_pairs={{0,1},{1,0},{2,3},{3,2},{4,5},{5,4},{6,7},{7,6},{8,9},{9,8},{10,11... | collective-permute-start | bytes 196616 | tf_op jit(solution)/shard_map/ppermute | solution.py:43
  76.5 5.0 %collective-permute-start.18 = (bf16[32,1024]{1,0:T(8,128)(2,1)S(1)}, bf16[32,1024]{1,0:T(8,128)(2,1)S(1)}, u32[]{:S(2)}, u32[]{:S(2)}) collective-permute-start(bf16[32,1024]{1,0:T(8,128)(2,1)S(1)} %get-tuple-element.89), channel_id=1, source_target_pairs={{0,2},{1,3},{2,0},{3,1},{4,6},{5,7},{6,4},{7,5},{8,10},{9,11},{10,... | collective-permute-start | bytes 196616 | tf_op jit(solution)/shard_map/ppermute | solution.py:43
  77.2 4.9 %collective-permute-start.19 = (bf16[32,1024]{1,0:T(8,128)(2,1)S(1)}, bf16[32,1024]{1,0:T(8,128)(2,1)S(1)}, u32[]{:S(2)}, u32[]{:S(2)}) collective-permute-start(bf16[32,1024]{1,0:T(8,128)(2,1)S(1)} %get-tuple-element.90), channel_id=1, source_target_pairs={{0,3},{1,2},{2,1},{3,0},{4,7},{5,6},{6,5},{7,4},{8,11},{9,10},{10,... | collective-permute-start | bytes 196616 | tf_op jit(solution)/shard_map/ppermute | solution.py:43
  79.6 6.9 %collective-permute-start.21 = (bf16[32,4096]{1,0:T(8,128)(2,1)S(1)}, bf16[32,4096]{1,0:T(8,128)(2,1)S(1)}, u32[]{:S(2)}, u32[]{:S(2)}) collective-permute-start(bf16[32,4096]{1,0:T(8,128)(2,1)S(1)} %get-tuple-element.101.current.refs_0_), channel_id=1, source_target_pairs={{0,1},{1,0},{2,3},{3,2},{4,5},{5,4},{6,7},{7,6},{8,9},{9,8},{10,11... | collective-permute-start | bytes 786440 | tf_op jit(solution)/shard_map/ppermute | solution.py:43
  79.7 6.9 %collective-permute-start.23 = (bf16[32,4096]{1,0:T(8,128)(2,1)S(1)}, bf16[32,4096]{1,0:T(8,128)(2,1)S(1)}, u32[]{:S(2)}, u32[]{:S(2)}) collective-permute-start(bf16[32,4096]{1,0:T(8,128)(2,1)S(1)} %collective-permute-done.22.refs_2_), channel_id=1, source_target_pairs={{0,1},{1,0},{2,3},{3,2},{4,5},{5,4},{6,7},{7,6},{8,9},{9,8},{10,11... | collective-permute-start | bytes 786440 | tf_op jit(solution)/shard_map/ppermute | solution.py:43
  82.0 37.5 %copy-start.3 = (bf16[1,4096,512]{2,1,0:T(8,128)(2,1)S(1)}, bf16[1,4096,512]{2,1,0:T(8,128)(2,1)}, u32[]{:S(2)}) copy-start(bf16[1,4096,512]{2,1,0:T(8,128)(2,1)} %param.18) | copy-start | bytes 12582916
  83.5 36.0 %copy-start.1 = (bf16[1,4096,512]{2,1,0:T(8,128)(2,1)S(1)}, bf16[1,4096,512]{2,1,0:T(8,128)(2,1)}, u32[]{:S(2)}) copy-start(bf16[1,4096,512]{2,1,0:T(8,128)(2,1)} %param.17) | copy-start | bytes 12582916
  83.5 27.4 %collective-permute-start.20 = (bf16[32,4096]{1,0:T(8,128)(2,1)S(1)}, bf16[32,4096]{1,0:T(8,128)(2,1)S(1)}, u32[]{:S(2)}, u32[]{:S(2)}) collective-permute-start(bf16[32,4096]{1,0:T(8,128)(2,1)S(1)} %get-tuple-element.93), channel_id=1, source_target_pairs={{4,0},{5,1},{6,2},{7,3},{20,16},{21,17},{22,18},{23,19}} | collective-permute-start | bytes 786440 | tf_op jit(solution)/shard_map/ppermute | solution.py:354
  111.5 6.4 %collective-permute-start.25 = (bf16[32,4096]{1,0:T(8,128)(2,1)S(1)}, bf16[32,4096]{1,0:T(8,128)(2,1)S(1)}, u32[]{:S(2)}, u32[]{:S(2)}) collective-permute-start(bf16[32,4096]{1,0:T(8,128)(2,1)S(1)} %shard_map.124.refs_0_), channel_id=1, source_target_pairs={{0,2},{1,3},{2,0},{3,1},{4,6},{5,7},{6,4},{7,5},{8,10},{9,11},{10,... | collective-permute-start | bytes 786440 | tf_op jit(solution)/shard_map/ppermute | solution.py:43
  113.1 6.3 %collective-permute-start.24 = (bf16[32,4096]{1,0:T(8,128)(2,1)S(1)}, bf16[32,4096]{1,0:T(8,128)(2,1)S(1)}, u32[]{:S(2)}, u32[]{:S(2)}) collective-permute-start(bf16[32,4096]{1,0:T(8,128)(2,1)S(1)} %shard_map.124.refs_0_), channel_id=1, source_target_pairs={{0,1},{1,0},{2,3},{3,2},{4,5},{5,4},{6,7},{7,6},{8,9},{9,8},{10,11... | collective-permute-start | bytes 786440 | tf_op jit(solution)/shard_map/ppermute | solution.py:43
  118.0 1.5 %collective-permute-start.26 = (bf16[32,4096]{1,0:T(8,128)(2,1)S(1)}, bf16[32,4096]{1,0:T(8,128)(2,1)S(1)}, u32[]{:S(2)}, u32[]{:S(2)}) collective-permute-start(bf16[32,4096]{1,0:T(8,128)(2,1)S(1)} %collective-permute-done.25.refs_2_), channel_id=1, source_target_pairs={{0,1},{1,0},{2,3},{3,2},{4,5},{5,4},{6,7},{7,6},{8,9},{9,8},{10,11... | collective-permute-start | bytes 786440 | tf_op jit(solution)/shard_map/ppermute | solution.py:43
  124.7 1.7 %collective-permute-start.27 = (bf16[32,4096]{1,0:T(8,128)(2,1)S(1)}, bf16[32,4096]{1,0:T(8,128)(2,1)S(1)}, u32[]{:S(2)}, u32[]{:S(2)}) collective-permute-start(bf16[32,4096]{1,0:T(8,128)(2,1)S(1)} %get-tuple-element.111), channel_id=1, source_target_pairs={{0,1},{1,0},{2,3},{3,2},{4,5},{5,4},{6,7},{7,6},{8,9},{9,8},{10,11... | collective-permute-start | bytes 786440 | tf_op jit(solution)/shard_map/ppermute | solution.py:43
  126.4 5.8 %collective-permute-start.28 = (bf16[16,4096]{1,0:T(8,128)(2,1)S(1)}, bf16[16,4096]{1,0:T(8,128)(2,1)S(1)}, u32[]{:S(2)}, u32[]{:S(2)}) collective-permute-start(bf16[16,4096]{1,0:T(8,128)(2,1)S(1)} %slice.49), channel_id=1, source_target_pairs={{0,2},{1,3},{2,0},{3,1},{4,6},{5,7},{6,4},{7,5},{8,10},{9,11},{10,... | collective-permute-start | bytes 393224 | tf_op jit(solution)/shard_map/ppermute | solution.py:43
  132.4 4.7 %collective-permute-start.29 = (bf16[4,4096]{1,0:T(4,128)(2,1)S(1)}, bf16[4,4096]{1,0:T(4,128)(2,1)S(1)}, u32[]{:S(2)}, u32[]{:S(2)}) collective-permute-start(bf16[4,4096]{1,0:T(4,128)(2,1)S(1)} %get-tuple-element.121), channel_id=1, source_target_pairs={{0,4},{4,0},{8,12},{12,8},{1,5},{5,1},{9,13},{13,9},{2,6},{6,2},{1... | collective-permute-start | bytes 98312 | tf_op jit(solution)/shard_map/ppermute | solution.py:43
  132.5 5.9 %collective-permute-start.31 = (bf16[4,4096]{1,0:T(4,128)(2,1)S(1)}, bf16[4,4096]{1,0:T(4,128)(2,1)S(1)}, u32[]{:S(2)}, u32[]{:S(2)}) collective-permute-start(bf16[4,4096]{1,0:T(4,128)(2,1)S(1)} %get-tuple-element.122), channel_id=1, source_target_pairs={{0,12},{4,8},{8,4},{12,0},{1,13},{5,9},{9,5},{13,1},{2,14},{6,10},... | collective-permute-start | bytes 98312 | tf_op jit(solution)/shard_map/ppermute | solution.py:43
  133.1 5.8 %collective-permute-start.30 = (bf16[4,4096]{1,0:T(4,128)(2,1)S(1)}, bf16[4,4096]{1,0:T(4,128)(2,1)S(1)}, u32[]{:S(2)}, u32[]{:S(2)}) collective-permute-start(bf16[4,4096]{1,0:T(4,128)(2,1)S(1)} %get-tuple-element.123), channel_id=1, source_target_pairs={{0,8},{4,12},{8,0},{12,4},{1,9},{5,13},{9,1},{13,5},{2,10},{6,14},... | collective-permute-start | bytes 98312 | tf_op jit(solution)/shard_map/ppermute | solution.py:43

commit v4 on v3

v4 whole, which is shorter than its diff:
```python
import functools
import math

import jax
import jax.numpy as jnp
from jax import lax
from jax.experimental import pallas as pl
from jax.experimental.pallas import tpu as pltpu
from jax.sharding import PartitionSpec as P

HD = 256
NEG_FILL = -1e30
KEEP_SCALE = 8.0 / 7.0
BF = jnp.bfloat16
F32 = jnp.float32
MEBI = 1024 * 1024
BESIDE_THE_GATHER = 32 * MEBI
NN = (((1,), (0,)), ((), ()))
NT = (((1,), (1,)), ((), ()))
SCALE = 1.0 / math.sqrt(HD)


def shifted_right(source_bits, amount):
    return lax.shift_right_logical(source_bits, jnp.full(source_bits.shape, amount, jnp.int32))


def keep_factor(seed_value, first_row, first_col, shape, col_count):
    rows = first_row + lax.broadcasted_iota(jnp.int32, shape, 0)
    position = rows * col_count + first_col + lax.broadcasted_iota(jnp.int32, shape, 1)
    hashed = position ^ seed_value * 1640531527
    hashed = hashed ^ shifted_right(hashed, 16)
    hashed = hashed * 2146121005
    hashed = hashed ^ shifted_right(hashed, 15)
    hashed = hashed * 1911520717
    hashed = hashed ^ shifted_right(hashed, 16)
    is_kept = shifted_right(hashed, 8) & 7 != 0
    return jnp.where(is_kept, KEEP_SCALE, 0.0).astype(F32)


def prepare_kernel(share, seeds, inputs, cotangent, factor, *refs):
    targets, sems = refs[:-1], refs[-1]
    rows, dim = factor.shape
    chunks = len(targets) // 2
    size = rows // chunks
    owner = lax.axis_index("mp")
    micro = lax.div(owner, share)
    first = pl.multiple_of(lax.rem(owner, share) * rows, rows)
    copies = []
    for k, target in enumerate(targets):
        source = inputs if k < chunks else cotangent
        tokens = pl.ds(first + k % chunks * size, size)
        copies.append(pltpu.make_async_copy(source.at[micro, tokens], target, sems.at[k]))
    for copy in copies:
        copy.start()
    width = min(dim, 512)
    for first_col in range(0, dim, width):
        cols = slice(first_col, first_col + width)
        factor[:, cols] = keep_factor(seeds[micro, 0], first, first_col, (rows, width), dim)
    for copy in copies:
        copy.wait()


def swap(array, axis, k):
    size = lax.axis_size(axis)
    return lax.ppermute(array, axis, [(i, i ^ k) for i in range(size)])


def even_mp(array):
    return [array] + [swap(array, "mp", k) for k in range(2, lax.axis_size("mp"), 2)]


def with_odd_mp(evens):
    pieces = []
    for even in evens:
        pieces += [even, swap(even, "mp", 1)]
    return pieces


def over_mp(array):
    return with_odd_mp(even_mp(array))


def product(left, right, dims):
    return lax.dot_general(left, right, dims, preferred_element_type=F32)


def softmax_down(scores, allowed, src):
    shape = scores.shape
    scores = jnp.where(allowed != 0, scores * SCALE, NEG_FILL).reshape(-1, src, shape[1])
    exp_terms = jnp.exp(scores - jnp.max(scores, axis=1, keepdims=True))
    return (exp_terms / jnp.sum(exp_terms, axis=1, keepdims=True)).reshape(shape)


def softmax_back(probs, d_probs, src):
    shape = probs.shape
    probs = probs.reshape(-1, src, shape[1])
    d_probs = d_probs.reshape(probs.shape)
    inner = jnp.sum(probs * d_probs, axis=1, keepdims=True)
    return (probs * (d_probs - inner) * SCALE).reshape(shape)


def spread(weights, fold):
    return product(jnp.transpose(weights).astype(BF), fold[...], NN)


def picked(step, came, held):
    return jnp.where(lax.axis_index("section") == step, came[...], held[...])


def store_folds(part, h, src, cols, folds):
    for k, fold in enumerate(folds):
        fold[h * src : (h + 1) * src, cols] = part[k * src : (k + 1) * src]


def columns(dim):
    width = min(dim, 1024)
    return [slice(first, first + width) for first in range(0, dim, width)]


def values_kernel(n, src, heads, by_owner, wv, wo, *refs):
    pieces, (values, *folds) = refs[:n], refs[n:]
    rows = jnp.concatenate([piece[...] for piece in pieces], axis=0)
    flat = product(rows, wv[...], NN).astype(BF)
    values[...] = product(by_owner[...], flat, NN).astype(BF)
    for h in range(heads):
        head = slice(h * HD, (h + 1) * HD)
        for cols in columns(wo.shape[1]):
            part = product(values[:, head], wo[head, cols], NN).astype(BF)
            store_folds(part, h, src, cols, folds)


def keys_kernel(n, src, heads, share, by_owner, allowed, inputs, wk, wq, *refs):
    pieces, (keys, *outs) = refs[:n], refs[n : 3 * n + 1]
    folds, probs = outs[:n], outs[n:]
    query = refs[3 * n + 1]
    rows = jnp.concatenate([piece[...] for piece in pieces], axis=0)
    flat = product(rows, wk[...], NN).astype(BF)
    keys[...] = product(by_owner[...], flat, NN).astype(BF)
    me = lax.axis_index("mp")
    count = allowed.shape[1]
    tokens = []
    for j in range(n):
        owner = me ^ j
        first = pl.multiple_of(lax.rem(owner, share) * count, count)
        tokens.append(inputs[lax.div(owner, share), pl.ds(first, count)])
    query[...] = product(jnp.concatenate(tokens, axis=0), wq[...], NN).astype(BF)
    for tile, toks, srcs, cols in heads_of(n, heads, count, src):
        k, h = divmod(tile.start // src, heads)
        own = softmax_down(product(keys[srcs, cols], query[toks, cols], NT), allowed[tile], src)
        probs[k][h * src : (h + 1) * src] = own.astype(BF)
    for h in range(heads):
        head = slice(h * HD, (h + 1) * HD)
        for cols in columns(wq.shape[0]):
            part = product(keys[:, head], wq[cols, head], NT).astype(BF)
            store_folds(part, h, src, cols, folds)


def part_of(array, c, size):
    return array[c * size : (c + 1) * size]


def forward(tokens, allowed, factor, query_fold, out_fold, src):
    probs = softmax_down(product(query_fold[...], tokens, NT), allowed[...], src)
    return (tokens.astype(F32) + factor * spread(probs, out_fold)).astype(BF)


def pack(blocks, fold):
    size = blocks[0].shape[0]
    for k, block in enumerate(blocks):
        fold[k * size : (k + 1) * size] = block[...]


def first_kernel(n, chunks, factor, *refs):
    helds, probs, refs = refs[:chunks], refs[chunks : n + chunks], refs[n + chunks :]
    blocks, (out_fold, *following) = refs[:n], refs[n:]
    pack(blocks, out_fold)
    weights = jnp.concatenate([block[...] for block in probs], axis=0).astype(F32)
    kept = factor[...] * spread(weights, out_fold)
    size = kept.shape[0] // chunks
    for c in range(chunks):
        total = helds[c][...].astype(F32) + kept[c * size : (c + 1) * size]
        following[c][...] = total.astype(BF)


def pack_kernel(n, *refs):
    pack(refs[:n], refs[n])


def forward_kernel(
    step, c, src, came, held, allowed, factor, query_fold, out_fold, current, following
):
    tokens = picked(step, came, held)
    current[...] = tokens
    factor = part_of(factor, c, tokens.shape[0])
    following[...] = forward(tokens, allowed, factor, query_fold, out_fold, src)


def backward(probs, grad, factor, query_fold, out_fold, src):
    d_out = (grad.astype(F32) * factor).astype(BF)
    d_scores = softmax_back(probs, product(out_fold[...], d_out, NT), src)
    return (grad.astype(F32) + spread(d_scores, query_fold)).astype(BF)


def turn_kernel(
    step, c, src, came, held, allowed, factor, query_fold, out_fold, grad, current, kept, before
):
    tokens = picked(step, came, held)
    current[...] = tokens
    probs = softmax_down(product(query_fold[...], tokens, NT), allowed[...], src)
    kept[...] = probs
    factor = part_of(factor, c, tokens.shape[0])
    before[...] = backward(probs, grad[...], factor, query_fold, out_fold, src)


def backward_kernel(
    step, c, src, came, held, probs, factor, query_fold, out_fold, current, before
):
    grad = picked(step, came, held)
    current[...] = grad
    factor = part_of(factor, c, grad.shape[0])
    before[...] = backward(probs[...], grad, factor, query_fold, out_fold, src)


def dropped_kernel(step, c, came, held, factor, d_out):
    grad = picked(step, came, held)
    d_out[...] = (grad.astype(F32) * part_of(factor, c, grad.shape[0])).astype(BF)


def outputs_kernel(n, chunks, factor, out_fold, *refs):
    currents, probs, (whole, *parts) = refs[:chunks], refs[chunks : 2 * chunks], refs[2 * chunks :]
    width = parts[0].shape[1]
    size = currents[0].shape[0]
    turned = [jnp.transpose(block[...]).astype(BF) for block in probs]
    turned = jnp.concatenate(turned, axis=0)
    for c in range(chunks):
        whole[c * size : (c + 1) * size] = currents[c][...]
    for j in range(n):
        cols = pl.ds(pl.multiple_of((lax.axis_index("mp") ^ j) * width, width), width)
        summed = product(turned, out_fold[:, cols], NN)
        total = whole[:, cols].astype(F32) + factor[:, cols] * summed
        parts[j][...] = total.astype(BF)


def order_kernel(n, *refs):
    for j in range(n):
        refs[n][lax.axis_index("mp") ^ j] = refs[j][...]


def heads_of(n, heads, rows, src):
    for k in range(n):
        for h in range(heads):
            tile = slice((k * heads + h) * src, (k * heads + h + 1) * src)
            cols = slice(h * HD, (h + 1) * HD)
            yield tile, slice(k * rows, (k + 1) * rows), slice(k * src, (k + 1) * src), cols


def query_kernel(n, src, heads, keys, wq, allowed, *refs):
    pieces, (query, probs) = refs[:n], refs[n:]
    rows = pieces[0].shape[0]
    tokens = jnp.concatenate([piece[...] for piece in pieces], axis=0)
    query[...] = product(tokens, wq[...], NN).astype(BF)
    for tile, toks, srcs, cols in heads_of(n, heads, rows, src):
        scores = product(keys[srcs, cols], query[toks, cols], NT)
        probs[tile] = softmax_down(scores, allowed[tile], src)


def terms_kernel(n, src, heads, keys, values, query, probs, by_micro, wk, wv, wo, *refs):
    pieces, (kept, sent, d_att, d_keys, d_values) = refs[:-5], refs[-5:]
    rows = query.shape[0] // n
    grads = jnp.concatenate([piece[...] for piece in pieces], axis=0)
    d_att[...] = product(grads, wo[...], NT).astype(BF)
    for tile, toks, srcs, cols in heads_of(n, heads, rows, src):
        own = probs[tile]
        d_scores = softmax_back(own, product(values[srcs, cols], d_att[toks, cols], NT), src)
        d_keys[srcs, cols] = product(d_scores.astype(BF), query[toks, cols], NN).astype(BF)
        d_values[srcs, cols] = product(own.astype(BF), d_att[toks, cols], NN).astype(BF)
    key_rows = product(by_micro[...], d_keys[...], NN).astype(BF)
    value_rows = product(by_micro[...], d_values[...], NN).astype(BF)
    size = key_rows.shape[0] // n
    dim = kept.shape[1]
    width = min(dim, 1024)
    for first in range(0, dim, width):
        cols = slice(first, first + width)
        part = product(key_rows, wk[cols], NT) + product(value_rows, wv[cols], NT)
        for k in range(0, n, 2):
            to = slice(k // 2 * size, (k // 2 + 1) * size)
            kept[to, cols] = part[k * size : (k + 1) * size]
            sent[to, cols] = part[(k + 1) * size : (k + 2) * size].astype(BF)


def on_chip(body, outs, *args, scratch=()):
    vmem = pl.BlockSpec(memory_space=pltpu.VMEM)
    outs = [jax.ShapeDtypeStruct(*out) for out in outs]
    size = sum(math.prod(a.shape) * a.dtype.itemsize for a in (*args, *outs, *scratch))
    return pl.pallas_call(
        body,
        out_shape=outs,
        in_specs=[vmem] * len(args),
        out_specs=[vmem] * len(outs),
        scratch_shapes=[pltpu.VMEM(s.shape, s.dtype) for s in scratch],
        compiler_params=pltpu.CompilerParams(vmem_limit_bytes=size + size // 2 + 4 * MEBI),
        cost_estimate=pl.CostEstimate(
            flops=64 * size, bytes_accessed=size, transcendentals=0
        ),
    )(*args)


def per_device(
    memory, decoder_in, cotangent, src_lengths, tgt_segments, seeds, w_query, w_key, w_value, w_out
):
    micro_count, tgt_rows, dim = decoder_in.shape
    local_cols = w_query.shape[2]
    heads = local_cols // HD
    sections = lax.axis_size("section")
    n_mp = lax.axis_size("mp")
    section = lax.axis_index("section")
    me = lax.axis_index("mp")
    share = n_mp // micro_count
    rows = tgt_rows // share
    src = sections * n_mp
    fold_rows = heads * src
    wq, wk, wv, wo = w_query[0], w_key[0], w_value[0], w_out[0]

    chunks = 2 if rows % 32 == 0 else 1
    wide = ((rows // chunks, dim), BF)
    anywhere = pl.BlockSpec(memory_space=pl.ANY)
    vmem = pl.BlockSpec(memory_space=pltpu.VMEM)
    factor, *tokens = pl.pallas_call(
        functools.partial(prepare_kernel, share),
        out_shape=[jax.ShapeDtypeStruct((rows, dim), F32)]
        + [jax.ShapeDtypeStruct(*wide)] * (2 * chunks),
        in_specs=[pl.BlockSpec(memory_space=pltpu.SMEM), anywhere, anywhere],
        out_specs=[vmem] * (1 + 2 * chunks),
        scratch_shapes=[pltpu.SemaphoreType.DMA((2 * chunks,))],
        compiler_params=pltpu.CompilerParams(vmem_limit_bytes=4 * MEBI),
        cost_estimate=pl.CostEstimate(
            flops=0, bytes_accessed=BESIDE_THE_GATHER, transcendentals=0
        ),
    )(seeds, decoder_in, cotangent)

    own = memory.reshape(micro_count, dim)
    over_z = [own if a == 0 else swap(own, "section", a) for a in range(sections)]
    over_z = jnp.concatenate(over_z, axis=0)
    over_z, factor, tokens = lax.optimization_barrier((over_z, factor, tokens))
    helds, grads = list(tokens[:chunks]), list(tokens[chunks:])
    pieces = over_mp(over_z)

    to_row = jnp.arange(n_mp * src, dtype=jnp.int32)[:, None]
    from_row = jnp.arange(src * micro_count, dtype=jnp.int32)[None, :]
    by_owner = (to_row % src == from_row // micro_count) & (
        (me ^ (to_row // src)) // share == from_row % micro_count
    )
    by_owner = by_owner.astype(BF)

    stacked = ((n_mp * src, local_cols), BF)
    block = ((fold_rows, dim), BF)
    whole_fold = ((n_mp * fold_rows, dim), BF)
    def row_ids(device):
        j = jnp.arange(n_mp, dtype=jnp.int32)[:, None]
        a = jnp.arange(sections, dtype=jnp.int32)[None, :]
        return ((section ^ a) * n_mp + (device ^ j)).reshape(src)

    doc_ends = jnp.cumsum(src_lengths, axis=1)

    def allowed_of(owner, heads_owner):
        micro = owner // share
        ends = lax.dynamic_index_in_dim(doc_ends, micro, 0, keepdims=False)
        segments = lax.dynamic_index_in_dim(tgt_segments, micro, 0, keepdims=False)
        segments = lax.dynamic_slice_in_dim(segments, (owner % share) * rows, rows, 0)
        docs = jnp.sum((ends[None, :] <= row_ids(heads_owner)[:, None]).astype(jnp.int32), axis=1)
        return docs[:, None] == segments[None, :]

    def every_head(blocks):
        blocks = jnp.broadcast_to(jnp.stack(blocks)[:, None], (n_mp, heads, src, rows))
        return blocks.astype(jnp.int32).reshape(n_mp * fold_rows, rows)

    own_allowed = every_head([allowed_of(me ^ j, me) for j in range(n_mp)])
    allowed = every_head([allowed_of(me, me ^ k) for k in range(n_mp)])
    size = rows // chunks
    masks = [lax.slice_in_dim(allowed, c * size, (c + 1) * size, axis=1) for c in range(chunks)]
    own_allowed, by_owner, by_micro, masks = lax.optimization_barrier(
        (own_allowed, by_owner, by_owner.T, masks)
    )
    values, *out_blocks = on_chip(
        functools.partial(values_kernel, n_mp, src, heads),
        [stacked] + [block] * n_mp,
        by_owner,
        wv,
        wo,
        *pieces,
    )
    keys, *blocks = on_chip(
        functools.partial(keys_kernel, n_mp, src, heads, share),
        [stacked] + [block] * n_mp + [((fold_rows, rows), BF)] * n_mp,
        by_owner,
        own_allowed,
        decoder_in,
        wk,
        wq,
        *pieces,
        scratch=[jax.ShapeDtypeStruct((n_mp * rows, local_cols), BF)],
    )
    query_blocks, own_probs = blocks[:n_mp], blocks[n_mp:]
    def to_owners(blocks):
        return [part if j == 0 else swap(part, "mp", j) for j, part in enumerate(blocks)]

    out_blocks = to_owners(out_blocks)
    first_probs = to_owners(own_probs)
    query_blocks = to_owners(query_blocks)
    out_fold, *followings = on_chip(
        functools.partial(first_kernel, n_mp, chunks),
        [whole_fold] + [wide] * chunks,
        factor,
        *helds,
        *first_probs,
        *out_blocks,
    )
    (query_fold,) = on_chip(
        functools.partial(pack_kernel, n_mp), [whole_fold], *query_blocks
    )
    folds = (query_fold, out_fold)
    for step in range(1, sections):
        cames = [lax.ppermute(part, "section", [(step - 1, step)]) for part in followings]
        if step < sections - 1:
            for c in range(chunks):
                helds[c], followings[c] = on_chip(
                    functools.partial(forward_kernel, step, c, src),
                    [wide, wide],
                                cames[c],
                    helds[c],
                    masks[c],
                    factor,
                    *folds,
                )
    currents, probs, befores = [], [], []
    for c in range(chunks):
        results = on_chip(
            functools.partial(turn_kernel, sections - 1, c, src),
            [wide, (masks[c].shape, F32), wide],
                cames[c],
            helds[c],
            masks[c],
            factor,
            *folds,
            grads[c],
        )
        for kept, result in zip((currents, probs, befores), results, strict=True):
            kept.append(result)

    out_cols = dim // n_mp
    for step in range(sections - 1, 0, -1):
        cames = [lax.ppermute(part, "section", [(step, step - 1)]) for part in befores]
        if step == 3:
            whole, *parts = on_chip(
                functools.partial(outputs_kernel, n_mp, chunks),
                [((rows, dim), BF)] + [((rows, out_cols), BF)] * n_mp,
                        factor,
                out_fold,
                *currents,
                *probs,
            )
            cames, whole, parts = lax.optimization_barrier((cames, whole, parts))
        if step == 2:
            cames, parts, evens = lax.optimization_barrier(
                (cames, to_owners(parts), even_mp(whole))
            )
        if step == 1:
            (section_out,) = on_chip(
                functools.partial(order_kernel, n_mp),
                [((n_mp, rows, out_cols), BF)],
                        *parts,
            )
            query, own_probs = on_chip(
                functools.partial(query_kernel, n_mp, src, heads),
                [((n_mp * rows, local_cols), BF), (own_allowed.shape, F32)],
                        keys,
                wq,
                own_allowed,
                *with_odd_mp(evens),
            )
            cames, section_out, query, own_probs = lax.optimization_barrier(
                (cames, section_out, query, own_probs)
            )
            break
        for c in range(chunks):
            grads[c], befores[c] = on_chip(
                functools.partial(backward_kernel, step - 1, c, src),
                [wide, wide],
                        cames[c],
                grads[c],
                probs[c],
                factor,
                *folds,
            )
    gathered = []
    for c in range(chunks):
        (d_out,) = on_chip(
            functools.partial(dropped_kernel, 0, c), [wide], cames[c], grads[c], factor
        )
        gathered.append(over_mp(d_out))
    every_d_out = [gathered[c][j] for j in range(n_mp) for c in range(chunks)]
    half_rows = n_mp // 2 * sections * micro_count
    kept, sent = on_chip(
        functools.partial(terms_kernel, n_mp, src, heads),
        [((half_rows, dim), F32), ((half_rows, dim), BF)],
        keys,
        values,
        query,
        own_probs,
        by_micro,
        wk,
        wv,
        wo,
        *every_d_out,
        scratch=[
            jax.ShapeDtypeStruct((n_mp * rows, local_cols), BF),
            jax.ShapeDtypeStruct(*stacked),
            jax.ShapeDtypeStruct(*stacked),
        ],
    )
    half = (kept + swap(sent, "mp", 1).astype(F32)).reshape(n_mp // 2, -1, dim)
    total = half[0]
    for j in range(1, n_mp // 2):
        total = total + swap(half[j].astype(BF), "mp", 2 * j).astype(F32)
    total = total.reshape(sections, micro_count, dim)
    mem_grad = total[0]
    for a in range(1, sections):
        mem_grad = mem_grad + swap(total[a].astype(BF), "section", a).astype(F32)
    return (section_out.reshape(1, micro_count, tgt_rows, out_cols), mem_grad[None])


def solution(mesh):
    return jax.shard_map(
        per_device,
        mesh=mesh,
        in_specs=(
            P(("section", "mp"), "groups", None),
            P("groups", None, None),
            P("groups", None, None),
            P("groups", None),
            P("groups", None),
            P("groups", "section"),
            P("section", None, "mp"),
            P("section", None, "mp"),
            P("section", None, "mp"),
            P("section", "mp", None),
        ),
        out_specs=(P("section", "groups", None, "mp"), P(("section", "mp"), "groups", None)),
        check_vma=False,
    )
```

time: 140 us -> 133 us (0.950)
  waiting for transfers between devices: 70.4 us -> 57.9 us
  starting transfers between devices: 30.5 us -> 38.4 us
  other arithmetic: 5.17 us -> 2.89 us
    ppermute x6 -> x12, waiting for transfers between devices: 30.4 us -> 19.5 us  [the longest x6 19.5 us: per_device(): lax.ppermute(part, 'section', [(step, step - 1)])]
    ppermute x6 -> x12, starting transfers between devices: 7.78 us -> 13 us  [the longest x6 7.26 us: per_device(): lax.ppermute(part, 'section', [(step - 1, step)])]
    ppermute x26 -> x32, starting transfers between devices: 22.7 us -> 25.4 us  [swap(): return lax.ppermute(array, axis, [(i, i ^ k) for i in range(size)])]
    ppermute x26 -> x32, waiting for transfers between devices: 40 us -> 38.4 us  [swap(): return lax.ppermute(array, axis, [(i, i ^ k) for i in range(size)])]
    unnamed x14 -> x19, local copies, waits for them, and re-layouts: 6.58 us -> 7.59 us
    pallas_call x13 -> x21, Pallas kernels: 23.6 us -> 23.2 us  [the longest x20 21.7 us: on_chip(): pl.pallas_call(body, out_shape=outs, in_specs=[vmem] * len(args), out_spe...]
  transfers between devices with their start and end apart: 32 -> 44, of which waited for: 18 -> 17; matrix products, arithmetic and copies ran while one was open for 4% -> 3% of each run, Pallas kernels for 6% -> 13%
where the time goes in v4:
time: 133 us; the launch traced here: 132 us
  waiting for transfers between devices  57.9 us (44%)
  starting transfers between devices  38.4 us (29%)
  Pallas kernels  23.2 us (17%)
  local copies, waits for them, and re-layouts  8.93 us (7%)
  other arithmetic  2.89 us (2%)
    ppermute x32, waiting for transfers between devices, swap(): return lax.ppermute(array, axis, [(i, i ^ k) for i in range(size)])  38.4 us
    ppermute x32, starting transfers between devices, swap(): return lax.ppermute(array, axis, [(i, i ^ k) for i in range(size)])  25.4 us
    pallas_call x20, Pallas kernels, on_chip(): pl.pallas_call(body, out_shape=outs, in_specs=[vmem] * len(args), out_spe...  21.7 us
    ppermute x6, waiting for transfers between devices, per_device(): lax.ppermute(part, 'section', [(step, step - 1)])  19.5 us
    unnamed x19, local copies, waits for them, and re-layouts  7.59 us
    ppermute x6, starting transfers between devices, per_device(): lax.ppermute(part, 'section', [(step - 1, step)])  7.26 us
    ppermute x6, starting transfers between devices, per_device(): lax.ppermute(part, 'section', [(step, step - 1)])  5.7 us
  transfers between devices with their start and end apart: 44, of which 17 were waited for; matrix products, arithmetic and copies ran while one was open for 3% of the time, Pallas kernels for 13%

profile of v4, /device:TPU:0, one launch (start us, length us, event | category | flops | bytes accessed | tf_op | source)
XLA Modules:
  0.0 132.4 jit_solution(2805935014239633396)
XLA Ops:
  0.6 5.1 %collective-permute-start.2 = (bf16[4,4096]{1,0:T(4,128)(2,1)}, bf16[4,4096]{1,0:T(4,128)(2,1)S(1)}, u32[]{:S(2)}, u32[]{:S(2)}) collective-permute-start(bf16[4,4096]{1,0:T(4,128)(2,1)} %bitcast.38), channel_id=1, source_target_pairs={{0,12},{4,8},{8,4},{12,0},{1,13},{5,9},{9,5},{13,1},{2,14},{6,10},... | collective-permute-start | bytes 98312 | tf_op jit(solution)/shard_map/ppermute | solution.py:65
  5.7 0.6 collective-permute-start
  6.4 0.9 reduce_window_sum.11
  7.3 0.8 fusion.12
  8.9 0.7 copy.13.seeds
  9.7 1.2 copy-done.6
  10.9 1.2 copy-done.8
  12.1 1.5 %shard_map.113 = (f32[32,4096]{1,0:T(8,128)S(1)}, bf16[16,4096]{1,0:T(8,128)(2,1)S(1)}, bf16[16,4096]{1,0:T(8,128)(2,1)S(1)}, bf16[16,4096]{1,0:T(8,128)(2,1)S(1)}, bf16[16,4096]{1,0:T(8,128)(2,1)S(1)}) custom-call(s32[4,1]{1,0:T(4,128)S(1)} %copy.13.seeds, bf16[4,32,4096]{2,1,0:T(8,128)(2,1)S(1)} %copy-done.6, bf16[4,32,4096]{2,1,0:T(8,128)(2,1)S(1)} %copy-done.8), custom_call_target="tpu_custom_call" | custom-call | bytes 33554432 | tf_op jit(solution)/shard_map/pallas_call | solution.py:328
  13.7 0.8 pad_maximum_fusion.refs_0_
  14.5 1.7 %collective-permute-start.4 = (bf16[16,4096]{1,0:T(8,128)(2,1)S(1)}, bf16[16,4096]{1,0:T(8,128)(2,1)S(1)}, u32[]{:S(2)}, u32[]{:S(2)}) collective-permute-start(bf16[16,4096]{1,0:T(8,128)(2,1)S(1)} %pad_maximum_fusion.refs_0_), channel_id=1, source_target_pairs={{0,2},{1,3},{2,0},{3,1},{4,6},{5,7},{6,4},{7,5},{8,10},{9,11},{10,... | collective-permute-start | bytes 393224 | tf_op jit(solution)/shard_map/ppermute | solution.py:65
  16.3 3.3 %collective-permute-done.4.refs_2_ = bf16[16,4096]{1,0:T(8,128)(2,1)S(1)} collective-permute-done((bf16[16,4096]{1,0:T(8,128)(2,1)S(1)}, bf16[16,4096]{1,0:T(8,128)(2,1)S(1)}, u32[]{:S(2)}, u32[]{:S(2)}) %collective-permute-start.4) | collective-permute-done | bytes 131104 | tf_op jit(solution)/shard_map/ppermute | solution.py:65
  19.7 1.2 collective-permute-done.5.refs_3_
  20.9 2.2 %copy-done.2 = bf16[1,4096,512]{2,1,0:T(8,128)(2,1)S(1)} copy-done((bf16[1,4096,512]{2,1,0:T(8,128)(2,1)S(1)}, bf16[1,4096,512]{2,1,0:T(8,128)(2,1)}, u32[]{:S(2)}) %copy-start.2) | copy-done | bytes 4194328
  23.1 2.2 %copy-done.4 = bf16[1,512,4096]{2,1,0:T(8,128)(2,1)S(1)} copy-done((bf16[1,512,4096]{2,1,0:T(8,128)(2,1)S(1)}, bf16[1,512,4096]{2,1,0:T(8,128)(2,1)}, u32[]{:S(2)}) %copy-start.4) | copy-done | bytes 4194328
  25.3 1.8 %shard_map.115 = (bf16[64,512]{1,0:T(8,128)(2,1)S(1)}, bf16[32,4096]{1,0:T(8,128)(2,1)S(1)}, bf16[32,4096]{1,0:T(8,128)(2,1)S(1)}, bf16[32,4096]{1,0:T(8,128)(2,1)S(1)}, bf16[32,4096]{1,0:T(8,128)(2,1)S(1)}) custom-call(bf16[64,64]{1,0:T(8,128)(2,1)S(1)} %get-tuple-element.94.by_owner, bf16[4096,512]{1,0:T(8,128)(2,1)S(1)} %bitcast.30, ...), custom_call_target="tpu_custom_call" | custom-call | flops 642252800 | bytes 10035200 | tf_op jit(solution)/shard_map/pallas_call | solution.py:295
  27.3 1.6 %collective-permute-start.10 = (bf16[32,4096]{1,0:T(8,128)(2,1)S(1)}, bf16[32,4096]{1,0:T(8,128)(2,1)S(1)}, u32[]{:S(2)}, u32[]{:S(2)}) collective-permute-start(bf16[32,4096]{1,0:T(8,128)(2,1)S(1)} %get-tuple-element.103), channel_id=1, source_target_pairs={{0,2},{1,3},{2,0},{3,1},{4,6},{5,7},{6,4},{7,5},{8,10},{9,11},{10,... | collective-permute-start | bytes 786440 | tf_op jit(solution)/shard_map/ppermute | solution.py:65
  29.0 3.0 %shard_map.114 = (bf16[64,512]{1,0:T(8,128)(2,1)S(1)}, bf16[32,4096]{1,0:T(8,128)(2,1)S(1)}, bf16[32,4096]{1,0:T(8,128)(2,1)S(1)}, bf16[32,4096]{1,0:T(8,128)(2,...) custom-call(bf16[64,64]{1,0:T(8,128)(2,1)S(1)} %get-tuple-element.94, ...), custom_call_target="tpu_custom_call" | custom-call | flops 719323136 | bytes 11239424 | tf_op jit(solution)/shard_map/pallas_call | solution.py:295
  32.5 1.6 %collective-permute-start.7 = (bf16[32,32]{1,0:T(8,128)(2,1)S(1)}, bf16[32,32]{1,0:T(8,128)(2,1)S(1)}, u32[]{:S(2)}, u32[]{:S(2)}) collective-permute-start(bf16[32,32]{1,0:T(8,128)(2,1)S(1)} %get-tuple-element.99), channel_id=1, source_target_pairs={{0,2},{1,3},{2,0},{3,1},{4,6},{5,7},{6,4},{7,5},{8,10},{9,11},{10,... | collective-permute-start | bytes 6152 | tf_op jit(solution)/shard_map/ppermute | solution.py:65
  34.2 0.8 collective-permute-start.8
  35.0 6.8 %collective-permute-done.7.refs_4_ = bf16[32,32]{1,0:T(8,128)(2,1)S(1)} collective-permute-done((bf16[32,32]{1,0:T(8,128)(2,1)S(1)}, bf16[32,32]{1,0:T(8,128)(2,1)S(1)}, u32[]{:S(2)}, u32[]{:S(2)}) %collective-permute-start.7) | collective-permute-done | bytes 2080 | tf_op jit(solution)/shard_map/ppermute | solution.py:65
  41.8 1.6 %collective-permute-start.14 = (bf16[32,4096]{1,0:T(8,128)(2,1)S(1)}, bf16[32,4096]{1,0:T(8,128)(2,1)S(1)}, u32[]{:S(2)}, u32[]{:S(2)}) collective-permute-start(bf16[32,4096]{1,0:T(8,128)(2,1)S(1)} %get-tuple-element.109), channel_id=1, source_target_pairs={{0,2},{1,3},{2,0},{3,1},{4,6},{5,7},{6,4},{7,5},{8,10},{9,11},{10,... | collective-permute-start | bytes 786440 | tf_op jit(solution)/shard_map/ppermute | solution.py:65
  44.0 3.3 %collective-permute-start.12 = (bf16[16,4096]{1,0:T(8,128)(2,1)S(1)}, bf16[16,4096]{1,0:T(8,128)(2,1)S(1)}, u32[]{:S(2)}, u32[]{:S(2)}) collective-permute-start(bf16[16,4096]{1,0:T(8,128)(2,1)S(1)} %get-tuple-element.105), channel_id=1, source_target_pairs={{0,4},{1,5},{2,6},{3,7},{16,20},{17,21},{18,22},{19,23}} | collective-permute-start | bytes 393224 | tf_op jit(solution)/shard_map/ppermute | solution.py:423
  47.3 1.3 collective-permute-start.19
  48.6 2.3 %collective-permute-done.14.refs_2_ = bf16[32,4096]{1,0:T(8,128)(2,1)S(1)} collective-permute-done((bf16[32,4096]{1,0:T(8,128)(2,1)S(1)}, bf16[32,4096]{1,0:T(8,128)(2,1)S(1)}, u32[]{:S(2)}, u32[]{:S(2)}) %collective-permute-start.14) | collective-permute-done | bytes 262176 | tf_op jit(solution)/shard_map/ppermute | solution.py:65
  50.9 4.8 %collective-permute-done.15.refs_3_ = bf16[32,4096]{1,0:T(8,128)(2,1)S(1)} collective-permute-done((bf16[32,4096]{1,0:T(8,128)(2,1)S(1)}, bf16[32,4096]{1,0:T(8,128)(2,1)S(1)}, u32[]{:S(2)}, u32[]{:S(2)}) %collective-permute-start.15) | collective-permute-done | bytes 262176 | tf_op jit(solution)/shard_map/ppermute | solution.py:65
  55.8 1.0 shard_map.118
  56.8 0.7 collective-permute-start.16
  57.5 1.0 shard_map.121
  58.5 0.7 collective-permute-start.20
  59.1 1.0 shard_map.119
  60.1 0.7 collective-permute-start.17
  60.8 1.0 shard_map.122
  61.8 0.7 collective-permute-start.21
  62.5 1.0 shard_map.120
  63.5 0.7 collective-permute-start.18
  64.2 1.0 shard_map.123
  65.2 0.7 collective-permute-start.22
  66.2 1.7 %collective-permute-start.28 = (bf16[32,4096]{1,0:T(8,128)(2,1)S(1)}, bf16[32,4096]{1,0:T(8,128)(2,1)S(1)}, u32[]{:S(2)}, u32[]{:S(2)}) collective-permute-start(bf16[32,4096]{1,0:T(8,128)(2,1)S(1)} %get-tuple-element.155.refs_0_), channel_id=1, source_target_pairs={{0,2},{1,3},{2,0},{3,1},{4,6},{5,7},{6,4},{7,5},{8,10},{9,11},{10,... | collective-permute-start | bytes 786440 | tf_op jit(solution)/shard_map/ppermute | solution.py:65
  67.9 1.0 shard_map.125
  68.9 1.0 shard_map.126
  69.9 0.7 collective-permute-start.24
  70.6 0.7 collective-permute-start.23
  71.7 1.4 %collective-permute-start.27 = (bf16[32,1024]{1,0:T(8,128)(2,1)S(1)}, bf16[32,1024]{1,0:T(8,128)(2,1)S(1)}, u32[]{:S(2)}, u32[]{:S(2)}) collective-permute-start(bf16[32,1024]{1,0:T(8,128)(2,1)S(1)} %get-tuple-element.142), channel_id=1, source_target_pairs={{0,3},{1,2},{2,1},{3,0},{4,7},{5,6},{6,5},{7,4},{8,11},{9,10},{10,... | collective-permute-start | bytes 196616 | tf_op jit(solution)/shard_map/ppermute | solution.py:65
  73.2 3.2 %collective-permute-done.26.refs_2_ = bf16[32,1024]{1,0:T(8,128)(2,1)S(1)} collective-permute-done((bf16[32,1024]{1,0:T(8,128)(2,1)S(1)}, bf16[32,1024]{1,0:T(8,128)(2,1)S(1)}, u32[]{:S(2)}, u32[]{:S(2)}) %collective-permute-start.26) | collective-permute-done | bytes 65568 | tf_op jit(solution)/shard_map/ppermute | solution.py:65
  76.4 0.9 collective-permute-done.27.refs_3_
  77.9 1.0 shard_map.127
  78.8 1.5 %collective-permute-start.29 = (bf16[16,4096]{1,0:T(8,128)(2,1)S(1)}, bf16[16,4096]{1,0:T(8,128)(2,1)S(1)}, u32[]{:S(2)}, u32[]{:S(2)}) collective-permute-start(bf16[16,4096]{1,0:T(8,128)(2,1)S(1)} %get-tuple-element.146), channel_id=1, source_target_pairs={{4,0},{5,1},{6,2},{7,3},{20,16},{21,17},{22,18},{23,19}} | collective-permute-start | bytes 393224 | tf_op jit(solution)/shard_map/ppermute | solution.py:452
  80.3 1.0 shard_map.128
  81.3 1.6 %collective-permute-start.30 = (bf16[16,4096]{1,0:T(8,128)(2,1)S(1)}, bf16[16,4096]{1,0:T(8,128)(2,1)S(1)}, u32[]{:S(2)}, u32[]{:S(2)}) collective-permute-start(bf16[16,4096]{1,0:T(8,128)(2,1)S(1)} %get-tuple-element.149), channel_id=1, source_target_pairs={{4,0},{5,1},{6,2},{7,3},{20,16},{21,17},{22,18},{23,19}} | collective-permute-start | bytes 393224 | tf_op jit(solution)/shard_map/ppermute | solution.py:452
  82.9 0.7 shard_map.129
  83.6 0.9 shard_map.130
  84.5 16.7 %collective-permute-done.29.came = bf16[16,4096]{1,0:T(8,128)(2,1)S(1)} collective-permute-done((bf16[16,4096]{1,0:T(8,128)(2,1)S(1)}, bf16[16,4096]{1,0:T(8,128)(2,1)S(1)}, u32[]{:S(2)}, u32[]{:S(2)}) %collective-permute-start.29) | collective-permute-done | bytes 131104 | tf_op jit(solution)/shard_map/ppermute | solution.py:452
  101.2 2.8 %collective-permute-done.30.came = bf16[16,4096]{1,0:T(8,128)(2,1)S(1)} collective-permute-done((bf16[16,4096]{1,0:T(8,128)(2,1)S(1)}, bf16[16,4096]{1,0:T(8,128)(2,1)S(1)}, u32[]{:S(2)}, u32[]{:S(2)}) %collective-permute-start.30) | collective-permute-done | bytes 131104 | tf_op jit(solution)/shard_map/ppermute | solution.py:452
  104.7 1.6 %collective-permute-start.36 = (bf16[16,4096]{1,0:T(8,128)(2,1)S(1)}, bf16[16,4096]{1,0:T(8,128)(2,1)S(1)}, u32[]{:S(2)}, u32[]{:S(2)}) collective-permute-start(bf16[16,4096]{1,0:T(8,128)(2,1)S(1)} %shard_map.132.refs_1_), channel_id=1, source_target_pairs={{0,2},{1,3},{2,0},{3,1},{4,6},{5,7},{6,4},{7,5},{8,10},{9,11},{10,... | collective-permute-start | bytes 393224 | tf_op jit(solution)/shard_map/ppermute | solution.py:65
  106.7 3.7 %collective-permute-done.35.refs_4_ = bf16[16,4096]{1,0:T(8,128)(2,1)S(1)} collective-permute-done((bf16[16,4096]{1,0:T(8,128)(2,1)S(1)}, bf16[16,4096]{1,0:T(8,128)(2,1)S(1)}, u32[]{:S(2)}, u32[]{:S(2)}) %collective-permute-start.35) | collective-permute-done | bytes 131104 | tf_op jit(solution)/shard_map/ppermute | solution.py:65
  110.5 1.4 %collective-permute-done.36.refs_5_ = bf16[16,4096]{1,0:T(8,128)(2,1)S(1)} collective-permute-done((bf16[16,4096]{1,0:T(8,128)(2,1)S(1)}, bf16[16,4096]{1,0:T(8,128)(2,1)S(1)}, u32[]{:S(2)}, u32[]{:S(2)}) %collective-permute-start.36) | collective-permute-done | bytes 131104 | tf_op jit(solution)/shard_map/ppermute | solution.py:65
  111.9 1.3 %collective-permute-done.38.refs_7_ = bf16[16,4096]{1,0:T(8,128)(2,1)S(1)} collective-permute-done((bf16[16,4096]{1,0:T(8,128)(2,1)S(1)}, bf16[16,4096]{1,0:T(8,128)(2,1)S(1)}, u32[]{:S(2)}, u32[]{:S(2)}) %collective-permute-start.38) | collective-permute-done | bytes 131104 | tf_op jit(solution)/shard_map/ppermute | solution.py:65
  113.2 4.6 %shard_map.133 = (f32[32,4096]{1,0:T(8,128)S(1)}, bf16[32,4096]{1,0:T(8,128)(2,1)S(1)}) custom-call(bf16[64,512]{1,0:T(8,128)(2,1)S(1)} %get-tuple-element.154.keys, bf16[64,512]{1,0:T(8,128)(2,1)S(1)} %get-tuple-element.160.values, bf16[128,512]{1,0:T(8,128)(2,1)S(1)} %get-tuple-element.161.query, f32[128,32]{1,0:T(8,128)S(1)} %get-tuple-element.162.probs, ...), custom_call_target="tpu_custom_call" | custom-call | flops 957874176 | bytes 14966784 | tf_op jit(solution)/shard_map/pallas_call | solution.py:295
  118.1 1.4 %collective-permute-done.39 = bf16[32,4096]{1,0:T(8,128)(2,1)S(1)} collective-permute-done((bf16[32,4096]{1,0:T(8,128)(2,1)S(1)}, bf16[32,4096]{1,0:T(8,128)(2,1)S(1)}, u32[]{:S(2)}, u32[]{:S(2)}) %collective-permute-start.39) | collective-permute-done | bytes 262176 | tf_op jit(solution)/shard_map/ppermute | solution.py:65
  120.1 5.0 %collective-permute-done.40 = bf16[16,4096]{1,0:T(8,128)(2,1)S(1)} collective-permute-done((bf16[16,4096]{1,0:T(8,128)(2,1)S(1)}, bf16[16,4096]{1,0:T(8,128)(2,1)S(1)}, u32[]{:S(2)}, u32[]{:S(2)}) %collective-permute-start.40) | collective-permute-done | bytes 131104 | tf_op jit(solution)/shard_map/ppermute | solution.py:65
  125.4 3.4 %collective-permute-start.42 = (bf16[4,4096]{1,0:T(4,128)(2,1)S(1)}, bf16[4,4096]{1,0:T(4,128)(2,1)S(1)}, u32[]{:S(2)}, u32[]{:S(2)}) collective-permute-start(bf16[4,4096]{1,0:T(4,128)(2,1)S(1)} %get-tuple-element.181), channel_id=1, source_target_pairs={{0,8},{4,12},{8,0},{12,4},{1,9},{5,13},{9,1},{13,5},{2,10},{6,14},... | collective-permute-start | bytes 98312 | tf_op jit(solution)/shard_map/ppermute | solution.py:65
  128.8 1.0 collective-permute-done.41
  129.8 1.4 %collective-permute-done.43 = bf16[4,4096]{1,0:T(4,128)(2,1)S(1)} collective-permute-done((bf16[4,4096]{1,0:T(4,128)(2,1)S(1)}, bf16[4,4096]{1,0:T(4,128)(2,1)S(1)}, u32[]{:S(2)}, u32[]{:S(2)}) %collective-permute-start.43) | collective-permute-done | bytes 32800 | tf_op jit(solution)/shard_map/ppermute | solution.py:65
  131.7 0.7 fusion.2
  (93 shorter events, 6.7 us)
Async XLA Ops:
  0.6 13.0 %collective-permute-start.2 = (bf16[4,4096]{1,0:T(4,128)(2,1)}, bf16[4,4096]{1,0:T(4,128)(2,1)S(1)}, u32[]{:S(2)}, u32[]{:S(2)}) collective-permute-start(bf16[4,4096]{1,0:T(4,128)(2,1)} %bitcast.38), channel_id=1, source_target_pairs={{0,12},{4,8},{8,4},{12,0},{1,13},{5,9},{9,5},{13,1},{2,14},{6,10},... | collective-permute-start | bytes 98312 | tf_op jit(solution)/shard_map/ppermute | solution.py:65
  5.7 7.9 %collective-permute-start.1 = (bf16[4,4096]{1,0:T(4,128)(2,1)}, bf16[4,4096]{1,0:T(4,128)(2,1)S(1)}, u32[]{:S(2)}, u32[]{:S(2)}) collective-permute-start(bf16[4,4096]{1,0:T(4,128)(2,1)} %bitcast.39), channel_id=1, source_target_pairs={{0,8},{4,12},{8,0},{12,4},{1,9},{5,13},{9,1},{13,5},{2,10},{6,14},... | collective-permute-start | bytes 98312 | tf_op jit(solution)/shard_map/ppermute | solution.py:65
  5.7 7.9 %collective-permute-start = (bf16[4,4096]{1,0:T(4,128)(2,1)}, bf16[4,4096]{1,0:T(4,128)(2,1)S(1)}, u32[]{:S(2)}, u32[]{:S(2)}) collective-permute-start(bf16[4,4096]{1,0:T(4,128)(2,1)} %bitcast.40), channel_id=1, source_target_pairs={{0,4},{4,0},{8,12},{12,8},{1,5},{5,1},{9,13},{13,9},{2,6},{6,2},{1... | collective-permute-start | bytes 98312 | tf_op jit(solution)/shard_map/ppermute | solution.py:65
  9.7 1.2 copy-start.6
  10.9 1.2 copy-start.8
  12.1 16.9 %copy-start.7 = (bf16[4,32,4096]{2,1,0:T(8,128)(2,1)S(1)}, bf16[4,32,4096]{2,1,0:T(8,128)(2,1)}, u32[]{:S(2)}) copy-start(bf16[4,32,4096]{2,1,0:T(8,128)(2,1)} %inputs.3) | copy-start | bytes 3145732
  14.5 5.0 %collective-permute-start.4 = (bf16[16,4096]{1,0:T(8,128)(2,1)S(1)}, bf16[16,4096]{1,0:T(8,128)(2,1)S(1)}, u32[]{:S(2)}, u32[]{:S(2)}) collective-permute-start(bf16[16,4096]{1,0:T(8,128)(2,1)S(1)} %pad_maximum_fusion.refs_0_), channel_id=1, source_target_pairs={{0,2},{1,3},{2,0},{3,1},{4,6},{5,7},{6,4},{7,5},{8,10},{9,11},{10,... | collective-permute-start | bytes 393224 | tf_op jit(solution)/shard_map/ppermute | solution.py:65
  16.3 3.5 %collective-permute-start.3 = (bf16[16,4096]{1,0:T(8,128)(2,1)S(1)}, bf16[16,4096]{1,0:T(8,128)(2,1)S(1)}, u32[]{:S(2)}, u32[]{:S(2)}) collective-permute-start(bf16[16,4096]{1,0:T(8,128)(2,1)S(1)} %pad_maximum_fusion.refs_0_), channel_id=1, source_target_pairs={{0,1},{1,0},{2,3},{3,2},{4,5},{5,4},{6,7},{7,6},{8,9},{9,8},{10,11... | collective-permute-start | bytes 393224 | tf_op jit(solution)/shard_map/ppermute | solution.py:65
  19.6 1.3 %collective-permute-start.5 = (bf16[16,4096]{1,0:T(8,128)(2,1)S(1)}, bf16[16,4096]{1,0:T(8,128)(2,1)S(1)}, u32[]{:S(2)}, u32[]{:S(2)}) collective-permute-start(bf16[16,4096]{1,0:T(8,128)(2,1)S(1)} %collective-permute-done.4.refs_2_), channel_id=1, source_target_pairs={{0,1},{1,0},{2,3},{3,2},{4,5},{5,4},{6,7},{7,6},{8,9},{9,8},{10,11... | collective-permute-start | bytes 393224 | tf_op jit(solution)/shard_map/ppermute | solution.py:65
  20.9 2.2 %copy-start.2 = (bf16[1,4096,512]{2,1,0:T(8,128)(2,1)S(1)}, bf16[1,4096,512]{2,1,0:T(8,128)(2,1)}, u32[]{:S(2)}) copy-start(bf16[1,4096,512]{2,1,0:T(8,128)(2,1)} %param.18) | copy-start | bytes 12582916
  23.1 2.2 %copy-start.4 = (bf16[1,512,4096]{2,1,0:T(8,128)(2,1)S(1)}, bf16[1,512,4096]{2,1,0:T(8,128)(2,1)}, u32[]{:S(2)}) copy-start(bf16[1,512,4096]{2,1,0:T(8,128)(2,1)} %param.19) | copy-start | bytes 12582916
  25.3 3.7 %copy-start = (bf16[1,4096,512]{2,1,0:T(8,128)(2,1)S(1)}, bf16[1,4096,512]{2,1,0:T(8,128)(2,1)}, u32[]{:S(2)}) copy-start(bf16[1,4096,512]{2,1,0:T(8,128)(2,1)} %param.16) | copy-start | bytes 12582916
  25.3 3.7 %copy-start.1 = (bf16[1,4096,512]{2,1,0:T(8,128)(2,1)S(1)}, bf16[1,4096,512]{2,1,0:T(8,128)(2,1)}, u32[]{:S(2)}) copy-start(bf16[1,4096,512]{2,1,0:T(8,128)(2,1)} %param.17) | copy-start | bytes 12582916
  27.1 16.3 %collective-permute-start.9 = (bf16[32,4096]{1,0:T(8,128)(2,1)S(1)}, bf16[32,4096]{1,0:T(8,128)(2,1)S(1)}, u32[]{:S(2)}, u32[]{:S(2)}) collective-permute-start(bf16[32,4096]{1,0:T(8,128)(2,1)S(1)} %get-tuple-element.102), channel_id=1, source_target_pairs={{0,1},{1,0},{2,3},{3,2},{4,5},{5,4},{6,7},{7,6},{8,9},{9,8},{10,11... | collective-permute-start | bytes 786440 | tf_op jit(solution)/shard_map/ppermute | solution.py:65
  27.3 16.3 %collective-permute-start.10 = (bf16[32,4096]{1,0:T(8,128)(2,1)S(1)}, bf16[32,4096]{1,0:T(8,128)(2,1)S(1)}, u32[]{:S(2)}, u32[]{:S(2)}) collective-permute-start(bf16[32,4096]{1,0:T(8,128)(2,1)S(1)} %get-tuple-element.103), channel_id=1, source_target_pairs={{0,2},{1,3},{2,0},{3,1},{4,6},{5,7},{6,4},{7,5},{8,10},{9,11},{10,... | collective-permute-start | bytes 786440 | tf_op jit(solution)/shard_map/ppermute | solution.py:65
  29.0 14.7 %collective-permute-start.11 = (bf16[32,4096]{1,0:T(8,128)(2,1)S(1)}, bf16[32,4096]{1,0:T(8,128)(2,1)S(1)}, u32[]{:S(2)}, u32[]{:S(2)}) collective-permute-start(bf16[32,4096]{1,0:T(8,128)(2,1)S(1)} %get-tuple-element.104), channel_id=1, source_target_pairs={{0,3},{1,2},{2,1},{3,0},{4,7},{5,6},{6,5},{7,4},{8,11},{9,10},{10,... | collective-permute-start | bytes 786440 | tf_op jit(solution)/shard_map/ppermute | solution.py:65
  32.0 2.1 %collective-permute-start.6 = (bf16[32,32]{1,0:T(8,128)(2,1)S(1)}, bf16[32,32]{1,0:T(8,128)(2,1)S(1)}, u32[]{:S(2)}, u32[]{:S(2)}) collective-permute-start(bf16[32,32]{1,0:T(8,128)(2,1)S(1)} %get-tuple-element.98), channel_id=1, source_target_pairs={{0,1},{1,0},{2,3},{3,2},{4,5},{5,4},{6,7},{7,6},{8,9},{9,8},{10,11... | collective-permute-start | bytes 6152 | tf_op jit(solution)/shard_map/ppermute | solution.py:65
  32.5 9.2 %collective-permute-start.7 = (bf16[32,32]{1,0:T(8,128)(2,1)S(1)}, bf16[32,32]{1,0:T(8,128)(2,1)S(1)}, u32[]{:S(2)}, u32[]{:S(2)}) collective-permute-start(bf16[32,32]{1,0:T(8,128)(2,1)S(1)} %get-tuple-element.99), channel_id=1, source_target_pairs={{0,2},{1,3},{2,0},{3,1},{4,6},{5,7},{6,4},{7,5},{8,10},{9,11},{10,... | collective-permute-start | bytes 6152 | tf_op jit(solution)/shard_map/ppermute | solution.py:65
  34.2 7.6 %collective-permute-start.8 = (bf16[32,32]{1,0:T(8,128)(2,1)S(1)}, bf16[32,32]{1,0:T(8,128)(2,1)S(1)}, u32[]{:S(2)}, u32[]{:S(2)}) collective-permute-start(bf16[32,32]{1,0:T(8,128)(2,1)S(1)} %get-tuple-element.100), channel_id=1, source_target_pairs={{0,3},{1,2},{2,1},{3,0},{4,7},{5,6},{6,5},{7,4},{8,11},{9,10},{10,... | collective-permute-start | bytes 6152 | tf_op jit(solution)/shard_map/ppermute | solution.py:65
  41.8 6.8 %collective-permute-start.13 = (bf16[32,4096]{1,0:T(8,128)(2,1)S(1)}, bf16[32,4096]{1,0:T(8,128)(2,1)S(1)}, u32[]{:S(2)}, u32[]{:S(2)}) collective-permute-start(bf16[32,4096]{1,0:T(8,128)(2,1)S(1)} %get-tuple-element.108), channel_id=1, source_target_pairs={{0,1},{1,0},{2,3},{3,2},{4,5},{5,4},{6,7},{7,6},{8,9},{9,8},{10,11... | collective-permute-start | bytes 786440 | tf_op jit(solution)/shard_map/ppermute | solution.py:65
  41.8 9.1 %collective-permute-start.14 = (bf16[32,4096]{1,0:T(8,128)(2,1)S(1)}, bf16[32,4096]{1,0:T(8,128)(2,1)S(1)}, u32[]{:S(2)}, u32[]{:S(2)}) collective-permute-start(bf16[32,4096]{1,0:T(8,128)(2,1)S(1)} %get-tuple-element.109), channel_id=1, source_target_pairs={{0,2},{1,3},{2,0},{3,1},{4,6},{5,7},{6,4},{7,5},{8,10},{9,11},{10,... | collective-permute-start | bytes 786440 | tf_op jit(solution)/shard_map/ppermute | solution.py:65
  43.4 12.3 %collective-permute-start.15 = (bf16[32,4096]{1,0:T(8,128)(2,1)S(1)}, bf16[32,4096]{1,0:T(8,128)(2,1)S(1)}, u32[]{:S(2)}, u32[]{:S(2)}) collective-permute-start(bf16[32,4096]{1,0:T(8,128)(2,1)S(1)} %get-tuple-element.110), channel_id=1, source_target_pairs={{0,3},{1,2},{2,1},{3,0},{4,7},{5,6},{6,5},{7,4},{8,11},{9,10},{10,... | collective-permute-start | bytes 786440 | tf_op jit(solution)/shard_map/ppermute | solution.py:65
  44.0 11.8 %collective-permute-start.12 = (bf16[16,4096]{1,0:T(8,128)(2,1)S(1)}, bf16[16,4096]{1,0:T(8,128)(2,1)S(1)}, u32[]{:S(2)}, u32[]{:S(2)}) collective-permute-start(bf16[16,4096]{1,0:T(8,128)(2,1)S(1)} %get-tuple-element.105), channel_id=1, source_target_pairs={{0,4},{1,5},{2,6},{3,7},{16,20},{17,21},{18,22},{19,23}} | collective-permute-start | bytes 393224 | tf_op jit(solution)/shard_map/ppermute | solution.py:423
  47.3 10.2 %collective-permute-start.19 = (bf16[16,4096]{1,0:T(8,128)(2,1)S(1)}, bf16[16,4096]{1,0:T(8,128)(2,1)S(1)}, u32[]{:S(2)}, u32[]{:S(2)}) collective-permute-start(bf16[16,4096]{1,0:T(8,128)(2,1)S(1)} %get-tuple-element.118), channel_id=1, source_target_pairs={{0,4},{1,5},{2,6},{3,7},{16,20},{17,21},{18,22},{19,23}} | collective-permute-start | bytes 393224 | tf_op jit(solution)/shard_map/ppermute | solution.py:423
  56.8 2.3 %collective-permute-start.16 = (bf16[16,4096]{1,0:T(8,128)(2,1)S(1)}, bf16[16,4096]{1,0:T(8,128)(2,1)S(1)}, u32[]{:S(2)}, u32[]{:S(2)}) collective-permute-start(bf16[16,4096]{1,0:T(8,128)(2,1)S(1)} %get-tuple-element.112), channel_id=1, source_target_pairs={{4,8},{5,9},{6,10},{7,11},{20,24},{21,25},{22,26},{23,27}} | collective-permute-start | bytes 393224 | tf_op jit(solution)/shard_map/ppermute | solution.py:423
  58.5 2.4 %collective-permute-start.20 = (bf16[16,4096]{1,0:T(8,128)(2,1)S(1)}, bf16[16,4096]{1,0:T(8,128)(2,1)S(1)}, u32[]{:S(2)}, u32[]{:S(2)}) collective-permute-start(bf16[16,4096]{1,0:T(8,128)(2,1)S(1)} %get-tuple-element.120), channel_id=1, source_target_pairs={{4,8},{5,9},{6,10},{7,11},{20,24},{21,25},{22,26},{23,27}} | collective-permute-start | bytes 393224 | tf_op jit(solution)/shard_map/ppermute | solution.py:423
  60.1 2.4 %collective-permute-start.17 = (bf16[16,4096]{1,0:T(8,128)(2,1)S(1)}, bf16[16,4096]{1,0:T(8,128)(2,1)S(1)}, u32[]{:S(2)}, u32[]{:S(2)}) collective-permute-start(bf16[16,4096]{1,0:T(8,128)(2,1)S(1)} %get-tuple-element.114), channel_id=1, source_target_pairs={{8,12},{9,13},{10,14},{11,15},{24,28},{25,29},{26,30},{27,31}} | collective-permute-start | bytes 393224 | tf_op jit(solution)/shard_map/ppermute | solution.py:423
  61.8 2.4 %collective-permute-start.21 = (bf16[16,4096]{1,0:T(8,128)(2,1)S(1)}, bf16[16,4096]{1,0:T(8,128)(2,1)S(1)}, u32[]{:S(2)}, u32[]{:S(2)}) collective-permute-start(bf16[16,4096]{1,0:T(8,128)(2,1)S(1)} %get-tuple-element.122), channel_id=1, source_target_pairs={{8,12},{9,13},{10,14},{11,15},{24,28},{25,29},{26,30},{27,31}} | collective-permute-start | bytes 393224 | tf_op jit(solution)/shard_map/ppermute | solution.py:423
  63.5 2.7 %collective-permute-start.18 = (bf16[16,4096]{1,0:T(8,128)(2,1)S(1)}, bf16[16,4096]{1,0:T(8,128)(2,1)S(1)}, u32[]{:S(2)}, u32[]{:S(2)}) collective-permute-start(bf16[16,4096]{1,0:T(8,128)(2,1)S(1)} %get-tuple-element.117), channel_id=1, source_target_pairs={{12,8},{13,9},{14,10},{15,11},{28,24},{29,25},{30,26},{31,27}} | collective-permute-start | bytes 393224 | tf_op jit(solution)/shard_map/ppermute | solution.py:452
  65.2 1.0 collective-permute-start.22
  66.2 11.1 %collective-permute-start.28 = (bf16[32,4096]{1,0:T(8,128)(2,1)S(1)}, bf16[32,4096]{1,0:T(8,128)(2,1)S(1)}, u32[]{:S(2)}, u32[]{:S(2)}) collective-permute-start(bf16[32,4096]{1,0:T(8,128)(2,1)S(1)} %get-tuple-element.155.refs_0_), channel_id=1, source_target_pairs={{0,2},{1,3},{2,0},{3,1},{4,6},{5,7},{6,4},{7,5},{8,10},{9,11},{10,... | collective-permute-start | bytes 786440 | tf_op jit(solution)/shard_map/ppermute | solution.py:65
  69.9 1.9 %collective-permute-start.25 = (bf16[32,1024]{1,0:T(8,128)(2,1)S(1)}, bf16[32,1024]{1,0:T(8,128)(2,1)S(1)}, u32[]{:S(2)}, u32[]{:S(2)}) collective-permute-start(bf16[32,1024]{1,0:T(8,128)(2,1)S(1)} %get-tuple-element.140), channel_id=1, source_target_pairs={{0,1},{1,0},{2,3},{3,2},{4,5},{5,4},{6,7},{7,6},{8,9},{9,8},{10,11... | collective-permute-start | bytes 196616 | tf_op jit(solution)/shard_map/ppermute | solution.py:65
  69.9 7.4 %collective-permute-start.24 = (bf16[16,4096]{1,0:T(8,128)(2,1)S(1)}, bf16[16,4096]{1,0:T(8,128)(2,1)S(1)}, u32[]{:S(2)}, u32[]{:S(2)}) collective-permute-start(bf16[16,4096]{1,0:T(8,128)(2,1)S(1)} %get-tuple-element.138), channel_id=1, source_target_pairs={{8,4},{9,5},{10,6},{11,7},{24,20},{25,21},{26,22},{27,23}} | collective-permute-start | bytes 393224 | tf_op jit(solution)/shard_map/ppermute | solution.py:452
  70.6 6.7 %collective-permute-start.23 = (bf16[16,4096]{1,0:T(8,128)(2,1)S(1)}, bf16[16,4096]{1,0:T(8,128)(2,1)S(1)}, u32[]{:S(2)}, u32[]{:S(2)}) collective-permute-start(bf16[16,4096]{1,0:T(8,128)(2,1)S(1)} %get-tuple-element.136), channel_id=1, source_target_pairs={{8,4},{9,5},{10,6},{11,7},{24,20},{25,21},{26,22},{27,23}} | collective-permute-start | bytes 393224 | tf_op jit(solution)/shard_map/ppermute | solution.py:452
  71.3 5.1 %collective-permute-start.26 = (bf16[32,1024]{1,0:T(8,128)(2,1)S(1)}, bf16[32,1024]{1,0:T(8,128)(2,1)S(1)}, u32[]{:S(2)}, u32[]{:S(2)}) collective-permute-start(bf16[32,1024]{1,0:T(8,128)(2,1)S(1)} %get-tuple-element.141), channel_id=1, source_target_pairs={{0,2},{1,3},{2,0},{3,1},{4,6},{5,7},{6,4},{7,5},{8,10},{9,11},{10,... | collective-permute-start | bytes 196616 | tf_op jit(solution)/shard_map/ppermute | solution.py:65
  71.7 5.6 %collective-permute-start.27 = (bf16[32,1024]{1,0:T(8,128)(2,1)S(1)}, bf16[32,1024]{1,0:T(8,128)(2,1)S(1)}, u32[]{:S(2)}, u32[]{:S(2)}) collective-permute-start(bf16[32,1024]{1,0:T(8,128)(2,1)S(1)} %get-tuple-element.142), channel_id=1, source_target_pairs={{0,3},{1,2},{2,1},{3,0},{4,7},{5,6},{6,5},{7,4},{8,11},{9,10},{10,... | collective-permute-start | bytes 196616 | tf_op jit(solution)/shard_map/ppermute | solution.py:65
  77.3 6.3 %collective-permute-start.31 = (bf16[32,4096]{1,0:T(8,128)(2,1)S(1)}, bf16[32,4096]{1,0:T(8,128)(2,1)S(1)}, u32[]{:S(2)}, u32[]{:S(2)}) collective-permute-start(bf16[32,4096]{1,0:T(8,128)(2,1)S(1)} %get-tuple-element.155.refs_0_), channel_id=1, source_target_pairs={{0,1},{1,0},{2,3},{3,2},{4,5},{5,4},{6,7},{7,6},{8,9},{9,8},{10,11... | collective-permute-start | bytes 786440 | tf_op jit(solution)/shard_map/ppermute | solution.py:65
  77.5 6.1 %collective-permute-start.32 = (bf16[32,4096]{1,0:T(8,128)(2,1)S(1)}, bf16[32,4096]{1,0:T(8,128)(2,1)S(1)}, u32[]{:S(2)}, u32[]{:S(2)}) collective-permute-start(bf16[32,4096]{1,0:T(8,128)(2,1)S(1)} %collective-permute-done.28.refs_2_), channel_id=1, source_target_pairs={{0,1},{1,0},{2,3},{3,2},{4,5},{5,4},{6,7},{7,6},{8,9},{9,8},{10,11... | collective-permute-start | bytes 786440 | tf_op jit(solution)/shard_map/ppermute | solution.py:65
  78.8 22.4 %collective-permute-start.29 = (bf16[16,4096]{1,0:T(8,128)(2,1)S(1)}, bf16[16,4096]{1,0:T(8,128)(2,1)S(1)}, u32[]{:S(2)}, u32[]{:S(2)}) collective-permute-start(bf16[16,4096]{1,0:T(8,128)(2,1)S(1)} %get-tuple-element.146), channel_id=1, source_target_pairs={{4,0},{5,1},{6,2},{7,3},{20,16},{21,17},{22,18},{23,19}} | collective-permute-start | bytes 393224 | tf_op jit(solution)/shard_map/ppermute | solution.py:452
  80.3 32.9 %copy-start.5 = (bf16[1,512,4096]{2,1,0:T(8,128)(2,1)S(1)}, bf16[1,512,4096]{2,1,0:T(8,128)(2,1)}, u32[]{:S(2)}) copy-start(bf16[1,512,4096]{2,1,0:T(8,128)(2,1)} %param.19) | copy-start | bytes 12582916
  81.3 31.9 %copy-start.3 = (bf16[1,4096,512]{2,1,0:T(8,128)(2,1)S(1)}, bf16[1,4096,512]{2,1,0:T(8,128)(2,1)}, u32[]{:S(2)}) copy-start(bf16[1,4096,512]{2,1,0:T(8,128)(2,1)} %param.18) | copy-start | bytes 12582916
  81.3 22.7 %collective-permute-start.30 = (bf16[16,4096]{1,0:T(8,128)(2,1)S(1)}, bf16[16,4096]{1,0:T(8,128)(2,1)S(1)}, u32[]{:S(2)}, u32[]{:S(2)}) collective-permute-start(bf16[16,4096]{1,0:T(8,128)(2,1)S(1)} %get-tuple-element.149), channel_id=1, source_target_pairs={{4,0},{5,1},{6,2},{7,3},{20,16},{21,17},{22,18},{23,19}} | collective-permute-start | bytes 393224 | tf_op jit(solution)/shard_map/ppermute | solution.py:452
  104.0 6.4 %collective-permute-start.35 = (bf16[16,4096]{1,0:T(8,128)(2,1)S(1)}, bf16[16,4096]{1,0:T(8,128)(2,1)S(1)}, u32[]{:S(2)}, u32[]{:S(2)}) collective-permute-start(bf16[16,4096]{1,0:T(8,128)(2,1)S(1)} %shard_map.131.refs_0_), channel_id=1, source_target_pairs={{0,2},{1,3},{2,0},{3,1},{4,6},{5,7},{6,4},{7,5},{8,10},{9,11},{10,... | collective-permute-start | bytes 393224 | tf_op jit(solution)/shard_map/ppermute | solution.py:65
  104.7 7.2 %collective-permute-start.36 = (bf16[16,4096]{1,0:T(8,128)(2,1)S(1)}, bf16[16,4096]{1,0:T(8,128)(2,1)S(1)}, u32[]{:S(2)}, u32[]{:S(2)}) collective-permute-start(bf16[16,4096]{1,0:T(8,128)(2,1)S(1)} %shard_map.132.refs_1_), channel_id=1, source_target_pairs={{0,2},{1,3},{2,0},{3,1},{4,6},{5,7},{6,4},{7,5},{8,10},{9,11},{10,... | collective-permute-start | bytes 393224 | tf_op jit(solution)/shard_map/ppermute | solution.py:65
  106.2 5.6 %collective-permute-start.33 = (bf16[16,4096]{1,0:T(8,128)(2,1)S(1)}, bf16[16,4096]{1,0:T(8,128)(2,1)S(1)}, u32[]{:S(2)}, u32[]{:S(2)}) collective-permute-start(bf16[16,4096]{1,0:T(8,128)(2,1)S(1)} %shard_map.131.refs_0_), channel_id=1, source_target_pairs={{0,1},{1,0},{2,3},{3,2},{4,5},{5,4},{6,7},{7,6},{8,9},{9,8},{10,11... | collective-permute-start | bytes 393224 | tf_op jit(solution)/shard_map/ppermute | solution.py:65
  106.2 5.6 %collective-permute-start.34 = (bf16[16,4096]{1,0:T(8,128)(2,1)S(1)}, bf16[16,4096]{1,0:T(8,128)(2,1)S(1)}, u32[]{:S(2)}, u32[]{:S(2)}) collective-permute-start(bf16[16,4096]{1,0:T(8,128)(2,1)S(1)} %shard_map.132.refs_1_), channel_id=1, source_target_pairs={{0,1},{1,0},{2,3},{3,2},{4,5},{5,4},{6,7},{7,6},{8,9},{9,8},{10,11... | collective-permute-start | bytes 393224 | tf_op jit(solution)/shard_map/ppermute | solution.py:65
  110.5 1.4 %collective-permute-start.37 = (bf16[16,4096]{1,0:T(8,128)(2,1)S(1)}, bf16[16,4096]{1,0:T(8,128)(2,1)S(1)}, u32[]{:S(2)}, u32[]{:S(2)}) collective-permute-start(bf16[16,4096]{1,0:T(8,128)(2,1)S(1)} %collective-permute-done.35.refs_4_), channel_id=1, source_target_pairs={{0,1},{1,0},{2,3},{3,2},{4,5},{5,4},{6,7},{7,6},{8,9},{9,8},{10,11... | collective-permute-start | bytes 393224 | tf_op jit(solution)/shard_map/ppermute | solution.py:65
  111.9 1.3 %collective-permute-start.38 = (bf16[16,4096]{1,0:T(8,128)(2,1)S(1)}, bf16[16,4096]{1,0:T(8,128)(2,1)S(1)}, u32[]{:S(2)}, u32[]{:S(2)}) collective-permute-start(bf16[16,4096]{1,0:T(8,128)(2,1)S(1)} %collective-permute-done.36.refs_5_), channel_id=1, source_target_pairs={{0,1},{1,0},{2,3},{3,2},{4,5},{5,4},{6,7},{7,6},{8,9},{9,8},{10,11... | collective-permute-start | bytes 393224 | tf_op jit(solution)/shard_map/ppermute | solution.py:65
  117.8 1.6 %collective-permute-start.39 = (bf16[32,4096]{1,0:T(8,128)(2,1)S(1)}, bf16[32,4096]{1,0:T(8,128)(2,1)S(1)}, u32[]{:S(2)}, u32[]{:S(2)}) collective-permute-start(bf16[32,4096]{1,0:T(8,128)(2,1)S(1)} %get-tuple-element.169), channel_id=1, source_target_pairs={{0,1},{1,0},{2,3},{3,2},{4,5},{5,4},{6,7},{7,6},{8,9},{9,8},{10,11... | collective-permute-start | bytes 786440 | tf_op jit(solution)/shard_map/ppermute | solution.py:65
  119.5 5.6 %collective-permute-start.40 = (bf16[16,4096]{1,0:T(8,128)(2,1)S(1)}, bf16[16,4096]{1,0:T(8,128)(2,1)S(1)}, u32[]{:S(2)}, u32[]{:S(2)}) collective-permute-start(bf16[16,4096]{1,0:T(8,128)(2,1)S(1)} %slice.59), channel_id=1, source_target_pairs={{0,2},{1,3},{2,0},{3,1},{4,6},{5,7},{6,4},{7,5},{8,10},{9,11},{10,... | collective-permute-start | bytes 393224 | tf_op jit(solution)/shard_map/ppermute | solution.py:65
  125.2 4.6 %collective-permute-start.41 = (bf16[4,4096]{1,0:T(4,128)(2,1)S(1)}, bf16[4,4096]{1,0:T(4,128)(2,1)S(1)}, u32[]{:S(2)}, u32[]{:S(2)}) collective-permute-start(bf16[4,4096]{1,0:T(4,128)(2,1)S(1)} %get-tuple-element.179), channel_id=1, source_target_pairs={{0,4},{4,0},{8,12},{12,8},{1,5},{5,1},{9,13},{13,9},{2,6},{6,2},{1... | collective-permute-start | bytes 98312 | tf_op jit(solution)/shard_map/ppermute | solution.py:65
  125.3 5.9 %collective-permute-start.43 = (bf16[4,4096]{1,0:T(4,128)(2,1)S(1)}, bf16[4,4096]{1,0:T(4,128)(2,1)S(1)}, u32[]{:S(2)}, u32[]{:S(2)}) collective-permute-start(bf16[4,4096]{1,0:T(4,128)(2,1)S(1)} %get-tuple-element.180), channel_id=1, source_target_pairs={{0,12},{4,8},{8,4},{12,0},{1,13},{5,9},{9,5},{13,1},{2,14},{6,10},... | collective-permute-start | bytes 98312 | tf_op jit(solution)/shard_map/ppermute | solution.py:65
  125.4 6.3 %collective-permute-start.42 = (bf16[4,4096]{1,0:T(4,128)(2,1)S(1)}, bf16[4,4096]{1,0:T(4,128)(2,1)S(1)}, u32[]{:S(2)}, u32[]{:S(2)}) collective-permute-start(bf16[4,4096]{1,0:T(4,128)(2,1)S(1)} %get-tuple-element.181), channel_id=1, source_target_pairs={{0,8},{4,12},{8,0},{12,4},{1,9},{5,13},{9,1},{13,5},{2,10},{6,14},... | collective-permute-start | bytes 98312 | tf_op jit(solution)/shard_map/ppermute | solution.py:65

commit v5 on v4

--- a/solution.py
+++ b/solution.py
@@ -14,7 +14,7 @@
 BF = jnp.bfloat16
 F32 = jnp.float32
 MEBI = 1024 * 1024
-BESIDE_THE_GATHER = 32 * MEBI
+LIGHT = pl.CostEstimate(flops=1, bytes_accessed=1, transcendentals=0)
 NN = (((1,), (0,)), ((), ()))
 NT = (((1,), (1,)), ((), ()))
 SCALE = 1.0 / math.sqrt(HD)
@@ -37,27 +37,21 @@
     return jnp.where(is_kept, KEEP_SCALE, 0.0).astype(F32)
 
 
-def prepare_kernel(share, seeds, inputs, cotangent, factor, *refs):
-    targets, sems = refs[:-1], refs[-1]
+def factor_kernel(share, seeds, factor):
     rows, dim = factor.shape
-    chunks = len(targets) // 2
-    size = rows // chunks
     owner = lax.axis_index("mp")
-    micro = lax.div(owner, share)
-    first = pl.multiple_of(lax.rem(owner, share) * rows, rows)
-    copies = []
-    for k, target in enumerate(targets):
-        source = inputs if k < chunks else cotangent
-        tokens = pl.ds(first + k % chunks * size, size)
-        copies.append(pltpu.make_async_copy(source.at[micro, tokens], target, sems.at[k]))
-    for copy in copies:
-        copy.start()
+    seed = seeds[lax.div(owner, share), 0]
+    first = lax.rem(owner, share) * rows
     width = min(dim, 512)
     for first_col in range(0, dim, width):
         cols = slice(first_col, first_col + width)
-        factor[:, cols] = keep_factor(seeds[micro, 0], first, first_col, (rows, width), dim)
-    for copy in copies:
-        copy.wait()
+        factor[:, cols] = keep_factor(seed, first, first_col, (rows, width), dim)
+
+
+def tokens_of(owner, share, array, first, count):
+    rows = array.shape[1] // share
+    first = pl.multiple_of(lax.rem(owner, share) * rows + first, count)
+    return array[lax.div(owner, share), pl.ds(first, count)]
 
 
 def swap(array, axis, k):
@@ -105,6 +99,23 @@
 
 def picked(step, came, held):
     return jnp.where(lax.axis_index("section") == step, came[...], held[...])
+
+
+def here_kernel(n, *refs):
+    pass
+
+
+def on_hand(*arrays):
+    vmem = pl.BlockSpec(memory_space=pltpu.VMEM)
+    size = sum(math.prod(a.shape) * a.dtype.itemsize for a in arrays)
+    return pl.pallas_call(
+        functools.partial(here_kernel, len(arrays)),
+        out_shape=[jax.ShapeDtypeStruct(a.shape, a.dtype) for a in arrays],
+        in_specs=[vmem] * len(arrays),
+        out_specs=[vmem] * len(arrays),
+        input_output_aliases={k: k for k in range(len(arrays))},
+        compiler_params=pltpu.CompilerParams(vmem_limit_bytes=size + 2 * MEBI),
+    )(*arrays)
 
 
 def store_folds(part, h, src, cols, folds):
@@ -140,9 +151,7 @@
     count = allowed.shape[1]
     tokens = []
     for j in range(n):
-        owner = me ^ j
-        first = pl.multiple_of(lax.rem(owner, share) * count, count)
-        tokens.append(inputs[lax.div(owner, share), pl.ds(first, count)])
+        tokens.append(tokens_of(me ^ j, share, inputs, 0, count))
     query[...] = product(jnp.concatenate(tokens, axis=0), wq[...], NN).astype(BF)
     for tile, toks, srcs, cols in heads_of(n, heads, count, src):
         k, h = divmod(tile.start // src, heads)
@@ -170,16 +179,17 @@
         fold[k * size : (k + 1) * size] = block[...]
 
 
-def first_kernel(n, chunks, factor, *refs):
-    helds, probs, refs = refs[:chunks], refs[chunks : n + chunks], refs[n + chunks :]
-    blocks, (out_fold, *following) = refs[:n], refs[n:]
+def first_kernel(n, chunks, share, factor, inputs, *refs):
+    probs, blocks, (out_fold, *outs) = refs[:n], refs[n : 2 * n], refs[2 * n :]
+    helds, following = outs[:chunks], outs[chunks:]
     pack(blocks, out_fold)
     weights = jnp.concatenate([block[...] for block in probs], axis=0).astype(F32)
     kept = factor[...] * spread(weights, out_fold)
     size = kept.shape[0] // chunks
     for c in range(chunks):
-        total = helds[c][...].astype(F32) + kept[c * size : (c + 1) * size]
-        following[c][...] = total.astype(BF)
+        held = tokens_of(lax.axis_index("mp"), share, inputs, c * size, size)
+        helds[c][...] = held
+        following[c][...] = (held.astype(F32) + kept[c * size : (c + 1) * size]).astype(BF)
 
 
 def pack_kernel(n, *refs):
@@ -202,13 +212,14 @@
 
 
 def turn_kernel(
-    step, c, src, came, held, allowed, factor, query_fold, out_fold, grad, current, kept, before
+    step, c, src, share, came, held, allowed, factor, query_fold, out_fold, cotangent, current, kept, grad, before
 ):
     tokens = picked(step, came, held)
     current[...] = tokens
     probs = softmax_down(product(query_fold[...], tokens, NT), allowed[...], src)
     kept[...] = probs
     factor = part_of(factor, c, tokens.shape[0])
+    grad[...] = tokens_of(lax.axis_index("mp"), share, cotangent, c * tokens.shape[0], tokens.shape[0])
     before[...] = backward(probs, grad[...], factor, query_fold, out_fold, src)
 
 
@@ -298,10 +309,8 @@
         in_specs=[vmem] * len(args),
         out_specs=[vmem] * len(outs),
         scratch_shapes=[pltpu.VMEM(s.shape, s.dtype) for s in scratch],
-        compiler_params=pltpu.CompilerParams(vmem_limit_bytes=size + size // 2 + 4 * MEBI),
-        cost_estimate=pl.CostEstimate(
-            flops=64 * size, bytes_accessed=size, transcendentals=0
-        ),
+        compiler_params=pltpu.CompilerParams(vmem_limit_bytes=size + 3 * MEBI),
+        cost_estimate=pl.CostEstimate(flops=64 * size, bytes_accessed=size, transcendentals=0),
     )(*args)
 
 
@@ -323,26 +332,21 @@
 
     chunks = 2 if rows % 32 == 0 else 1
     wide = ((rows // chunks, dim), BF)
-    anywhere = pl.BlockSpec(memory_space=pl.ANY)
-    vmem = pl.BlockSpec(memory_space=pltpu.VMEM)
-    factor, *tokens = pl.pallas_call(
-        functools.partial(prepare_kernel, share),
-        out_shape=[jax.ShapeDtypeStruct((rows, dim), F32)]
-        + [jax.ShapeDtypeStruct(*wide)] * (2 * chunks),
-        in_specs=[pl.BlockSpec(memory_space=pltpu.SMEM), anywhere, anywhere],
-        out_specs=[vmem] * (1 + 2 * chunks),
-        scratch_shapes=[pltpu.SemaphoreType.DMA((2 * chunks,))],
-        compiler_params=pltpu.CompilerParams(vmem_limit_bytes=4 * MEBI),
-        cost_estimate=pl.CostEstimate(
-            flops=0, bytes_accessed=BESIDE_THE_GATHER, transcendentals=0
-        ),
-    )(seeds, decoder_in, cotangent)
 
     own = memory.reshape(micro_count, dim)
     over_z = [own if a == 0 else swap(own, "section", a) for a in range(sections)]
     over_z = jnp.concatenate(over_z, axis=0)
-    over_z, factor, tokens = lax.optimization_barrier((over_z, factor, tokens))
-    helds, grads = list(tokens[:chunks]), list(tokens[chunks:])
+    factor = pl.pallas_call(
+        functools.partial(factor_kernel, share),
+        out_shape=jax.ShapeDtypeStruct((rows, dim), F32),
+        in_specs=[pl.BlockSpec(memory_space=pltpu.SMEM)],
+        out_specs=pl.BlockSpec(memory_space=pltpu.VMEM),
+        compiler_params=pltpu.CompilerParams(vmem_limit_bytes=4 * MEBI),
+        cost_estimate=LIGHT,
+    )(seeds)
+    over_z, factor, wv_near, wo_near = lax.optimization_barrier(
+        (over_z, factor, *on_hand(wv, wo))
+    )
     pieces = over_mp(over_z)
 
     to_row = jnp.arange(n_mp * src, dtype=jnp.int32)[:, None]
@@ -385,10 +389,15 @@
         functools.partial(values_kernel, n_mp, src, heads),
         [stacked] + [block] * n_mp,
         by_owner,
-        wv,
-        wo,
+        wv_near,
+        wo_near,
         *pieces,
     )
+    def to_owners(blocks):
+        return [part if j == 0 else swap(part, "mp", j) for j, part in enumerate(blocks)]
+
+    out_blocks = to_owners(out_blocks)
+    out_blocks[1], pieces = lax.optimization_barrier((out_blocks[1], pieces))
     keys, *blocks = on_chip(
         functools.partial(keys_kernel, n_mp, src, heads, share),
         [stacked] + [block] * n_mp + [((fold_rows, rows), BF)] * n_mp,
@@ -401,20 +410,20 @@
         scratch=[jax.ShapeDtypeStruct((n_mp * rows, local_cols), BF)],
     )
     query_blocks, own_probs = blocks[:n_mp], blocks[n_mp:]
-    def to_owners(blocks):
-        return [part if j == 0 else swap(part, "mp", j) for j, part in enumerate(blocks)]
-
-    out_blocks = to_owners(out_blocks)
     first_probs = to_owners(own_probs)
+    out_blocks, first_probs, query_blocks = lax.optimization_barrier(
+        (out_blocks, first_probs, query_blocks)
+    )
     query_blocks = to_owners(query_blocks)
-    out_fold, *followings = on_chip(
-        functools.partial(first_kernel, n_mp, chunks),
-        [whole_fold] + [wide] * chunks,
+    out_fold, *outs = on_chip(
+        functools.partial(first_kernel, n_mp, chunks, share),
+        [whole_fold] + [wide] * (2 * chunks),
         factor,
-        *helds,
+        decoder_in,
         *first_probs,
         *out_blocks,
     )
+    helds, followings = outs[:chunks], outs[chunks:]
     (query_fold,) = on_chip(
         functools.partial(pack_kernel, n_mp), [whole_fold], *query_blocks
     )
@@ -432,19 +441,19 @@
                     factor,
                     *folds,
                 )
-    currents, probs, befores = [], [], []
+    currents, probs, grads, befores = [], [], [], []
     for c in range(chunks):
         results = on_chip(
-            functools.partial(turn_kernel, sections - 1, c, src),
-            [wide, (masks[c].shape, F32), wide],
+            functools.partial(turn_kernel, sections - 1, c, src, share),
+            [wide, (masks[c].shape, F32), wide, wide],
                 cames[c],
             helds[c],
             masks[c],
             factor,
             *folds,
-            grads[c],
+            cotangent,
         )
-        for kept, result in zip((currents, probs, befores), results, strict=True):
+        for kept, result in zip((currents, probs, grads, befores), results, strict=True):
             kept.append(result)
 
     out_cols = dim // n_mp
@@ -494,6 +503,8 @@
             )
     gathered = []
     for c in range(chunks):
+        if gathered:
+            cames[c], gathered[-1][1] = lax.optimization_barrier((cames[c], gathered[-1][1]))
         (d_out,) = on_chip(
             functools.partial(dropped_kernel, 0, c), [wide], cames[c], grads[c], factor
         )

time: 133 us -> 128 us (0.962)
  local copies, waits for them, and re-layouts: 8.93 us -> 6.74 us
    ppermute x32, waiting for transfers between devices: 38.4 us -> 40.6 us  [swap(): return lax.ppermute(array, axis, [(i, i ^ k) for i in range(size)])]
    unnamed x19 -> x17, local copies, waits for them, and re-layouts: 7.59 us -> 5.4 us
    ppermute x6, waiting for transfers between devices: 19.5 us -> 17.8 us  [per_device(): lax.ppermute(part, 'section', [(step, step - 1)])]
  transfers between devices with their start and end apart: 44 -> 44, of which waited for: 17 -> 19; matrix products, arithmetic and copies ran while one was open for 3% -> 5% of each run, Pallas kernels for 13% -> 12%
where the time goes in v5:
time: 128 us
  waiting for transfers between devices  58.5 us (46%)
  starting transfers between devices  37.1 us (29%)
  Pallas kernels  22.4 us (18%)
  local copies, waits for them, and re-layouts  6.74 us (5%)
  other arithmetic  2.14 us (2%)
    ppermute x32, waiting for transfers between devices, swap(): return lax.ppermute(array, axis, [(i, i ^ k) for i in range(size)])  40.6 us
    ppermute x32, starting transfers between devices, swap(): return lax.ppermute(array, axis, [(i, i ^ k) for i in range(size)])  24.6 us
    pallas_call x20, Pallas kernels, on_chip(): pl.pallas_call(body, out_shape=outs, in_specs=[vmem] * len(args), out_spe...  21.6 us
    ppermute x6, waiting for transfers between devices, per_device(): lax.ppermute(part, 'section', [(step, step - 1)])  17.8 us
    ppermute x6, starting transfers between devices, per_device(): lax.ppermute(part, 'section', [(step - 1, step)])  6.77 us
    ppermute x6, starting transfers between devices, per_device(): lax.ppermute(part, 'section', [(step, step - 1)])  5.69 us
    unnamed x17, local copies, waits for them, and re-layouts  5.4 us
  transfers between devices with their start and end apart: 44, of which 19 were waited for; matrix products, arithmetic and copies ran while one was open for 5% of the time, Pallas kernels for 12%

profile of v5, /device:TPU:0, one launch (start us, length us, event | category | flops | bytes accessed | tf_op | source)
XLA Modules:
  0.0 128.0 jit_solution(5499379549292800653)
XLA Ops:
  0.6 3.1 %collective-permute-start = (bf16[4,4096]{1,0:T(4,128)(2,1)}, bf16[4,4096]{1,0:T(4,128)(2,1)S(1)}, u32[]{:S(2)}, u32[]{:S(2)}) collective-permute-start(bf16[4,4096]{1,0:T(4,128)(2,1)} %bitcast.38), channel_id=1, source_target_pairs={{0,4},{4,0},{8,12},{12,8},{1,5},{5,1},{9,13},{13,9},{2,6},{6,2},{1... | collective-permute-start | bytes 98312 | tf_op jit(solution)/shard_map/ppermute | solution.py:59
  3.7 2.6 %collective-permute-start.1 = (bf16[4,4096]{1,0:T(4,128)(2,1)}, bf16[4,4096]{1,0:T(4,128)(2,1)S(1)}, u32[]{:S(2)}, u32[]{:S(2)}) collective-permute-start(bf16[4,4096]{1,0:T(4,128)(2,1)} %bitcast.39), channel_id=1, source_target_pairs={{0,8},{4,12},{8,0},{12,4},{1,9},{5,13},{9,1},{13,5},{2,10},{6,14},... | collective-permute-start | bytes 98312 | tf_op jit(solution)/shard_map/ppermute | solution.py:59
  6.3 0.9 reduce_window_sum.11
  7.6 0.8 fusion.12
  8.5 0.7 copy.15.seeds
  9.6 0.8 shard_map.113.factor
  10.4 2.3 %copy.16.refs_0_ = bf16[4096,512]{1,0:T(8,128)(2,1)S(1)} copy(bf16[4096,512]{1,0:T(8,128)(2,1)} %bitcast.30) | data formatting | bytes 8388608
  12.8 1.1 copy-done.3
  14.4 0.7 copy-done.6
  15.2 1.8 %collective-permute-start.4 = (bf16[16,4096]{1,0:T(8,128)(2,1)S(1)}, bf16[16,4096]{1,0:T(8,128)(2,1)S(1)}, u32[]{:S(2)}, u32[]{:S(2)}) collective-permute-start(bf16[16,4096]{1,0:T(8,128)(2,1)S(1)} %pad_maximum_fusion.refs_0_), channel_id=1, source_target_pairs={{0,2},{1,3},{2,0},{3,1},{4,6},{5,7},{6,4},{7,5},{8,10},{9,11},{10,... | collective-permute-start | bytes 393224 | tf_op jit(solution)/shard_map/ppermute | solution.py:59
  17.0 3.2 %collective-permute-done.4.refs_2_ = bf16[16,4096]{1,0:T(8,128)(2,1)S(1)} collective-permute-done((bf16[16,4096]{1,0:T(8,128)(2,1)S(1)}, bf16[16,4096]{1,0:T(8,128)(2,1)S(1)}, u32[]{:S(2)}, u32[]{:S(2)}) %collective-permute-start.4) | collective-permute-done | bytes 131104 | tf_op jit(solution)/shard_map/ppermute | solution.py:59
  20.4 1.2 collective-permute-done.5.refs_3_
  21.6 1.8 %shard_map.115 = (bf16[64,512]{1,0:T(8,128)(2,1)S(1)}, bf16[32,4096]{1,0:T(8,128)(2,1)S(1)}, bf16[32,4096]{1,0:T(8,128)(2,1)S(1)}, bf16[32,4096]{1,0:T(8,128)(2,1)S(1)}, bf16[32,4096]{1,0:T(8,128)(2,1)S(1)}) custom-call(bf16[64,64]{1,0:T(8,128)(2,1)S(1)} %get-tuple-element.107.by_owner, bf16[4096,512]{1,0:T(8,128)(2,1)S(1)} %get-tuple-element.108.wv, ...), custom_call_target="tpu_custom_call" | custom-call | flops 642252800 | bytes 10035200 | tf_op jit(solution)/shard_map/pallas_call | solution.py:306
  23.6 1.7 %collective-permute-start.7 = (bf16[32,4096]{1,0:T(8,128)(2,1)S(1)}, bf16[32,4096]{1,0:T(8,128)(2,1)S(1)}, u32[]{:S(2)}, u32[]{:S(2)}) collective-permute-start(bf16[32,4096]{1,0:T(8,128)(2,1)S(1)} %get-tuple-element.114), channel_id=1, source_target_pairs={{0,2},{1,3},{2,0},{3,1},{4,6},{5,7},{6,4},{7,5},{8,10},{9,11},{10,... | collective-permute-start | bytes 786440 | tf_op jit(solution)/shard_map/ppermute | solution.py:59
  25.3 3.0 %shard_map.116 = (bf16[64,512]{1,0:T(8,128)(2,1)S(1)}, bf16[32,4096]{1,0:T(8,128)(2,1)S(1)}, bf16[32,4096]{1,0:T(8,128)(2,1)S(1)}, bf16[32,4096]{1,0:T(8,128)(2,...) custom-call(bf16[64,64]{1,0:T(8,128)(2,1)S(1)} %get-tuple-element.10, ...), custom_call_target="tpu_custom_call" | custom-call | flops 719323136 | bytes 11239424 | tf_op jit(solution)/shard_map/pallas_call | solution.py:306
  28.3 1.7 %collective-permute-start.10 = (bf16[32,32]{1,0:T(8,128)(2,1)S(1)}, bf16[32,32]{1,0:T(8,128)(2,1)S(1)}, u32[]{:S(2)}, u32[]{:S(2)}) collective-permute-start(bf16[32,32]{1,0:T(8,128)(2,1)S(1)} %get-tuple-element.123), channel_id=1, source_target_pairs={{0,2},{1,3},{2,0},{3,1},{4,6},{5,7},{6,4},{7,5},{8,10},{9,11},{10,... | collective-permute-start | bytes 6152 | tf_op jit(solution)/shard_map/ppermute | solution.py:59
  30.5 2.2 %collective-permute-done.7.refs_6_ = bf16[32,4096]{1,0:T(8,128)(2,1)S(1)} collective-permute-done((bf16[32,4096]{1,0:T(8,128)(2,1)S(1)}, bf16[32,4096]{1,0:T(8,128)(2,1)S(1)}, u32[]{:S(2)}, u32[]{:S(2)}) %collective-permute-start.7) | collective-permute-done | bytes 262176 | tf_op jit(solution)/shard_map/ppermute | solution.py:59
  32.7 4.5 %collective-permute-done.8.refs_7_ = bf16[32,4096]{1,0:T(8,128)(2,1)S(1)} collective-permute-done((bf16[32,4096]{1,0:T(8,128)(2,1)S(1)}, bf16[32,4096]{1,0:T(8,128)(2,1)S(1)}, u32[]{:S(2)}, u32[]{:S(2)}) %collective-permute-start.8) | collective-permute-done | bytes 262176 | tf_op jit(solution)/shard_map/ppermute | solution.py:59
  37.2 0.8 collective-permute-done.10.refs_2_
  38.2 1.7 %collective-permute-start.14 = (bf16[32,4096]{1,0:T(8,128)(2,1)S(1)}, bf16[32,4096]{1,0:T(8,128)(2,1)S(1)}, u32[]{:S(2)}, u32[]{:S(2)}) collective-permute-start(bf16[32,4096]{1,0:T(8,128)(2,1)S(1)} %get-tuple-element.142), channel_id=1, source_target_pairs={{0,2},{1,3},{2,0},{3,1},{4,6},{5,7},{6,4},{7,5},{8,10},{9,11},{10,... | collective-permute-start | bytes 786440 | tf_op jit(solution)/shard_map/ppermute | solution.py:59
  40.3 2.8 %collective-permute-start.19 = (bf16[16,4096]{1,0:T(8,128)(2,1)S(1)}, bf16[16,4096]{1,0:T(8,128)(2,1)S(1)}, u32[]{:S(2)}, u32[]{:S(2)}) collective-permute-start(bf16[16,4096]{1,0:T(8,128)(2,1)S(1)} %get-tuple-element.150), channel_id=1, source_target_pairs={{0,4},{1,5},{2,6},{3,7},{16,20},{17,21},{18,22},{19,23}} | collective-permute-start | bytes 393224 | tf_op jit(solution)/shard_map/ppermute | solution.py:432
  43.1 1.3 %collective-permute-start.12 = (bf16[16,4096]{1,0:T(8,128)(2,1)S(1)}, bf16[16,4096]{1,0:T(8,128)(2,1)S(1)}, u32[]{:S(2)}, u32[]{:S(2)}) collective-permute-start(bf16[16,4096]{1,0:T(8,128)(2,1)S(1)} %get-tuple-element.137), channel_id=1, source_target_pairs={{0,4},{1,5},{2,6},{3,7},{16,20},{17,21},{18,22},{19,23}} | collective-permute-start | bytes 393224 | tf_op jit(solution)/shard_map/ppermute | solution.py:432
  44.4 2.9 %collective-permute-done.14.refs_2_ = bf16[32,4096]{1,0:T(8,128)(2,1)S(1)} collective-permute-done((bf16[32,4096]{1,0:T(8,128)(2,1)S(1)}, bf16[32,4096]{1,0:T(8,128)(2,1)S(1)}, u32[]{:S(2)}, u32[]{:S(2)}) %collective-permute-start.14) | collective-permute-done | bytes 262176 | tf_op jit(solution)/shard_map/ppermute | solution.py:59
  47.3 4.7 %collective-permute-done.15.refs_3_ = bf16[32,4096]{1,0:T(8,128)(2,1)S(1)} collective-permute-done((bf16[32,4096]{1,0:T(8,128)(2,1)S(1)}, bf16[32,4096]{1,0:T(8,128)(2,1)S(1)}, u32[]{:S(2)}, u32[]{:S(2)}) %collective-permute-start.15) | collective-permute-done | bytes 262176 | tf_op jit(solution)/shard_map/ppermute | solution.py:59
  52.0 1.0 shard_map.122
  53.0 0.7 collective-permute-start.20
  53.7 1.0 shard_map.119
  54.7 0.7 collective-permute-start.16
  55.4 1.0 shard_map.123
  56.4 0.7 collective-permute-start.21
  57.0 1.0 shard_map.120
  58.0 0.7 collective-permute-start.17
  58.7 1.0 shard_map.124
  59.7 0.7 collective-permute-start.22
  60.4 1.0 shard_map.121
  61.4 0.7 collective-permute-start.18
  62.5 1.8 %collective-permute-start.28 = (bf16[32,4096]{1,0:T(8,128)(2,1)S(1)}, bf16[32,4096]{1,0:T(8,128)(2,1)S(1)}, u32[]{:S(2)}, u32[]{:S(2)}) collective-permute-start(bf16[32,4096]{1,0:T(8,128)(2,1)S(1)} %get-tuple-element.189.refs_0_), channel_id=1, source_target_pairs={{0,2},{1,3},{2,0},{3,1},{4,6},{5,7},{6,4},{7,5},{8,10},{9,11},{10,... | collective-permute-start | bytes 786440 | tf_op jit(solution)/shard_map/ppermute | solution.py:59
  64.2 1.0 shard_map.127
  65.2 0.7 collective-permute-start.24
  66.0 1.0 shard_map.126
  66.9 0.8 collective-permute-start.23
  68.2 1.5 %collective-permute-start.27 = (bf16[32,1024]{1,0:T(8,128)(2,1)S(1)}, bf16[32,1024]{1,0:T(8,128)(2,1)S(1)}, u32[]{:S(2)}, u32[]{:S(2)}) collective-permute-start(bf16[32,1024]{1,0:T(8,128)(2,1)S(1)} %get-tuple-element.176), channel_id=1, source_target_pairs={{0,3},{1,2},{2,1},{3,0},{4,7},{5,6},{6,5},{7,4},{8,11},{9,10},{10,... | collective-permute-start | bytes 196616 | tf_op jit(solution)/shard_map/ppermute | solution.py:59
  69.7 3.0 %collective-permute-done.26.refs_2_ = bf16[32,1024]{1,0:T(8,128)(2,1)S(1)} collective-permute-done((bf16[32,1024]{1,0:T(8,128)(2,1)S(1)}, bf16[32,1024]{1,0:T(8,128)(2,1)S(1)}, u32[]{:S(2)}, u32[]{:S(2)}) %collective-permute-start.26) | collective-permute-done | bytes 65568 | tf_op jit(solution)/shard_map/ppermute | solution.py:59
  72.7 0.9 collective-permute-done.27.refs_3_
  74.2 1.0 shard_map.129
  75.1 1.3 %collective-permute-start.30 = (bf16[16,4096]{1,0:T(8,128)(2,1)S(1)}, bf16[16,4096]{1,0:T(8,128)(2,1)S(1)}, u32[]{:S(2)}, u32[]{:S(2)}) collective-permute-start(bf16[16,4096]{1,0:T(8,128)(2,1)S(1)} %get-tuple-element.183), channel_id=1, source_target_pairs={{4,0},{5,1},{6,2},{7,3},{20,16},{21,17},{22,18},{23,19}} | collective-permute-start | bytes 393224 | tf_op jit(solution)/shard_map/ppermute | solution.py:461
  76.4 1.0 shard_map.128
  77.4 1.6 %collective-permute-start.29 = (bf16[16,4096]{1,0:T(8,128)(2,1)S(1)}, bf16[16,4096]{1,0:T(8,128)(2,1)S(1)}, u32[]{:S(2)}, u32[]{:S(2)}) collective-permute-start(bf16[16,4096]{1,0:T(8,128)(2,1)S(1)} %get-tuple-element.180), channel_id=1, source_target_pairs={{4,0},{5,1},{6,2},{7,3},{20,16},{21,17},{22,18},{23,19}} | collective-permute-start | bytes 393224 | tf_op jit(solution)/shard_map/ppermute | solution.py:461
  79.0 0.7 shard_map.130
  79.7 0.9 shard_map.131
  80.6 15.2 %collective-permute-done.30.came = bf16[16,4096]{1,0:T(8,128)(2,1)S(1)} collective-permute-done((bf16[16,4096]{1,0:T(8,128)(2,1)S(1)}, bf16[16,4096]{1,0:T(8,128)(2,1)S(1)}, u32[]{:S(2)}, u32[]{:S(2)}) %collective-permute-start.30) | collective-permute-done | bytes 131104 | tf_op jit(solution)/shard_map/ppermute | solution.py:461
  95.8 2.6 %collective-permute-done.29.came = bf16[16,4096]{1,0:T(8,128)(2,1)S(1)} collective-permute-done((bf16[16,4096]{1,0:T(8,128)(2,1)S(1)}, bf16[16,4096]{1,0:T(8,128)(2,1)S(1)}, u32[]{:S(2)}, u32[]{:S(2)}) %collective-permute-start.29) | collective-permute-done | bytes 131104 | tf_op jit(solution)/shard_map/ppermute | solution.py:461
  99.1 0.7 collective-permute-done.33.refs_2_
  99.9 0.8 collective-permute-start.36
  100.7 4.2 %collective-permute-done.35.refs_4_ = bf16[16,4096]{1,0:T(8,128)(2,1)S(1)} collective-permute-done((bf16[16,4096]{1,0:T(8,128)(2,1)S(1)}, bf16[16,4096]{1,0:T(8,128)(2,1)S(1)}, u32[]{:S(2)}, u32[]{:S(2)}) %collective-permute-start.35) | collective-permute-done | bytes 131104 | tf_op jit(solution)/shard_map/ppermute | solution.py:59
  104.9 2.4 %collective-permute-done.36.refs_5_ = bf16[16,4096]{1,0:T(8,128)(2,1)S(1)} collective-permute-done((bf16[16,4096]{1,0:T(8,128)(2,1)S(1)}, bf16[16,4096]{1,0:T(8,128)(2,1)S(1)}, u32[]{:S(2)}, u32[]{:S(2)}) %collective-permute-start.36) | collective-permute-done | bytes 131104 | tf_op jit(solution)/shard_map/ppermute | solution.py:59
  107.3 1.3 %collective-permute-done.38.refs_7_ = bf16[16,4096]{1,0:T(8,128)(2,1)S(1)} collective-permute-done((bf16[16,4096]{1,0:T(8,128)(2,1)S(1)}, bf16[16,4096]{1,0:T(8,128)(2,1)S(1)}, u32[]{:S(2)}, u32[]{:S(2)}) %collective-permute-start.38) | collective-permute-done | bytes 131104 | tf_op jit(solution)/shard_map/ppermute | solution.py:59
  108.6 4.6 %shard_map.134 = (f32[32,4096]{1,0:T(8,128)S(1)}, bf16[32,4096]{1,0:T(8,128)(2,1)S(1)}) custom-call(bf16[64,512]{1,0:T(8,128)(2,1)S(1)} %get-tuple-element.188.keys, bf16[64,512]{1,0:T(8,128)(2,1)S(1)} %get-tuple-element.194.values, bf16[128,512]{1,0:T(8,128)(2,1)S(1)} %get-tuple-element.195.query, f32[128,32]{1,0:T(8,128)S(1)} %get-tuple-element.196.probs, ...), custom_call_target="tpu_custom_call" | custom-call | flops 957874176 | bytes 14966784 | tf_op jit(solution)/shard_map/pallas_call | solution.py:306
  113.5 1.4 %collective-permute-done.39 = bf16[32,4096]{1,0:T(8,128)(2,1)S(1)} collective-permute-done((bf16[32,4096]{1,0:T(8,128)(2,1)S(1)}, bf16[32,4096]{1,0:T(8,128)(2,1)S(1)}, u32[]{:S(2)}, u32[]{:S(2)}) %collective-permute-start.39) | collective-permute-done | bytes 262176 | tf_op jit(solution)/shard_map/ppermute | solution.py:59
  115.5 5.0 %collective-permute-done.40 = bf16[16,4096]{1,0:T(8,128)(2,1)S(1)} collective-permute-done((bf16[16,4096]{1,0:T(8,128)(2,1)S(1)}, bf16[16,4096]{1,0:T(8,128)(2,1)S(1)}, u32[]{:S(2)}, u32[]{:S(2)}) %collective-permute-start.40) | collective-permute-done | bytes 131104 | tf_op jit(solution)/shard_map/ppermute | solution.py:59
  120.8 4.3 %collective-permute-start.43 = (bf16[4,4096]{1,0:T(4,128)(2,1)S(1)}, bf16[4,4096]{1,0:T(4,128)(2,1)S(1)}, u32[]{:S(2)}, u32[]{:S(2)}) collective-permute-start(bf16[4,4096]{1,0:T(4,128)(2,1)S(1)} %get-tuple-element.216), channel_id=1, source_target_pairs={{0,12},{4,8},{8,4},{12,0},{1,13},{5,9},{9,5},{13,1},{2,14},{6,10},... | collective-permute-start | bytes 98312 | tf_op jit(solution)/shard_map/ppermute | solution.py:59
  125.1 0.7 collective-permute-done.42
  125.8 1.6 %collective-permute-done.43 = bf16[4,4096]{1,0:T(4,128)(2,1)S(1)} collective-permute-done((bf16[4,4096]{1,0:T(4,128)(2,1)S(1)}, bf16[4,4096]{1,0:T(4,128)(2,1)S(1)}, u32[]{:S(2)}, u32[]{:S(2)}) %collective-permute-start.43) | collective-permute-done | bytes 32800 | tf_op jit(solution)/shard_map/ppermute | solution.py:59
  127.3 0.7 fusion.2
  (92 shorter events, 6.1 us)
Async XLA Ops:
  0.6 13.8 %collective-permute-start = (bf16[4,4096]{1,0:T(4,128)(2,1)}, bf16[4,4096]{1,0:T(4,128)(2,1)S(1)}, u32[]{:S(2)}, u32[]{:S(2)}) collective-permute-start(bf16[4,4096]{1,0:T(4,128)(2,1)} %bitcast.38), channel_id=1, source_target_pairs={{0,4},{4,0},{8,12},{12,8},{1,5},{5,1},{9,13},{13,9},{2,6},{6,2},{1... | collective-permute-start | bytes 98312 | tf_op jit(solution)/shard_map/ppermute | solution.py:59
  3.7 10.7 %collective-permute-start.1 = (bf16[4,4096]{1,0:T(4,128)(2,1)}, bf16[4,4096]{1,0:T(4,128)(2,1)S(1)}, u32[]{:S(2)}, u32[]{:S(2)}) collective-permute-start(bf16[4,4096]{1,0:T(4,128)(2,1)} %bitcast.39), channel_id=1, source_target_pairs={{0,8},{4,12},{8,0},{12,4},{1,9},{5,13},{9,1},{13,5},{2,10},{6,14},... | collective-permute-start | bytes 98312 | tf_op jit(solution)/shard_map/ppermute | solution.py:59
  6.3 8.1 %collective-permute-start.2 = (bf16[4,4096]{1,0:T(4,128)(2,1)}, bf16[4,4096]{1,0:T(4,128)(2,1)S(1)}, u32[]{:S(2)}, u32[]{:S(2)}) collective-permute-start(bf16[4,4096]{1,0:T(4,128)(2,1)} %bitcast.40), channel_id=1, source_target_pairs={{0,12},{4,8},{8,4},{12,0},{1,13},{5,9},{9,5},{13,1},{2,14},{6,10},... | collective-permute-start | bytes 98312 | tf_op jit(solution)/shard_map/ppermute | solution.py:59
  10.4 3.5 %copy-start.3 = (bf16[1,512,4096]{2,1,0:T(8,128)(2,1)S(1)}, bf16[1,512,4096]{2,1,0:T(8,128)(2,1)}, u32[]{:S(2)}) copy-start(bf16[1,512,4096]{2,1,0:T(8,128)(2,1)} %param.19) | copy-start | bytes 12582916
  14.4 0.8 copy-start.6
  14.4 10.9 %copy-start.4 = (bf16[4,32,4096]{2,1,0:T(8,128)(2,1)S(1)}, bf16[4,32,4096]{2,1,0:T(8,128)(2,1)}, u32[]{:S(2)}) copy-start(bf16[4,32,4096]{2,1,0:T(8,128)(2,1)} %inputs.3) | copy-start | bytes 3145732
  15.2 5.0 %collective-permute-start.4 = (bf16[16,4096]{1,0:T(8,128)(2,1)S(1)}, bf16[16,4096]{1,0:T(8,128)(2,1)S(1)}, u32[]{:S(2)}, u32[]{:S(2)}) collective-permute-start(bf16[16,4096]{1,0:T(8,128)(2,1)S(1)} %pad_maximum_fusion.refs_0_), channel_id=1, source_target_pairs={{0,2},{1,3},{2,0},{3,1},{4,6},{5,7},{6,4},{7,5},{8,10},{9,11},{10,... | collective-permute-start | bytes 393224 | tf_op jit(solution)/shard_map/ppermute | solution.py:59
  17.0 3.4 %collective-permute-start.3 = (bf16[16,4096]{1,0:T(8,128)(2,1)S(1)}, bf16[16,4096]{1,0:T(8,128)(2,1)S(1)}, u32[]{:S(2)}, u32[]{:S(2)}) collective-permute-start(bf16[16,4096]{1,0:T(8,128)(2,1)S(1)} %pad_maximum_fusion.refs_0_), channel_id=1, source_target_pairs={{0,1},{1,0},{2,3},{3,2},{4,5},{5,4},{6,7},{7,6},{8,9},{9,8},{10,11... | collective-permute-start | bytes 393224 | tf_op jit(solution)/shard_map/ppermute | solution.py:59
  20.3 1.3 %collective-permute-start.5 = (bf16[16,4096]{1,0:T(8,128)(2,1)S(1)}, bf16[16,4096]{1,0:T(8,128)(2,1)S(1)}, u32[]{:S(2)}, u32[]{:S(2)}) collective-permute-start(bf16[16,4096]{1,0:T(8,128)(2,1)S(1)} %collective-permute-done.4.refs_2_), channel_id=1, source_target_pairs={{0,1},{1,0},{2,3},{3,2},{4,5},{5,4},{6,7},{7,6},{8,9},{9,8},{10,11... | collective-permute-start | bytes 393224 | tf_op jit(solution)/shard_map/ppermute | solution.py:59
  20.4 5.0 %copy-start = (bf16[1,4096,512]{2,1,0:T(8,128)(2,1)S(1)}, bf16[1,4096,512]{2,1,0:T(8,128)(2,1)}, u32[]{:S(2)}) copy-start(bf16[1,4096,512]{2,1,0:T(8,128)(2,1)} %param.16) | copy-start | bytes 12582916
  20.4 5.0 %copy-start.1 = (bf16[1,4096,512]{2,1,0:T(8,128)(2,1)S(1)}, bf16[1,4096,512]{2,1,0:T(8,128)(2,1)}, u32[]{:S(2)}) copy-start(bf16[1,4096,512]{2,1,0:T(8,128)(2,1)} %param.17) | copy-start | bytes 12582916
  23.4 1.9 %collective-permute-start.6 = (bf16[32,4096]{1,0:T(8,128)(2,1)S(1)}, bf16[32,4096]{1,0:T(8,128)(2,1)S(1)}, u32[]{:S(2)}, u32[]{:S(2)}) collective-permute-start(bf16[32,4096]{1,0:T(8,128)(2,1)S(1)} %get-tuple-element.112), channel_id=1, source_target_pairs={{0,1},{1,0},{2,3},{3,2},{4,5},{5,4},{6,7},{7,6},{8,9},{9,8},{10,11... | collective-permute-start | bytes 786440 | tf_op jit(solution)/shard_map/ppermute | solution.py:59
  23.6 9.1 %collective-permute-start.7 = (bf16[32,4096]{1,0:T(8,128)(2,1)S(1)}, bf16[32,4096]{1,0:T(8,128)(2,1)S(1)}, u32[]{:S(2)}, u32[]{:S(2)}) collective-permute-start(bf16[32,4096]{1,0:T(8,128)(2,1)S(1)} %get-tuple-element.114), channel_id=1, source_target_pairs={{0,2},{1,3},{2,0},{3,1},{4,6},{5,7},{6,4},{7,5},{8,10},{9,11},{10,... | collective-permute-start | bytes 786440 | tf_op jit(solution)/shard_map/ppermute | solution.py:59
  25.3 11.9 %collective-permute-start.8 = (bf16[32,4096]{1,0:T(8,128)(2,1)S(1)}, bf16[32,4096]{1,0:T(8,128)(2,1)S(1)}, u32[]{:S(2)}, u32[]{:S(2)}) collective-permute-start(bf16[32,4096]{1,0:T(8,128)(2,1)S(1)} %get-tuple-element.115), channel_id=1, source_target_pairs={{0,3},{1,2},{2,1},{3,0},{4,7},{5,6},{6,5},{7,4},{8,11},{9,10},{10,... | collective-permute-start | bytes 786440 | tf_op jit(solution)/shard_map/ppermute | solution.py:59
  28.3 9.7 %collective-permute-start.10 = (bf16[32,32]{1,0:T(8,128)(2,1)S(1)}, bf16[32,32]{1,0:T(8,128)(2,1)S(1)}, u32[]{:S(2)}, u32[]{:S(2)}) collective-permute-start(bf16[32,32]{1,0:T(8,128)(2,1)S(1)} %get-tuple-element.123), channel_id=1, source_target_pairs={{0,2},{1,3},{2,0},{3,1},{4,6},{5,7},{6,4},{7,5},{8,10},{9,11},{10,... | collective-permute-start | bytes 6152 | tf_op jit(solution)/shard_map/ppermute | solution.py:59
  30.1 8.0 %collective-permute-start.11 = (bf16[32,32]{1,0:T(8,128)(2,1)S(1)}, bf16[32,32]{1,0:T(8,128)(2,1)S(1)}, u32[]{:S(2)}, u32[]{:S(2)}) collective-permute-start(bf16[32,32]{1,0:T(8,128)(2,1)S(1)} %get-tuple-element.124), channel_id=1, source_target_pairs={{0,3},{1,2},{2,1},{3,0},{4,7},{5,6},{6,5},{7,4},{8,11},{9,10},{10,... | collective-permute-start | bytes 6152 | tf_op jit(solution)/shard_map/ppermute | solution.py:59
  30.2 7.9 %collective-permute-start.9 = (bf16[32,32]{1,0:T(8,128)(2,1)S(1)}, bf16[32,32]{1,0:T(8,128)(2,1)S(1)}, u32[]{:S(2)}, u32[]{:S(2)}) collective-permute-start(bf16[32,32]{1,0:T(8,128)(2,1)S(1)} %get-tuple-element.122), channel_id=1, source_target_pairs={{0,1},{1,0},{2,3},{3,2},{4,5},{5,4},{6,7},{7,6},{8,9},{9,8},{10,11... | collective-permute-start | bytes 6152 | tf_op jit(solution)/shard_map/ppermute | solution.py:59
  38.1 6.4 %collective-permute-start.13 = (bf16[32,4096]{1,0:T(8,128)(2,1)S(1)}, bf16[32,4096]{1,0:T(8,128)(2,1)S(1)}, u32[]{:S(2)}, u32[]{:S(2)}) collective-permute-start(bf16[32,4096]{1,0:T(8,128)(2,1)S(1)} %get-tuple-element.141), channel_id=1, source_target_pairs={{0,1},{1,0},{2,3},{3,2},{4,5},{5,4},{6,7},{7,6},{8,9},{9,8},{10,11... | collective-permute-start | bytes 786440 | tf_op jit(solution)/shard_map/ppermute | solution.py:59
  38.2 9.1 %collective-permute-start.14 = (bf16[32,4096]{1,0:T(8,128)(2,1)S(1)}, bf16[32,4096]{1,0:T(8,128)(2,1)S(1)}, u32[]{:S(2)}, u32[]{:S(2)}) collective-permute-start(bf16[32,4096]{1,0:T(8,128)(2,1)S(1)} %get-tuple-element.142), channel_id=1, source_target_pairs={{0,2},{1,3},{2,0},{3,1},{4,6},{5,7},{6,4},{7,5},{8,10},{9,11},{10,... | collective-permute-start | bytes 786440 | tf_op jit(solution)/shard_map/ppermute | solution.py:59
  39.9 12.1 %collective-permute-start.15 = (bf16[32,4096]{1,0:T(8,128)(2,1)S(1)}, bf16[32,4096]{1,0:T(8,128)(2,1)S(1)}, u32[]{:S(2)}, u32[]{:S(2)}) collective-permute-start(bf16[32,4096]{1,0:T(8,128)(2,1)S(1)} %get-tuple-element.143), channel_id=1, source_target_pairs={{0,3},{1,2},{2,1},{3,0},{4,7},{5,6},{6,5},{7,4},{8,11},{9,10},{10,... | collective-permute-start | bytes 786440 | tf_op jit(solution)/shard_map/ppermute | solution.py:59
  40.3 11.7 %collective-permute-start.19 = (bf16[16,4096]{1,0:T(8,128)(2,1)S(1)}, bf16[16,4096]{1,0:T(8,128)(2,1)S(1)}, u32[]{:S(2)}, u32[]{:S(2)}) collective-permute-start(bf16[16,4096]{1,0:T(8,128)(2,1)S(1)} %get-tuple-element.150), channel_id=1, source_target_pairs={{0,4},{1,5},{2,6},{3,7},{16,20},{17,21},{18,22},{19,23}} | collective-permute-start | bytes 393224 | tf_op jit(solution)/shard_map/ppermute | solution.py:432
  43.1 10.6 %collective-permute-start.12 = (bf16[16,4096]{1,0:T(8,128)(2,1)S(1)}, bf16[16,4096]{1,0:T(8,128)(2,1)S(1)}, u32[]{:S(2)}, u32[]{:S(2)}) collective-permute-start(bf16[16,4096]{1,0:T(8,128)(2,1)S(1)} %get-tuple-element.137), channel_id=1, source_target_pairs={{0,4},{1,5},{2,6},{3,7},{16,20},{17,21},{18,22},{19,23}} | collective-permute-start | bytes 393224 | tf_op jit(solution)/shard_map/ppermute | solution.py:432
  53.0 2.4 %collective-permute-start.20 = (bf16[16,4096]{1,0:T(8,128)(2,1)S(1)}, bf16[16,4096]{1,0:T(8,128)(2,1)S(1)}, u32[]{:S(2)}, u32[]{:S(2)}) collective-permute-start(bf16[16,4096]{1,0:T(8,128)(2,1)S(1)} %get-tuple-element.153), channel_id=1, source_target_pairs={{4,8},{5,9},{6,10},{7,11},{20,24},{21,25},{22,26},{23,27}} | collective-permute-start | bytes 393224 | tf_op jit(solution)/shard_map/ppermute | solution.py:432
  53.7 5.0 %copy-start.5 = (bf16[4,32,4096]{2,1,0:T(8,128)(2,1)S(1)}, bf16[4,32,4096]{2,1,0:T(8,128)(2,1)}, u32[]{:S(2)}) copy-start(bf16[4,32,4096]{2,1,0:T(8,128)(2,1)} %cotangent.3) | copy-start | bytes 3145732
  54.7 2.3 %collective-permute-start.16 = (bf16[16,4096]{1,0:T(8,128)(2,1)S(1)}, bf16[16,4096]{1,0:T(8,128)(2,1)S(1)}, u32[]{:S(2)}, u32[]{:S(2)}) collective-permute-start(bf16[16,4096]{1,0:T(8,128)(2,1)S(1)} %get-tuple-element.145), channel_id=1, source_target_pairs={{4,8},{5,9},{6,10},{7,11},{20,24},{21,25},{22,26},{23,27}} | collective-permute-start | bytes 393224 | tf_op jit(solution)/shard_map/ppermute | solution.py:432
  56.4 2.3 %collective-permute-start.21 = (bf16[16,4096]{1,0:T(8,128)(2,1)S(1)}, bf16[16,4096]{1,0:T(8,128)(2,1)S(1)}, u32[]{:S(2)}, u32[]{:S(2)}) collective-permute-start(bf16[16,4096]{1,0:T(8,128)(2,1)S(1)} %get-tuple-element.155), channel_id=1, source_target_pairs={{8,12},{9,13},{10,14},{11,15},{24,28},{25,29},{26,30},{27,31}} | collective-permute-start | bytes 393224 | tf_op jit(solution)/shard_map/ppermute | solution.py:432
  58.0 2.4 %collective-permute-start.17 = (bf16[16,4096]{1,0:T(8,128)(2,1)S(1)}, bf16[16,4096]{1,0:T(8,128)(2,1)S(1)}, u32[]{:S(2)}, u32[]{:S(2)}) collective-permute-start(bf16[16,4096]{1,0:T(8,128)(2,1)S(1)} %get-tuple-element.147), channel_id=1, source_target_pairs={{8,12},{9,13},{10,14},{11,15},{24,28},{25,29},{26,30},{27,31}} | collective-permute-start | bytes 393224 | tf_op jit(solution)/shard_map/ppermute | solution.py:432
  59.7 2.7 %collective-permute-start.22 = (bf16[16,4096]{1,0:T(8,128)(2,1)S(1)}, bf16[16,4096]{1,0:T(8,128)(2,1)S(1)}, u32[]{:S(2)}, u32[]{:S(2)}) collective-permute-start(bf16[16,4096]{1,0:T(8,128)(2,1)S(1)} %get-tuple-element.157), channel_id=1, source_target_pairs={{12,8},{13,9},{14,10},{15,11},{28,24},{29,25},{30,26},{31,27}} | collective-permute-start | bytes 393224 | tf_op jit(solution)/shard_map/ppermute | solution.py:461
  61.4 1.0 collective-permute-start.18
  62.5 11.1 %collective-permute-start.28 = (bf16[32,4096]{1,0:T(8,128)(2,1)S(1)}, bf16[32,4096]{1,0:T(8,128)(2,1)S(1)}, u32[]{:S(2)}, u32[]{:S(2)}) collective-permute-start(bf16[32,4096]{1,0:T(8,128)(2,1)S(1)} %get-tuple-element.189.refs_0_), channel_id=1, source_target_pairs={{0,2},{1,3},{2,0},{3,1},{4,6},{5,7},{6,4},{7,5},{8,10},{9,11},{10,... | collective-permute-start | bytes 786440 | tf_op jit(solution)/shard_map/ppermute | solution.py:59
  65.2 8.4 %collective-permute-start.24 = (bf16[16,4096]{1,0:T(8,128)(2,1)S(1)}, bf16[16,4096]{1,0:T(8,128)(2,1)S(1)}, u32[]{:S(2)}, u32[]{:S(2)}) collective-permute-start(bf16[16,4096]{1,0:T(8,128)(2,1)S(1)} %get-tuple-element.172), channel_id=1, source_target_pairs={{8,4},{9,5},{10,6},{11,7},{24,20},{25,21},{26,22},{27,23}} | collective-permute-start | bytes 393224 | tf_op jit(solution)/shard_map/ppermute | solution.py:461
  65.9 2.3 %collective-permute-start.25 = (bf16[32,1024]{1,0:T(8,128)(2,1)S(1)}, bf16[32,1024]{1,0:T(8,128)(2,1)S(1)}, u32[]{:S(2)}, u32[]{:S(2)}) collective-permute-start(bf16[32,1024]{1,0:T(8,128)(2,1)S(1)} %get-tuple-element.174), channel_id=1, source_target_pairs={{0,1},{1,0},{2,3},{3,2},{4,5},{5,4},{6,7},{7,6},{8,9},{9,8},{10,11... | collective-permute-start | bytes 196616 | tf_op jit(solution)/shard_map/ppermute | solution.py:59
  66.9 6.7 %collective-permute-start.23 = (bf16[16,4096]{1,0:T(8,128)(2,1)S(1)}, bf16[16,4096]{1,0:T(8,128)(2,1)S(1)}, u32[]{:S(2)}, u32[]{:S(2)}) collective-permute-start(bf16[16,4096]{1,0:T(8,128)(2,1)S(1)} %get-tuple-element.169), channel_id=1, source_target_pairs={{8,4},{9,5},{10,6},{11,7},{24,20},{25,21},{26,22},{27,23}} | collective-permute-start | bytes 393224 | tf_op jit(solution)/shard_map/ppermute | solution.py:461
  67.8 5.0 %collective-permute-start.26 = (bf16[32,1024]{1,0:T(8,128)(2,1)S(1)}, bf16[32,1024]{1,0:T(8,128)(2,1)S(1)}, u32[]{:S(2)}, u32[]{:S(2)}) collective-permute-start(bf16[32,1024]{1,0:T(8,128)(2,1)S(1)} %get-tuple-element.175), channel_id=1, source_target_pairs={{0,2},{1,3},{2,0},{3,1},{4,6},{5,7},{6,4},{7,5},{8,10},{9,11},{10,... | collective-permute-start | bytes 196616 | tf_op jit(solution)/shard_map/ppermute | solution.py:59
  68.2 5.4 %collective-permute-start.27 = (bf16[32,1024]{1,0:T(8,128)(2,1)S(1)}, bf16[32,1024]{1,0:T(8,128)(2,1)S(1)}, u32[]{:S(2)}, u32[]{:S(2)}) collective-permute-start(bf16[32,1024]{1,0:T(8,128)(2,1)S(1)} %get-tuple-element.176), channel_id=1, source_target_pairs={{0,3},{1,2},{2,1},{3,0},{4,7},{5,6},{6,5},{7,4},{8,11},{9,10},{10,... | collective-permute-start | bytes 196616 | tf_op jit(solution)/shard_map/ppermute | solution.py:59
  73.6 6.1 %collective-permute-start.31 = (bf16[32,4096]{1,0:T(8,128)(2,1)S(1)}, bf16[32,4096]{1,0:T(8,128)(2,1)S(1)}, u32[]{:S(2)}, u32[]{:S(2)}) collective-permute-start(bf16[32,4096]{1,0:T(8,128)(2,1)S(1)} %get-tuple-element.189.refs_0_), channel_id=1, source_target_pairs={{0,1},{1,0},{2,3},{3,2},{4,5},{5,4},{6,7},{7,6},{8,9},{9,8},{10,11... | collective-permute-start | bytes 786440 | tf_op jit(solution)/shard_map/ppermute | solution.py:59
  73.8 5.9 %collective-permute-start.32 = (bf16[32,4096]{1,0:T(8,128)(2,1)S(1)}, bf16[32,4096]{1,0:T(8,128)(2,1)S(1)}, u32[]{:S(2)}, u32[]{:S(2)}) collective-permute-start(bf16[32,4096]{1,0:T(8,128)(2,1)S(1)} %collective-permute-done.28.refs_2_), channel_id=1, source_target_pairs={{0,1},{1,0},{2,3},{3,2},{4,5},{5,4},{6,7},{7,6},{8,9},{9,8},{10,11... | collective-permute-start | bytes 786440 | tf_op jit(solution)/shard_map/ppermute | solution.py:59
  75.1 20.7 %collective-permute-start.30 = (bf16[16,4096]{1,0:T(8,128)(2,1)S(1)}, bf16[16,4096]{1,0:T(8,128)(2,1)S(1)}, u32[]{:S(2)}, u32[]{:S(2)}) collective-permute-start(bf16[16,4096]{1,0:T(8,128)(2,1)S(1)} %get-tuple-element.183), channel_id=1, source_target_pairs={{4,0},{5,1},{6,2},{7,3},{20,16},{21,17},{22,18},{23,19}} | collective-permute-start | bytes 393224 | tf_op jit(solution)/shard_map/ppermute | solution.py:461
  77.4 31.2 %copy-start.2 = (bf16[1,4096,512]{2,1,0:T(8,128)(2,1)S(1)}, bf16[1,4096,512]{2,1,0:T(8,128)(2,1)}, u32[]{:S(2)}) copy-start(bf16[1,4096,512]{2,1,0:T(8,128)(2,1)} %param.18) | copy-start | bytes 12582916
  77.4 21.0 %collective-permute-start.29 = (bf16[16,4096]{1,0:T(8,128)(2,1)S(1)}, bf16[16,4096]{1,0:T(8,128)(2,1)S(1)}, u32[]{:S(2)}, u32[]{:S(2)}) collective-permute-start(bf16[16,4096]{1,0:T(8,128)(2,1)S(1)} %get-tuple-element.180), channel_id=1, source_target_pairs={{4,0},{5,1},{6,2},{7,3},{20,16},{21,17},{22,18},{23,19}} | collective-permute-start | bytes 393224 | tf_op jit(solution)/shard_map/ppermute | solution.py:461
  98.5 1.4 %collective-permute-start.33 = (bf16[16,4096]{1,0:T(8,128)(2,1)S(1)}, bf16[16,4096]{1,0:T(8,128)(2,1)S(1)}, u32[]{:S(2)}, u32[]{:S(2)}) collective-permute-start(bf16[16,4096]{1,0:T(8,128)(2,1)S(1)} %shard_map.132.refs_0_), channel_id=1, source_target_pairs={{0,1},{1,0},{2,3},{3,2},{4,5},{5,4},{6,7},{7,6},{8,9},{9,8},{10,11... | collective-permute-start | bytes 393224 | tf_op jit(solution)/shard_map/ppermute | solution.py:59
  98.5 6.4 %collective-permute-start.35 = (bf16[16,4096]{1,0:T(8,128)(2,1)S(1)}, bf16[16,4096]{1,0:T(8,128)(2,1)S(1)}, u32[]{:S(2)}, u32[]{:S(2)}) collective-permute-start(bf16[16,4096]{1,0:T(8,128)(2,1)S(1)} %shard_map.132.refs_0_), channel_id=1, source_target_pairs={{0,2},{1,3},{2,0},{3,1},{4,6},{5,7},{6,4},{7,5},{8,10},{9,11},{10,... | collective-permute-start | bytes 393224 | tf_op jit(solution)/shard_map/ppermute | solution.py:59
  99.9 7.3 %collective-permute-start.36 = (bf16[16,4096]{1,0:T(8,128)(2,1)S(1)}, bf16[16,4096]{1,0:T(8,128)(2,1)S(1)}, u32[]{:S(2)}, u32[]{:S(2)}) collective-permute-start(bf16[16,4096]{1,0:T(8,128)(2,1)S(1)} %shard_map.133.refs_1_), channel_id=1, source_target_pairs={{0,2},{1,3},{2,0},{3,1},{4,6},{5,7},{6,4},{7,5},{8,10},{9,11},{10,... | collective-permute-start | bytes 393224 | tf_op jit(solution)/shard_map/ppermute | solution.py:59
  100.7 6.5 %collective-permute-start.34 = (bf16[16,4096]{1,0:T(8,128)(2,1)S(1)}, bf16[16,4096]{1,0:T(8,128)(2,1)S(1)}, u32[]{:S(2)}, u32[]{:S(2)}) collective-permute-start(bf16[16,4096]{1,0:T(8,128)(2,1)S(1)} %shard_map.133.refs_1_), channel_id=1, source_target_pairs={{0,1},{1,0},{2,3},{3,2},{4,5},{5,4},{6,7},{7,6},{8,9},{9,8},{10,11... | collective-permute-start | bytes 393224 | tf_op jit(solution)/shard_map/ppermute | solution.py:59
  104.9 2.4 %collective-permute-start.37 = (bf16[16,4096]{1,0:T(8,128)(2,1)S(1)}, bf16[16,4096]{1,0:T(8,128)(2,1)S(1)}, u32[]{:S(2)}, u32[]{:S(2)}) collective-permute-start(bf16[16,4096]{1,0:T(8,128)(2,1)S(1)} %collective-permute-done.35.refs_4_), channel_id=1, source_target_pairs={{0,1},{1,0},{2,3},{3,2},{4,5},{5,4},{6,7},{7,6},{8,9},{9,8},{10,11... | collective-permute-start | bytes 393224 | tf_op jit(solution)/shard_map/ppermute | solution.py:59
  107.3 1.3 %collective-permute-start.38 = (bf16[16,4096]{1,0:T(8,128)(2,1)S(1)}, bf16[16,4096]{1,0:T(8,128)(2,1)S(1)}, u32[]{:S(2)}, u32[]{:S(2)}) collective-permute-start(bf16[16,4096]{1,0:T(8,128)(2,1)S(1)} %collective-permute-done.36.refs_5_), channel_id=1, source_target_pairs={{0,1},{1,0},{2,3},{3,2},{4,5},{5,4},{6,7},{7,6},{8,9},{9,8},{10,11... | collective-permute-start | bytes 393224 | tf_op jit(solution)/shard_map/ppermute | solution.py:59
  113.3 1.6 %collective-permute-start.39 = (bf16[32,4096]{1,0:T(8,128)(2,1)S(1)}, bf16[32,4096]{1,0:T(8,128)(2,1)S(1)}, u32[]{:S(2)}, u32[]{:S(2)}) collective-permute-start(bf16[32,4096]{1,0:T(8,128)(2,1)S(1)} %get-tuple-element.205), channel_id=1, source_target_pairs={{0,1},{1,0},{2,3},{3,2},{4,5},{5,4},{6,7},{7,6},{8,9},{9,8},{10,11... | collective-permute-start | bytes 786440 | tf_op jit(solution)/shard_map/ppermute | solution.py:59
  114.9 5.6 %collective-permute-start.40 = (bf16[16,4096]{1,0:T(8,128)(2,1)S(1)}, bf16[16,4096]{1,0:T(8,128)(2,1)S(1)}, u32[]{:S(2)}, u32[]{:S(2)}) collective-permute-start(bf16[16,4096]{1,0:T(8,128)(2,1)S(1)} %slice.59), channel_id=1, source_target_pairs={{0,2},{1,3},{2,0},{3,1},{4,6},{5,7},{6,4},{7,5},{8,10},{9,11},{10,... | collective-permute-start | bytes 393224 | tf_op jit(solution)/shard_map/ppermute | solution.py:59
  120.6 4.5 %collective-permute-start.41 = (bf16[4,4096]{1,0:T(4,128)(2,1)S(1)}, bf16[4,4096]{1,0:T(4,128)(2,1)S(1)}, u32[]{:S(2)}, u32[]{:S(2)}) collective-permute-start(bf16[4,4096]{1,0:T(4,128)(2,1)S(1)} %get-tuple-element.215), channel_id=1, source_target_pairs={{0,4},{4,0},{8,12},{12,8},{1,5},{5,1},{9,13},{13,9},{2,6},{6,2},{1... | collective-permute-start | bytes 98312 | tf_op jit(solution)/shard_map/ppermute | solution.py:59
  120.7 5.0 %collective-permute-start.42 = (bf16[4,4096]{1,0:T(4,128)(2,1)S(1)}, bf16[4,4096]{1,0:T(4,128)(2,1)S(1)}, u32[]{:S(2)}, u32[]{:S(2)}) collective-permute-start(bf16[4,4096]{1,0:T(4,128)(2,1)S(1)} %get-tuple-element.217), channel_id=1, source_target_pairs={{0,8},{4,12},{8,0},{12,4},{1,9},{5,13},{9,1},{13,5},{2,10},{6,14},... | collective-permute-start | bytes 98312 | tf_op jit(solution)/shard_map/ppermute | solution.py:59
  120.8 6.5 %collective-permute-start.43 = (bf16[4,4096]{1,0:T(4,128)(2,1)S(1)}, bf16[4,4096]{1,0:T(4,128)(2,1)S(1)}, u32[]{:S(2)}, u32[]{:S(2)}) collective-permute-start(bf16[4,4096]{1,0:T(4,128)(2,1)S(1)} %get-tuple-element.216), channel_id=1, source_target_pairs={{0,12},{4,8},{8,4},{12,0},{1,13},{5,9},{9,5},{13,1},{2,14},{6,10},... | collective-permute-start | bytes 98312 | tf_op jit(solution)/shard_map/ppermute | solution.py:59

commit v6 on v5

--- a/solution.py
+++ b/solution.py
@@ -503,8 +503,6 @@
             )
     gathered = []
     for c in range(chunks):
-        if gathered:
-            cames[c], gathered[-1][1] = lax.optimization_barrier((cames[c], gathered[-1][1]))
         (d_out,) = on_chip(
             functools.partial(dropped_kernel, 0, c), [wide], cames[c], grads[c], factor
         )

time: 128 us -> 128 us (level)
  waiting for transfers between devices: 58.5 us -> 56.6 us
    ppermute x32, waiting for transfers between devices: 40.6 us -> 38.7 us  [swap(): return lax.ppermute(array, axis, [(i, i ^ k) for i in range(size)])]
  transfers between devices with their start and end apart: 44 -> 44, of which waited for: 19 -> 18; matrix products, arithmetic and copies ran while one was open for 5% -> 5% of each run, Pallas kernels for 12% -> 13%
where the time goes in v6:
time: 128 us; the launch traced here: 127 us
  waiting for transfers between devices  56.6 us (44%)
  starting transfers between devices  38.2 us (30%)
  Pallas kernels  22.4 us (18%)
  local copies, waits for them, and re-layouts  6.74 us (5%)
  other arithmetic  2.14 us (2%)
    ppermute x32, waiting for transfers between devices, swap(): return lax.ppermute(array, axis, [(i, i ^ k) for i in range(size)])  38.7 us
    ppermute x32, starting transfers between devices, swap(): return lax.ppermute(array, axis, [(i, i ^ k) for i in range(size)])  25.8 us
    pallas_call x20, Pallas kernels, on_chip(): pl.pallas_call(body, out_shape=outs, in_specs=[vmem] * len(args), out_spe...  21.6 us
    ppermute x6, waiting for transfers between devices, per_device(): lax.ppermute(part, 'section', [(step, step - 1)])  17.8 us
    ppermute x6, starting transfers between devices, per_device(): lax.ppermute(part, 'section', [(step - 1, step)])  6.77 us
    ppermute x6, starting transfers between devices, per_device(): lax.ppermute(part, 'section', [(step, step - 1)])  5.69 us
    unnamed x17, local copies, waits for them, and re-layouts  5.4 us
  transfers between devices with their start and end apart: 44, of which 18 were waited for; matrix products, arithmetic and copies ran while one was open for 5% of the time, Pallas kernels for 13%

profile of v6, /device:TPU:0, one launch (start us, length us, event | category | flops | bytes accessed | tf_op | source)
XLA Modules:
  0.0 127.2 jit_solution(17602363838937600265)
XLA Ops:
  0.6 3.1 %collective-permute-start = (bf16[4,4096]{1,0:T(4,128)(2,1)}, bf16[4,4096]{1,0:T(4,128)(2,1)S(1)}, u32[]{:S(2)}, u32[]{:S(2)}) collective-permute-start(bf16[4,4096]{1,0:T(4,128)(2,1)} %bitcast.38), channel_id=1, source_target_pairs={{0,4},{4,0},{8,12},{12,8},{1,5},{5,1},{9,13},{13,9},{2,6},{6,2},{1... | collective-permute-start | bytes 98312 | tf_op jit(solution)/shard_map/ppermute | solution.py:59
  3.7 2.6 %collective-permute-start.1 = (bf16[4,4096]{1,0:T(4,128)(2,1)}, bf16[4,4096]{1,0:T(4,128)(2,1)S(1)}, u32[]{:S(2)}, u32[]{:S(2)}) collective-permute-start(bf16[4,4096]{1,0:T(4,128)(2,1)} %bitcast.39), channel_id=1, source_target_pairs={{0,8},{4,12},{8,0},{12,4},{1,9},{5,13},{9,1},{13,5},{2,10},{6,14},... | collective-permute-start | bytes 98312 | tf_op jit(solution)/shard_map/ppermute | solution.py:59
  6.3 0.9 reduce_window_sum.11
  7.6 0.8 fusion.12
  8.5 0.7 copy.15.seeds
  9.6 0.8 shard_map.113.factor
  10.4 2.3 %copy.16.refs_0_ = bf16[4096,512]{1,0:T(8,128)(2,1)S(1)} copy(bf16[4096,512]{1,0:T(8,128)(2,1)} %bitcast.30) | data formatting | bytes 8388608
  12.8 1.1 copy-done.3
  14.4 0.7 copy-done.6
  15.2 1.8 %collective-permute-start.4 = (bf16[16,4096]{1,0:T(8,128)(2,1)S(1)}, bf16[16,4096]{1,0:T(8,128)(2,1)S(1)}, u32[]{:S(2)}, u32[]{:S(2)}) collective-permute-start(bf16[16,4096]{1,0:T(8,128)(2,1)S(1)} %pad_maximum_fusion.refs_0_), channel_id=1, source_target_pairs={{0,2},{1,3},{2,0},{3,1},{4,6},{5,7},{6,4},{7,5},{8,10},{9,11},{10,... | collective-permute-start | bytes 393224 | tf_op jit(solution)/shard_map/ppermute | solution.py:59
  17.0 3.2 %collective-permute-done.4.refs_2_ = bf16[16,4096]{1,0:T(8,128)(2,1)S(1)} collective-permute-done((bf16[16,4096]{1,0:T(8,128)(2,1)S(1)}, bf16[16,4096]{1,0:T(8,128)(2,1)S(1)}, u32[]{:S(2)}, u32[]{:S(2)}) %collective-permute-start.4) | collective-permute-done | bytes 131104 | tf_op jit(solution)/shard_map/ppermute | solution.py:59
  20.4 1.2 collective-permute-done.5.refs_3_
  21.6 1.8 %shard_map.115 = (bf16[64,512]{1,0:T(8,128)(2,1)S(1)}, bf16[32,4096]{1,0:T(8,128)(2,1)S(1)}, bf16[32,4096]{1,0:T(8,128)(2,1)S(1)}, bf16[32,4096]{1,0:T(8,128)(2,1)S(1)}, bf16[32,4096]{1,0:T(8,128)(2,1)S(1)}) custom-call(bf16[64,64]{1,0:T(8,128)(2,1)S(1)} %get-tuple-element.105.by_owner, bf16[4096,512]{1,0:T(8,128)(2,1)S(1)} %get-tuple-element.106.wv, ...), custom_call_target="tpu_custom_call" | custom-call | flops 642252800 | bytes 10035200 | tf_op jit(solution)/shard_map/pallas_call | solution.py:306
  23.6 1.7 %collective-permute-start.7 = (bf16[32,4096]{1,0:T(8,128)(2,1)S(1)}, bf16[32,4096]{1,0:T(8,128)(2,1)S(1)}, u32[]{:S(2)}, u32[]{:S(2)}) collective-permute-start(bf16[32,4096]{1,0:T(8,128)(2,1)S(1)} %get-tuple-element.112), channel_id=1, source_target_pairs={{0,2},{1,3},{2,0},{3,1},{4,6},{5,7},{6,4},{7,5},{8,10},{9,11},{10,... | collective-permute-start | bytes 786440 | tf_op jit(solution)/shard_map/ppermute | solution.py:59
  25.3 3.0 %shard_map.116 = (bf16[64,512]{1,0:T(8,128)(2,1)S(1)}, bf16[32,4096]{1,0:T(8,128)(2,1)S(1)}, bf16[32,4096]{1,0:T(8,128)(2,1)S(1)}, bf16[32,4096]{1,0:T(8,128)(2,...) custom-call(bf16[64,64]{1,0:T(8,128)(2,1)S(1)} %get-tuple-element.10, ...), custom_call_target="tpu_custom_call" | custom-call | flops 719323136 | bytes 11239424 | tf_op jit(solution)/shard_map/pallas_call | solution.py:306
  28.3 1.7 %collective-permute-start.10 = (bf16[32,32]{1,0:T(8,128)(2,1)S(1)}, bf16[32,32]{1,0:T(8,128)(2,1)S(1)}, u32[]{:S(2)}, u32[]{:S(2)}) collective-permute-start(bf16[32,32]{1,0:T(8,128)(2,1)S(1)} %get-tuple-element.121), channel_id=1, source_target_pairs={{0,2},{1,3},{2,0},{3,1},{4,6},{5,7},{6,4},{7,5},{8,10},{9,11},{10,... | collective-permute-start | bytes 6152 | tf_op jit(solution)/shard_map/ppermute | solution.py:59
  30.5 2.2 %collective-permute-done.7.refs_6_ = bf16[32,4096]{1,0:T(8,128)(2,1)S(1)} collective-permute-done((bf16[32,4096]{1,0:T(8,128)(2,1)S(1)}, bf16[32,4096]{1,0:T(8,128)(2,1)S(1)}, u32[]{:S(2)}, u32[]{:S(2)}) %collective-permute-start.7) | collective-permute-done | bytes 262176 | tf_op jit(solution)/shard_map/ppermute | solution.py:59
  32.7 4.5 %collective-permute-done.8.refs_7_ = bf16[32,4096]{1,0:T(8,128)(2,1)S(1)} collective-permute-done((bf16[32,4096]{1,0:T(8,128)(2,1)S(1)}, bf16[32,4096]{1,0:T(8,128)(2,1)S(1)}, u32[]{:S(2)}, u32[]{:S(2)}) %collective-permute-start.8) | collective-permute-done | bytes 262176 | tf_op jit(solution)/shard_map/ppermute | solution.py:59
  37.2 0.8 collective-permute-done.10.refs_2_
  38.2 1.7 %collective-permute-start.14 = (bf16[32,4096]{1,0:T(8,128)(2,1)S(1)}, bf16[32,4096]{1,0:T(8,128)(2,1)S(1)}, u32[]{:S(2)}, u32[]{:S(2)}) collective-permute-start(bf16[32,4096]{1,0:T(8,128)(2,1)S(1)} %get-tuple-element.140), channel_id=1, source_target_pairs={{0,2},{1,3},{2,0},{3,1},{4,6},{5,7},{6,4},{7,5},{8,10},{9,11},{10,... | collective-permute-start | bytes 786440 | tf_op jit(solution)/shard_map/ppermute | solution.py:59
  40.3 2.8 %collective-permute-start.19 = (bf16[16,4096]{1,0:T(8,128)(2,1)S(1)}, bf16[16,4096]{1,0:T(8,128)(2,1)S(1)}, u32[]{:S(2)}, u32[]{:S(2)}) collective-permute-start(bf16[16,4096]{1,0:T(8,128)(2,1)S(1)} %get-tuple-element.148), channel_id=1, source_target_pairs={{0,4},{1,5},{2,6},{3,7},{16,20},{17,21},{18,22},{19,23}} | collective-permute-start | bytes 393224 | tf_op jit(solution)/shard_map/ppermute | solution.py:432
  43.1 1.3 %collective-permute-start.12 = (bf16[16,4096]{1,0:T(8,128)(2,1)S(1)}, bf16[16,4096]{1,0:T(8,128)(2,1)S(1)}, u32[]{:S(2)}, u32[]{:S(2)}) collective-permute-start(bf16[16,4096]{1,0:T(8,128)(2,1)S(1)} %get-tuple-element.135), channel_id=1, source_target_pairs={{0,4},{1,5},{2,6},{3,7},{16,20},{17,21},{18,22},{19,23}} | collective-permute-start | bytes 393224 | tf_op jit(solution)/shard_map/ppermute | solution.py:432
  44.4 2.9 %collective-permute-done.14.refs_2_ = bf16[32,4096]{1,0:T(8,128)(2,1)S(1)} collective-permute-done((bf16[32,4096]{1,0:T(8,128)(2,1)S(1)}, bf16[32,4096]{1,0:T(8,128)(2,1)S(1)}, u32[]{:S(2)}, u32[]{:S(2)}) %collective-permute-start.14) | collective-permute-done | bytes 262176 | tf_op jit(solution)/shard_map/ppermute | solution.py:59
  47.3 4.7 %collective-permute-done.15.refs_3_ = bf16[32,4096]{1,0:T(8,128)(2,1)S(1)} collective-permute-done((bf16[32,4096]{1,0:T(8,128)(2,1)S(1)}, bf16[32,4096]{1,0:T(8,128)(2,1)S(1)}, u32[]{:S(2)}, u32[]{:S(2)}) %collective-permute-start.15) | collective-permute-done | bytes 262176 | tf_op jit(solution)/shard_map/ppermute | solution.py:59
  52.0 1.0 shard_map.122
  53.0 0.7 collective-permute-start.20
  53.7 1.0 shard_map.119
  54.7 0.7 collective-permute-start.16
  55.4 1.0 shard_map.123
  56.4 0.7 collective-permute-start.21
  57.0 1.0 shard_map.120
  58.0 0.7 collective-permute-start.17
  58.7 1.0 shard_map.124
  59.7 0.7 collective-permute-start.22
  60.4 1.0 shard_map.121
  61.4 0.7 collective-permute-start.18
  62.5 1.8 %collective-permute-start.28 = (bf16[32,4096]{1,0:T(8,128)(2,1)S(1)}, bf16[32,4096]{1,0:T(8,128)(2,1)S(1)}, u32[]{:S(2)}, u32[]{:S(2)}) collective-permute-start(bf16[32,4096]{1,0:T(8,128)(2,1)S(1)} %get-tuple-element.187.refs_0_), channel_id=1, source_target_pairs={{0,2},{1,3},{2,0},{3,1},{4,6},{5,7},{6,4},{7,5},{8,10},{9,11},{10,... | collective-permute-start | bytes 786440 | tf_op jit(solution)/shard_map/ppermute | solution.py:59
  64.2 1.0 shard_map.127
  65.2 0.7 collective-permute-start.24
  66.0 1.0 shard_map.126
  66.9 0.8 collective-permute-start.23
  68.2 1.5 %collective-permute-start.27 = (bf16[32,1024]{1,0:T(8,128)(2,1)S(1)}, bf16[32,1024]{1,0:T(8,128)(2,1)S(1)}, u32[]{:S(2)}, u32[]{:S(2)}) collective-permute-start(bf16[32,1024]{1,0:T(8,128)(2,1)S(1)} %get-tuple-element.174), channel_id=1, source_target_pairs={{0,3},{1,2},{2,1},{3,0},{4,7},{5,6},{6,5},{7,4},{8,11},{9,10},{10,... | collective-permute-start | bytes 196616 | tf_op jit(solution)/shard_map/ppermute | solution.py:59
  69.7 3.0 %collective-permute-done.26.refs_2_ = bf16[32,1024]{1,0:T(8,128)(2,1)S(1)} collective-permute-done((bf16[32,1024]{1,0:T(8,128)(2,1)S(1)}, bf16[32,1024]{1,0:T(8,128)(2,1)S(1)}, u32[]{:S(2)}, u32[]{:S(2)}) %collective-permute-start.26) | collective-permute-done | bytes 65568 | tf_op jit(solution)/shard_map/ppermute | solution.py:59
  72.7 0.9 collective-permute-done.27.refs_3_
  74.2 1.0 shard_map.129
  75.1 1.3 %collective-permute-start.30 = (bf16[16,4096]{1,0:T(8,128)(2,1)S(1)}, bf16[16,4096]{1,0:T(8,128)(2,1)S(1)}, u32[]{:S(2)}, u32[]{:S(2)}) collective-permute-start(bf16[16,4096]{1,0:T(8,128)(2,1)S(1)} %get-tuple-element.181), channel_id=1, source_target_pairs={{4,0},{5,1},{6,2},{7,3},{20,16},{21,17},{22,18},{23,19}} | collective-permute-start | bytes 393224 | tf_op jit(solution)/shard_map/ppermute | solution.py:461
  76.4 1.0 shard_map.128
  77.4 1.6 %collective-permute-start.29 = (bf16[16,4096]{1,0:T(8,128)(2,1)S(1)}, bf16[16,4096]{1,0:T(8,128)(2,1)S(1)}, u32[]{:S(2)}, u32[]{:S(2)}) collective-permute-start(bf16[16,4096]{1,0:T(8,128)(2,1)S(1)} %get-tuple-element.178), channel_id=1, source_target_pairs={{4,0},{5,1},{6,2},{7,3},{20,16},{21,17},{22,18},{23,19}} | collective-permute-start | bytes 393224 | tf_op jit(solution)/shard_map/ppermute | solution.py:461
  79.0 0.7 shard_map.130
  79.7 0.9 shard_map.131
  80.6 15.2 %collective-permute-done.30.came = bf16[16,4096]{1,0:T(8,128)(2,1)S(1)} collective-permute-done((bf16[16,4096]{1,0:T(8,128)(2,1)S(1)}, bf16[16,4096]{1,0:T(8,128)(2,1)S(1)}, u32[]{:S(2)}, u32[]{:S(2)}) %collective-permute-start.30) | collective-permute-done | bytes 131104 | tf_op jit(solution)/shard_map/ppermute | solution.py:461
  95.8 2.6 %collective-permute-done.29.came = bf16[16,4096]{1,0:T(8,128)(2,1)S(1)} collective-permute-done((bf16[16,4096]{1,0:T(8,128)(2,1)S(1)}, bf16[16,4096]{1,0:T(8,128)(2,1)S(1)}, u32[]{:S(2)}, u32[]{:S(2)}) %collective-permute-start.29) | collective-permute-done | bytes 131104 | tf_op jit(solution)/shard_map/ppermute | solution.py:461
  98.5 0.6 collective-permute-start.36
  99.1 1.6 %collective-permute-start.35 = (bf16[16,4096]{1,0:T(8,128)(2,1)S(1)}, bf16[16,4096]{1,0:T(8,128)(2,1)S(1)}, u32[]{:S(2)}, u32[]{:S(2)}) collective-permute-start(bf16[16,4096]{1,0:T(8,128)(2,1)S(1)} %shard_map.132.refs_0_), channel_id=1, source_target_pairs={{0,2},{1,3},{2,0},{3,1},{4,6},{5,7},{6,4},{7,5},{8,10},{9,11},{10,... | collective-permute-start | bytes 393224 | tf_op jit(solution)/shard_map/ppermute | solution.py:59
  101.2 3.7 %collective-permute-done.36.refs_5_ = bf16[16,4096]{1,0:T(8,128)(2,1)S(1)} collective-permute-done((bf16[16,4096]{1,0:T(8,128)(2,1)S(1)}, bf16[16,4096]{1,0:T(8,128)(2,1)S(1)}, u32[]{:S(2)}, u32[]{:S(2)}) %collective-permute-start.36) | collective-permute-done | bytes 131104 | tf_op jit(solution)/shard_map/ppermute | solution.py:59
  104.9 1.6 %collective-permute-done.35.refs_4_ = bf16[16,4096]{1,0:T(8,128)(2,1)S(1)} collective-permute-done((bf16[16,4096]{1,0:T(8,128)(2,1)S(1)}, bf16[16,4096]{1,0:T(8,128)(2,1)S(1)}, u32[]{:S(2)}, u32[]{:S(2)}) %collective-permute-start.35) | collective-permute-done | bytes 131104 | tf_op jit(solution)/shard_map/ppermute | solution.py:59
  106.5 1.3 %collective-permute-done.37.refs_6_ = bf16[16,4096]{1,0:T(8,128)(2,1)S(1)} collective-permute-done((bf16[16,4096]{1,0:T(8,128)(2,1)S(1)}, bf16[16,4096]{1,0:T(8,128)(2,1)S(1)}, u32[]{:S(2)}, u32[]{:S(2)}) %collective-permute-start.37) | collective-permute-done | bytes 131104 | tf_op jit(solution)/shard_map/ppermute | solution.py:59
  107.8 4.6 %shard_map.134 = (f32[32,4096]{1,0:T(8,128)S(1)}, bf16[32,4096]{1,0:T(8,128)(2,1)S(1)}) custom-call(bf16[64,512]{1,0:T(8,128)(2,1)S(1)} %get-tuple-element.186.keys, bf16[64,512]{1,0:T(8,128)(2,1)S(1)} %get-tuple-element.192.values, bf16[128,512]{1,0:T(8,128)(2,1)S(1)} %get-tuple-element.193.query, f32[128,32]{1,0:T(8,128)S(1)} %get-tuple-element.194.probs, ...), custom_call_target="tpu_custom_call" | custom-call | flops 957874176 | bytes 14966784 | tf_op jit(solution)/shard_map/pallas_call | solution.py:306
  112.7 1.4 %collective-permute-done.39 = bf16[32,4096]{1,0:T(8,128)(2,1)S(1)} collective-permute-done((bf16[32,4096]{1,0:T(8,128)(2,1)S(1)}, bf16[32,4096]{1,0:T(8,128)(2,1)S(1)}, u32[]{:S(2)}, u32[]{:S(2)}) %collective-permute-start.39) | collective-permute-done | bytes 262176 | tf_op jit(solution)/shard_map/ppermute | solution.py:59
  114.8 5.0 %collective-permute-done.40 = bf16[16,4096]{1,0:T(8,128)(2,1)S(1)} collective-permute-done((bf16[16,4096]{1,0:T(8,128)(2,1)S(1)}, bf16[16,4096]{1,0:T(8,128)(2,1)S(1)}, u32[]{:S(2)}, u32[]{:S(2)}) %collective-permute-start.40) | collective-permute-done | bytes 131104 | tf_op jit(solution)/shard_map/ppermute | solution.py:59
  120.0 4.3 %collective-permute-start.43 = (bf16[4,4096]{1,0:T(4,128)(2,1)S(1)}, bf16[4,4096]{1,0:T(4,128)(2,1)S(1)}, u32[]{:S(2)}, u32[]{:S(2)}) collective-permute-start(bf16[4,4096]{1,0:T(4,128)(2,1)S(1)} %get-tuple-element.212), channel_id=1, source_target_pairs={{0,12},{4,8},{8,4},{12,0},{1,13},{5,9},{9,5},{13,1},{2,14},{6,10},... | collective-permute-start | bytes 98312 | tf_op jit(solution)/shard_map/ppermute | solution.py:59
  124.3 0.7 collective-permute-done.42
  125.0 1.6 %collective-permute-done.43 = bf16[4,4096]{1,0:T(4,128)(2,1)S(1)} collective-permute-done((bf16[4,4096]{1,0:T(4,128)(2,1)S(1)}, bf16[4,4096]{1,0:T(4,128)(2,1)S(1)}, u32[]{:S(2)}, u32[]{:S(2)}) %collective-permute-start.43) | collective-permute-done | bytes 32800 | tf_op jit(solution)/shard_map/ppermute | solution.py:59
  126.6 0.7 fusion.2
  (92 shorter events, 6.0 us)
Async XLA Ops:
  0.6 13.8 %collective-permute-start = (bf16[4,4096]{1,0:T(4,128)(2,1)}, bf16[4,4096]{1,0:T(4,128)(2,1)S(1)}, u32[]{:S(2)}, u32[]{:S(2)}) collective-permute-start(bf16[4,4096]{1,0:T(4,128)(2,1)} %bitcast.38), channel_id=1, source_target_pairs={{0,4},{4,0},{8,12},{12,8},{1,5},{5,1},{9,13},{13,9},{2,6},{6,2},{1... | collective-permute-start | bytes 98312 | tf_op jit(solution)/shard_map/ppermute | solution.py:59
  3.7 10.7 %collective-permute-start.1 = (bf16[4,4096]{1,0:T(4,128)(2,1)}, bf16[4,4096]{1,0:T(4,128)(2,1)S(1)}, u32[]{:S(2)}, u32[]{:S(2)}) collective-permute-start(bf16[4,4096]{1,0:T(4,128)(2,1)} %bitcast.39), channel_id=1, source_target_pairs={{0,8},{4,12},{8,0},{12,4},{1,9},{5,13},{9,1},{13,5},{2,10},{6,14},... | collective-permute-start | bytes 98312 | tf_op jit(solution)/shard_map/ppermute | solution.py:59
  6.3 8.1 %collective-permute-start.2 = (bf16[4,4096]{1,0:T(4,128)(2,1)}, bf16[4,4096]{1,0:T(4,128)(2,1)S(1)}, u32[]{:S(2)}, u32[]{:S(2)}) collective-permute-start(bf16[4,4096]{1,0:T(4,128)(2,1)} %bitcast.40), channel_id=1, source_target_pairs={{0,12},{4,8},{8,4},{12,0},{1,13},{5,9},{9,5},{13,1},{2,14},{6,10},... | collective-permute-start | bytes 98312 | tf_op jit(solution)/shard_map/ppermute | solution.py:59
  10.4 3.5 %copy-start.3 = (bf16[1,512,4096]{2,1,0:T(8,128)(2,1)S(1)}, bf16[1,512,4096]{2,1,0:T(8,128)(2,1)}, u32[]{:S(2)}) copy-start(bf16[1,512,4096]{2,1,0:T(8,128)(2,1)} %param.19) | copy-start | bytes 12582916
  14.4 0.8 copy-start.6
  14.4 10.9 %copy-start.4 = (bf16[4,32,4096]{2,1,0:T(8,128)(2,1)S(1)}, bf16[4,32,4096]{2,1,0:T(8,128)(2,1)}, u32[]{:S(2)}) copy-start(bf16[4,32,4096]{2,1,0:T(8,128)(2,1)} %inputs.3) | copy-start | bytes 3145732
  15.2 5.0 %collective-permute-start.4 = (bf16[16,4096]{1,0:T(8,128)(2,1)S(1)}, bf16[16,4096]{1,0:T(8,128)(2,1)S(1)}, u32[]{:S(2)}, u32[]{:S(2)}) collective-permute-start(bf16[16,4096]{1,0:T(8,128)(2,1)S(1)} %pad_maximum_fusion.refs_0_), channel_id=1, source_target_pairs={{0,2},{1,3},{2,0},{3,1},{4,6},{5,7},{6,4},{7,5},{8,10},{9,11},{10,... | collective-permute-start | bytes 393224 | tf_op jit(solution)/shard_map/ppermute | solution.py:59
  17.0 3.4 %collective-permute-start.3 = (bf16[16,4096]{1,0:T(8,128)(2,1)S(1)}, bf16[16,4096]{1,0:T(8,128)(2,1)S(1)}, u32[]{:S(2)}, u32[]{:S(2)}) collective-permute-start(bf16[16,4096]{1,0:T(8,128)(2,1)S(1)} %pad_maximum_fusion.refs_0_), channel_id=1, source_target_pairs={{0,1},{1,0},{2,3},{3,2},{4,5},{5,4},{6,7},{7,6},{8,9},{9,8},{10,11... | collective-permute-start | bytes 393224 | tf_op jit(solution)/shard_map/ppermute | solution.py:59
  20.3 1.3 %collective-permute-start.5 = (bf16[16,4096]{1,0:T(8,128)(2,1)S(1)}, bf16[16,4096]{1,0:T(8,128)(2,1)S(1)}, u32[]{:S(2)}, u32[]{:S(2)}) collective-permute-start(bf16[16,4096]{1,0:T(8,128)(2,1)S(1)} %collective-permute-done.4.refs_2_), channel_id=1, source_target_pairs={{0,1},{1,0},{2,3},{3,2},{4,5},{5,4},{6,7},{7,6},{8,9},{9,8},{10,11... | collective-permute-start | bytes 393224 | tf_op jit(solution)/shard_map/ppermute | solution.py:59
  20.4 5.0 %copy-start = (bf16[1,4096,512]{2,1,0:T(8,128)(2,1)S(1)}, bf16[1,4096,512]{2,1,0:T(8,128)(2,1)}, u32[]{:S(2)}) copy-start(bf16[1,4096,512]{2,1,0:T(8,128)(2,1)} %param.16) | copy-start | bytes 12582916
  20.4 5.0 %copy-start.1 = (bf16[1,4096,512]{2,1,0:T(8,128)(2,1)S(1)}, bf16[1,4096,512]{2,1,0:T(8,128)(2,1)}, u32[]{:S(2)}) copy-start(bf16[1,4096,512]{2,1,0:T(8,128)(2,1)} %param.17) | copy-start | bytes 12582916
  23.4 1.9 %collective-permute-start.6 = (bf16[32,4096]{1,0:T(8,128)(2,1)S(1)}, bf16[32,4096]{1,0:T(8,128)(2,1)S(1)}, u32[]{:S(2)}, u32[]{:S(2)}) collective-permute-start(bf16[32,4096]{1,0:T(8,128)(2,1)S(1)} %get-tuple-element.110), channel_id=1, source_target_pairs={{0,1},{1,0},{2,3},{3,2},{4,5},{5,4},{6,7},{7,6},{8,9},{9,8},{10,11... | collective-permute-start | bytes 786440 | tf_op jit(solution)/shard_map/ppermute | solution.py:59
  23.6 9.1 %collective-permute-start.7 = (bf16[32,4096]{1,0:T(8,128)(2,1)S(1)}, bf16[32,4096]{1,0:T(8,128)(2,1)S(1)}, u32[]{:S(2)}, u32[]{:S(2)}) collective-permute-start(bf16[32,4096]{1,0:T(8,128)(2,1)S(1)} %get-tuple-element.112), channel_id=1, source_target_pairs={{0,2},{1,3},{2,0},{3,1},{4,6},{5,7},{6,4},{7,5},{8,10},{9,11},{10,... | collective-permute-start | bytes 786440 | tf_op jit(solution)/shard_map/ppermute | solution.py:59
  25.3 11.9 %collective-permute-start.8 = (bf16[32,4096]{1,0:T(8,128)(2,1)S(1)}, bf16[32,4096]{1,0:T(8,128)(2,1)S(1)}, u32[]{:S(2)}, u32[]{:S(2)}) collective-permute-start(bf16[32,4096]{1,0:T(8,128)(2,1)S(1)} %get-tuple-element.113), channel_id=1, source_target_pairs={{0,3},{1,2},{2,1},{3,0},{4,7},{5,6},{6,5},{7,4},{8,11},{9,10},{10,... | collective-permute-start | bytes 786440 | tf_op jit(solution)/shard_map/ppermute | solution.py:59
  28.3 9.7 %collective-permute-start.10 = (bf16[32,32]{1,0:T(8,128)(2,1)S(1)}, bf16[32,32]{1,0:T(8,128)(2,1)S(1)}, u32[]{:S(2)}, u32[]{:S(2)}) collective-permute-start(bf16[32,32]{1,0:T(8,128)(2,1)S(1)} %get-tuple-element.121), channel_id=1, source_target_pairs={{0,2},{1,3},{2,0},{3,1},{4,6},{5,7},{6,4},{7,5},{8,10},{9,11},{10,... | collective-permute-start | bytes 6152 | tf_op jit(solution)/shard_map/ppermute | solution.py:59
  30.1 8.0 %collective-permute-start.11 = (bf16[32,32]{1,0:T(8,128)(2,1)S(1)}, bf16[32,32]{1,0:T(8,128)(2,1)S(1)}, u32[]{:S(2)}, u32[]{:S(2)}) collective-permute-start(bf16[32,32]{1,0:T(8,128)(2,1)S(1)} %get-tuple-element.122), channel_id=1, source_target_pairs={{0,3},{1,2},{2,1},{3,0},{4,7},{5,6},{6,5},{7,4},{8,11},{9,10},{10,... | collective-permute-start | bytes 6152 | tf_op jit(solution)/shard_map/ppermute | solution.py:59
  30.2 7.9 %collective-permute-start.9 = (bf16[32,32]{1,0:T(8,128)(2,1)S(1)}, bf16[32,32]{1,0:T(8,128)(2,1)S(1)}, u32[]{:S(2)}, u32[]{:S(2)}) collective-permute-start(bf16[32,32]{1,0:T(8,128)(2,1)S(1)} %get-tuple-element.120), channel_id=1, source_target_pairs={{0,1},{1,0},{2,3},{3,2},{4,5},{5,4},{6,7},{7,6},{8,9},{9,8},{10,11... | collective-permute-start | bytes 6152 | tf_op jit(solution)/shard_map/ppermute | solution.py:59
  38.1 6.4 %collective-permute-start.13 = (bf16[32,4096]{1,0:T(8,128)(2,1)S(1)}, bf16[32,4096]{1,0:T(8,128)(2,1)S(1)}, u32[]{:S(2)}, u32[]{:S(2)}) collective-permute-start(bf16[32,4096]{1,0:T(8,128)(2,1)S(1)} %get-tuple-element.139), channel_id=1, source_target_pairs={{0,1},{1,0},{2,3},{3,2},{4,5},{5,4},{6,7},{7,6},{8,9},{9,8},{10,11... | collective-permute-start | bytes 786440 | tf_op jit(solution)/shard_map/ppermute | solution.py:59
  38.2 9.1 %collective-permute-start.14 = (bf16[32,4096]{1,0:T(8,128)(2,1)S(1)}, bf16[32,4096]{1,0:T(8,128)(2,1)S(1)}, u32[]{:S(2)}, u32[]{:S(2)}) collective-permute-start(bf16[32,4096]{1,0:T(8,128)(2,1)S(1)} %get-tuple-element.140), channel_id=1, source_target_pairs={{0,2},{1,3},{2,0},{3,1},{4,6},{5,7},{6,4},{7,5},{8,10},{9,11},{10,... | collective-permute-start | bytes 786440 | tf_op jit(solution)/shard_map/ppermute | solution.py:59
  39.9 12.1 %collective-permute-start.15 = (bf16[32,4096]{1,0:T(8,128)(2,1)S(1)}, bf16[32,4096]{1,0:T(8,128)(2,1)S(1)}, u32[]{:S(2)}, u32[]{:S(2)}) collective-permute-start(bf16[32,4096]{1,0:T(8,128)(2,1)S(1)} %get-tuple-element.141), channel_id=1, source_target_pairs={{0,3},{1,2},{2,1},{3,0},{4,7},{5,6},{6,5},{7,4},{8,11},{9,10},{10,... | collective-permute-start | bytes 786440 | tf_op jit(solution)/shard_map/ppermute | solution.py:59
  40.3 11.7 %collective-permute-start.19 = (bf16[16,4096]{1,0:T(8,128)(2,1)S(1)}, bf16[16,4096]{1,0:T(8,128)(2,1)S(1)}, u32[]{:S(2)}, u32[]{:S(2)}) collective-permute-start(bf16[16,4096]{1,0:T(8,128)(2,1)S(1)} %get-tuple-element.148), channel_id=1, source_target_pairs={{0,4},{1,5},{2,6},{3,7},{16,20},{17,21},{18,22},{19,23}} | collective-permute-start | bytes 393224 | tf_op jit(solution)/shard_map/ppermute | solution.py:432
  43.1 10.6 %collective-permute-start.12 = (bf16[16,4096]{1,0:T(8,128)(2,1)S(1)}, bf16[16,4096]{1,0:T(8,128)(2,1)S(1)}, u32[]{:S(2)}, u32[]{:S(2)}) collective-permute-start(bf16[16,4096]{1,0:T(8,128)(2,1)S(1)} %get-tuple-element.135), channel_id=1, source_target_pairs={{0,4},{1,5},{2,6},{3,7},{16,20},{17,21},{18,22},{19,23}} | collective-permute-start | bytes 393224 | tf_op jit(solution)/shard_map/ppermute | solution.py:432
  53.0 2.4 %collective-permute-start.20 = (bf16[16,4096]{1,0:T(8,128)(2,1)S(1)}, bf16[16,4096]{1,0:T(8,128)(2,1)S(1)}, u32[]{:S(2)}, u32[]{:S(2)}) collective-permute-start(bf16[16,4096]{1,0:T(8,128)(2,1)S(1)} %get-tuple-element.151), channel_id=1, source_target_pairs={{4,8},{5,9},{6,10},{7,11},{20,24},{21,25},{22,26},{23,27}} | collective-permute-start | bytes 393224 | tf_op jit(solution)/shard_map/ppermute | solution.py:432
  53.7 5.0 %copy-start.5 = (bf16[4,32,4096]{2,1,0:T(8,128)(2,1)S(1)}, bf16[4,32,4096]{2,1,0:T(8,128)(2,1)}, u32[]{:S(2)}) copy-start(bf16[4,32,4096]{2,1,0:T(8,128)(2,1)} %cotangent.3) | copy-start | bytes 3145732
  54.7 2.3 %collective-permute-start.16 = (bf16[16,4096]{1,0:T(8,128)(2,1)S(1)}, bf16[16,4096]{1,0:T(8,128)(2,1)S(1)}, u32[]{:S(2)}, u32[]{:S(2)}) collective-permute-start(bf16[16,4096]{1,0:T(8,128)(2,1)S(1)} %get-tuple-element.143), channel_id=1, source_target_pairs={{4,8},{5,9},{6,10},{7,11},{20,24},{21,25},{22,26},{23,27}} | collective-permute-start | bytes 393224 | tf_op jit(solution)/shard_map/ppermute | solution.py:432
  56.4 2.3 %collective-permute-start.21 = (bf16[16,4096]{1,0:T(8,128)(2,1)S(1)}, bf16[16,4096]{1,0:T(8,128)(2,1)S(1)}, u32[]{:S(2)}, u32[]{:S(2)}) collective-permute-start(bf16[16,4096]{1,0:T(8,128)(2,1)S(1)} %get-tuple-element.153), channel_id=1, source_target_pairs={{8,12},{9,13},{10,14},{11,15},{24,28},{25,29},{26,30},{27,31}} | collective-permute-start | bytes 393224 | tf_op jit(solution)/shard_map/ppermute | solution.py:432
  58.0 2.4 %collective-permute-start.17 = (bf16[16,4096]{1,0:T(8,128)(2,1)S(1)}, bf16[16,4096]{1,0:T(8,128)(2,1)S(1)}, u32[]{:S(2)}, u32[]{:S(2)}) collective-permute-start(bf16[16,4096]{1,0:T(8,128)(2,1)S(1)} %get-tuple-element.145), channel_id=1, source_target_pairs={{8,12},{9,13},{10,14},{11,15},{24,28},{25,29},{26,30},{27,31}} | collective-permute-start | bytes 393224 | tf_op jit(solution)/shard_map/ppermute | solution.py:432
  59.7 2.7 %collective-permute-start.22 = (bf16[16,4096]{1,0:T(8,128)(2,1)S(1)}, bf16[16,4096]{1,0:T(8,128)(2,1)S(1)}, u32[]{:S(2)}, u32[]{:S(2)}) collective-permute-start(bf16[16,4096]{1,0:T(8,128)(2,1)S(1)} %get-tuple-element.155), channel_id=1, source_target_pairs={{12,8},{13,9},{14,10},{15,11},{28,24},{29,25},{30,26},{31,27}} | collective-permute-start | bytes 393224 | tf_op jit(solution)/shard_map/ppermute | solution.py:461
  61.4 1.0 collective-permute-start.18
  62.5 11.1 %collective-permute-start.28 = (bf16[32,4096]{1,0:T(8,128)(2,1)S(1)}, bf16[32,4096]{1,0:T(8,128)(2,1)S(1)}, u32[]{:S(2)}, u32[]{:S(2)}) collective-permute-start(bf16[32,4096]{1,0:T(8,128)(2,1)S(1)} %get-tuple-element.187.refs_0_), channel_id=1, source_target_pairs={{0,2},{1,3},{2,0},{3,1},{4,6},{5,7},{6,4},{7,5},{8,10},{9,11},{10,... | collective-permute-start | bytes 786440 | tf_op jit(solution)/shard_map/ppermute | solution.py:59
  65.2 8.4 %collective-permute-start.24 = (bf16[16,4096]{1,0:T(8,128)(2,1)S(1)}, bf16[16,4096]{1,0:T(8,128)(2,1)S(1)}, u32[]{:S(2)}, u32[]{:S(2)}) collective-permute-start(bf16[16,4096]{1,0:T(8,128)(2,1)S(1)} %get-tuple-element.170), channel_id=1, source_target_pairs={{8,4},{9,5},{10,6},{11,7},{24,20},{25,21},{26,22},{27,23}} | collective-permute-start | bytes 393224 | tf_op jit(solution)/shard_map/ppermute | solution.py:461
  65.9 2.3 %collective-permute-start.25 = (bf16[32,1024]{1,0:T(8,128)(2,1)S(1)}, bf16[32,1024]{1,0:T(8,128)(2,1)S(1)}, u32[]{:S(2)}, u32[]{:S(2)}) collective-permute-start(bf16[32,1024]{1,0:T(8,128)(2,1)S(1)} %get-tuple-element.172), channel_id=1, source_target_pairs={{0,1},{1,0},{2,3},{3,2},{4,5},{5,4},{6,7},{7,6},{8,9},{9,8},{10,11... | collective-permute-start | bytes 196616 | tf_op jit(solution)/shard_map/ppermute | solution.py:59
  66.9 6.7 %collective-permute-start.23 = (bf16[16,4096]{1,0:T(8,128)(2,1)S(1)}, bf16[16,4096]{1,0:T(8,128)(2,1)S(1)}, u32[]{:S(2)}, u32[]{:S(2)}) collective-permute-start(bf16[16,4096]{1,0:T(8,128)(2,1)S(1)} %get-tuple-element.167), channel_id=1, source_target_pairs={{8,4},{9,5},{10,6},{11,7},{24,20},{25,21},{26,22},{27,23}} | collective-permute-start | bytes 393224 | tf_op jit(solution)/shard_map/ppermute | solution.py:461
  67.8 5.0 %collective-permute-start.26 = (bf16[32,1024]{1,0:T(8,128)(2,1)S(1)}, bf16[32,1024]{1,0:T(8,128)(2,1)S(1)}, u32[]{:S(2)}, u32[]{:S(2)}) collective-permute-start(bf16[32,1024]{1,0:T(8,128)(2,1)S(1)} %get-tuple-element.173), channel_id=1, source_target_pairs={{0,2},{1,3},{2,0},{3,1},{4,6},{5,7},{6,4},{7,5},{8,10},{9,11},{10,... | collective-permute-start | bytes 196616 | tf_op jit(solution)/shard_map/ppermute | solution.py:59
  68.2 5.4 %collective-permute-start.27 = (bf16[32,1024]{1,0:T(8,128)(2,1)S(1)}, bf16[32,1024]{1,0:T(8,128)(2,1)S(1)}, u32[]{:S(2)}, u32[]{:S(2)}) collective-permute-start(bf16[32,1024]{1,0:T(8,128)(2,1)S(1)} %get-tuple-element.174), channel_id=1, source_target_pairs={{0,3},{1,2},{2,1},{3,0},{4,7},{5,6},{6,5},{7,4},{8,11},{9,10},{10,... | collective-permute-start | bytes 196616 | tf_op jit(solution)/shard_map/ppermute | solution.py:59
  73.6 6.1 %collective-permute-start.31 = (bf16[32,4096]{1,0:T(8,128)(2,1)S(1)}, bf16[32,4096]{1,0:T(8,128)(2,1)S(1)}, u32[]{:S(2)}, u32[]{:S(2)}) collective-permute-start(bf16[32,4096]{1,0:T(8,128)(2,1)S(1)} %get-tuple-element.187.refs_0_), channel_id=1, source_target_pairs={{0,1},{1,0},{2,3},{3,2},{4,5},{5,4},{6,7},{7,6},{8,9},{9,8},{10,11... | collective-permute-start | bytes 786440 | tf_op jit(solution)/shard_map/ppermute | solution.py:59
  73.8 5.9 %collective-permute-start.32 = (bf16[32,4096]{1,0:T(8,128)(2,1)S(1)}, bf16[32,4096]{1,0:T(8,128)(2,1)S(1)}, u32[]{:S(2)}, u32[]{:S(2)}) collective-permute-start(bf16[32,4096]{1,0:T(8,128)(2,1)S(1)} %collective-permute-done.28.refs_2_), channel_id=1, source_target_pairs={{0,1},{1,0},{2,3},{3,2},{4,5},{5,4},{6,7},{7,6},{8,9},{9,8},{10,11... | collective-permute-start | bytes 786440 | tf_op jit(solution)/shard_map/ppermute | solution.py:59
  75.1 20.7 %collective-permute-start.30 = (bf16[16,4096]{1,0:T(8,128)(2,1)S(1)}, bf16[16,4096]{1,0:T(8,128)(2,1)S(1)}, u32[]{:S(2)}, u32[]{:S(2)}) collective-permute-start(bf16[16,4096]{1,0:T(8,128)(2,1)S(1)} %get-tuple-element.181), channel_id=1, source_target_pairs={{4,0},{5,1},{6,2},{7,3},{20,16},{21,17},{22,18},{23,19}} | collective-permute-start | bytes 393224 | tf_op jit(solution)/shard_map/ppermute | solution.py:461
  77.4 30.4 %copy-start.2 = (bf16[1,4096,512]{2,1,0:T(8,128)(2,1)S(1)}, bf16[1,4096,512]{2,1,0:T(8,128)(2,1)}, u32[]{:S(2)}) copy-start(bf16[1,4096,512]{2,1,0:T(8,128)(2,1)} %param.18) | copy-start | bytes 12582916
  77.4 21.0 %collective-permute-start.29 = (bf16[16,4096]{1,0:T(8,128)(2,1)S(1)}, bf16[16,4096]{1,0:T(8,128)(2,1)S(1)}, u32[]{:S(2)}, u32[]{:S(2)}) collective-permute-start(bf16[16,4096]{1,0:T(8,128)(2,1)S(1)} %get-tuple-element.178), channel_id=1, source_target_pairs={{4,0},{5,1},{6,2},{7,3},{20,16},{21,17},{22,18},{23,19}} | collective-permute-start | bytes 393224 | tf_op jit(solution)/shard_map/ppermute | solution.py:461
  98.5 6.5 %collective-permute-start.36 = (bf16[16,4096]{1,0:T(8,128)(2,1)S(1)}, bf16[16,4096]{1,0:T(8,128)(2,1)S(1)}, u32[]{:S(2)}, u32[]{:S(2)}) collective-permute-start(bf16[16,4096]{1,0:T(8,128)(2,1)S(1)} %shard_map.133.refs_1_), channel_id=1, source_target_pairs={{0,2},{1,3},{2,0},{3,1},{4,6},{5,7},{6,4},{7,5},{8,10},{9,11},{10,... | collective-permute-start | bytes 393224 | tf_op jit(solution)/shard_map/ppermute | solution.py:59
  99.1 7.4 %collective-permute-start.35 = (bf16[16,4096]{1,0:T(8,128)(2,1)S(1)}, bf16[16,4096]{1,0:T(8,128)(2,1)S(1)}, u32[]{:S(2)}, u32[]{:S(2)}) collective-permute-start(bf16[16,4096]{1,0:T(8,128)(2,1)S(1)} %shard_map.132.refs_0_), channel_id=1, source_target_pairs={{0,2},{1,3},{2,0},{3,1},{4,6},{5,7},{6,4},{7,5},{8,10},{9,11},{10,... | collective-permute-start | bytes 393224 | tf_op jit(solution)/shard_map/ppermute | solution.py:59
  100.7 5.8 %collective-permute-start.34 = (bf16[16,4096]{1,0:T(8,128)(2,1)S(1)}, bf16[16,4096]{1,0:T(8,128)(2,1)S(1)}, u32[]{:S(2)}, u32[]{:S(2)}) collective-permute-start(bf16[16,4096]{1,0:T(8,128)(2,1)S(1)} %shard_map.133.refs_1_), channel_id=1, source_target_pairs={{0,1},{1,0},{2,3},{3,2},{4,5},{5,4},{6,7},{7,6},{8,9},{9,8},{10,11... | collective-permute-start | bytes 393224 | tf_op jit(solution)/shard_map/ppermute | solution.py:59
  100.7 5.8 %collective-permute-start.33 = (bf16[16,4096]{1,0:T(8,128)(2,1)S(1)}, bf16[16,4096]{1,0:T(8,128)(2,1)S(1)}, u32[]{:S(2)}, u32[]{:S(2)}) collective-permute-start(bf16[16,4096]{1,0:T(8,128)(2,1)S(1)} %shard_map.132.refs_0_), channel_id=1, source_target_pairs={{0,1},{1,0},{2,3},{3,2},{4,5},{5,4},{6,7},{7,6},{8,9},{9,8},{10,11... | collective-permute-start | bytes 393224 | tf_op jit(solution)/shard_map/ppermute | solution.py:59
  104.9 1.6 %collective-permute-start.38 = (bf16[16,4096]{1,0:T(8,128)(2,1)S(1)}, bf16[16,4096]{1,0:T(8,128)(2,1)S(1)}, u32[]{:S(2)}, u32[]{:S(2)}) collective-permute-start(bf16[16,4096]{1,0:T(8,128)(2,1)S(1)} %collective-permute-done.36.refs_5_), channel_id=1, source_target_pairs={{0,1},{1,0},{2,3},{3,2},{4,5},{5,4},{6,7},{7,6},{8,9},{9,8},{10,11... | collective-permute-start | bytes 393224 | tf_op jit(solution)/shard_map/ppermute | solution.py:59
  106.5 1.3 %collective-permute-start.37 = (bf16[16,4096]{1,0:T(8,128)(2,1)S(1)}, bf16[16,4096]{1,0:T(8,128)(2,1)S(1)}, u32[]{:S(2)}, u32[]{:S(2)}) collective-permute-start(bf16[16,4096]{1,0:T(8,128)(2,1)S(1)} %collective-permute-done.35.refs_4_), channel_id=1, source_target_pairs={{0,1},{1,0},{2,3},{3,2},{4,5},{5,4},{6,7},{7,6},{8,9},{9,8},{10,11... | collective-permute-start | bytes 393224 | tf_op jit(solution)/shard_map/ppermute | solution.py:59
  112.5 1.6 %collective-permute-start.39 = (bf16[32,4096]{1,0:T(8,128)(2,1)S(1)}, bf16[32,4096]{1,0:T(8,128)(2,1)S(1)}, u32[]{:S(2)}, u32[]{:S(2)}) collective-permute-start(bf16[32,4096]{1,0:T(8,128)(2,1)S(1)} %get-tuple-element.201), channel_id=1, source_target_pairs={{0,1},{1,0},{2,3},{3,2},{4,5},{5,4},{6,7},{7,6},{8,9},{9,8},{10,11... | collective-permute-start | bytes 786440 | tf_op jit(solution)/shard_map/ppermute | solution.py:59
  114.2 5.6 %collective-permute-start.40 = (bf16[16,4096]{1,0:T(8,128)(2,1)S(1)}, bf16[16,4096]{1,0:T(8,128)(2,1)S(1)}, u32[]{:S(2)}, u32[]{:S(2)}) collective-permute-start(bf16[16,4096]{1,0:T(8,128)(2,1)S(1)} %slice.59), channel_id=1, source_target_pairs={{0,2},{1,3},{2,0},{3,1},{4,6},{5,7},{6,4},{7,5},{8,10},{9,11},{10,... | collective-permute-start | bytes 393224 | tf_op jit(solution)/shard_map/ppermute | solution.py:59
  119.9 4.5 %collective-permute-start.41 = (bf16[4,4096]{1,0:T(4,128)(2,1)S(1)}, bf16[4,4096]{1,0:T(4,128)(2,1)S(1)}, u32[]{:S(2)}, u32[]{:S(2)}) collective-permute-start(bf16[4,4096]{1,0:T(4,128)(2,1)S(1)} %get-tuple-element.211), channel_id=1, source_target_pairs={{0,4},{4,0},{8,12},{12,8},{1,5},{5,1},{9,13},{13,9},{2,6},{6,2},{1... | collective-permute-start | bytes 98312 | tf_op jit(solution)/shard_map/ppermute | solution.py:59
  119.9 5.0 %collective-permute-start.42 = (bf16[4,4096]{1,0:T(4,128)(2,1)S(1)}, bf16[4,4096]{1,0:T(4,128)(2,1)S(1)}, u32[]{:S(2)}, u32[]{:S(2)}) collective-permute-start(bf16[4,4096]{1,0:T(4,128)(2,1)S(1)} %get-tuple-element.213), channel_id=1, source_target_pairs={{0,8},{4,12},{8,0},{12,4},{1,9},{5,13},{9,1},{13,5},{2,10},{6,14},... | collective-permute-start | bytes 98312 | tf_op jit(solution)/shard_map/ppermute | solution.py:59
  120.0 6.5 %collective-permute-start.43 = (bf16[4,4096]{1,0:T(4,128)(2,1)S(1)}, bf16[4,4096]{1,0:T(4,128)(2,1)S(1)}, u32[]{:S(2)}, u32[]{:S(2)}) collective-permute-start(bf16[4,4096]{1,0:T(4,128)(2,1)S(1)} %get-tuple-element.212), channel_id=1, source_target_pairs={{0,12},{4,8},{8,4},{12,0},{1,13},{5,9},{9,5},{13,1},{2,14},{6,10},... | collective-permute-start | bytes 98312 | tf_op jit(solution)/shard_map/ppermute | solution.py:59
